TPU v7x, 512 devices: a whole 4x8x8 slice. The times are simulated.
512 devices in a mesh: region: 8 (over x, core), owner: 64 (over y, z).
Axes of the slice: x: 4, y: 8, z: 8, core: 2. Of those that a mesh axis runs over, the one named last changes fastest.
Arguments:
- voxels: bfloat16 [8, 64, 1, 256, 1024], P('region', 'owner'), may hold values from -6 to 6
- norm_gain: float32 [1024], replicated, may hold values from 0.5 to 1.5
- qkv_weight: bfloat16 [1024, 3072], P(('region', 'owner')), may hold values from -0.14453125 to 0.14453125
- out_weight: bfloat16 [1024, 1024], P(('region', 'owner')), may hold values from -0.1875 to 0.1875
- neighbours: int32 [8, 64, 1, 8], P('region', 'owner'), may hold values from -1 to 511, as said below
Outputs:
- attended_voxels: bfloat16 [8, 64, 1, 256, 1024], P('region', 'owner')
Inputs may be any that keep to these rules, and one draw needn't show every extreme that they name: `neighbours`: each entry is -1 or the number (r * 64 + o) + c of a block c held by the device at region r and owner o, where r and o each differ by at most one from those of the list's own block; a list never names its own block and names no block twice.
All inputs are finite; a program needn't handle non-finite values.
Results may differ from a plain program's by a relative error of at most 0.0057.
Values may be sent and summed in bfloat16 or wider, within the bound.
No kernel may reach another device: no remote copies, remote signals or barrier semaphores. Data moves between devices by JAX's collectives and lax.ppermute only.
A program may use at most 64 MiB of HBM per device.

v0:
```python
import jax
import jax.numpy as jnp
from jax import lax
from jax.sharding import PartitionSpec as P

HEAD_DIM = 64


def in_order(blocks, dim):
    shape = list(blocks.shape[1:])
    shape[dim] *= blocks.shape[0]
    return jnp.moveaxis(blocks, 0, dim).reshape(shape)


def from_everyone(value, axis):
    devices = lax.axis_size(axis)
    return lax.all_to_all(
        jnp.broadcast_to(value[None], (devices, *value.shape)), axis, 0, 0, tiled=True
    )


def gathered_copies(value, axis, dim):
    return in_order(from_everyone(value, axis), dim)


def padded(value, sides, width):
    for axis, dim in sides:
        devices, length = (lax.axis_size(axis), value.shape[dim])
        up = [(i, (i + 1) % devices) for i in range(devices - 1)]
        down = [(j, i) for i, j in up]
        last = lax.slice_in_dim(value, length - width, length, axis=dim)
        first = lax.slice_in_dim(value, 0, width, axis=dim)
        before = lax.ppermute(last, axis, up)
        after = lax.ppermute(first, axis, down)
        value = jnp.concatenate([before, value, after], axis=dim)
    return value


def layer_norm(inputs, norm_gain):
    widened = inputs.astype(jnp.float32)
    average = jnp.mean(widened, axis=-1, keepdims=True)
    spread = jnp.mean((widened - average) ** 2, axis=-1, keepdims=True)
    return ((widened - average) * lax.rsqrt(spread + 1e-06) * norm_gain).astype(jnp.bfloat16)


def shards(voxels, norm_gain, qkv_weight, out_weight, neighbours):
    capacity = voxels.shape[2]
    block_size = voxels.shape[3]
    model_width = voxels.shape[4]
    token_count = capacity * block_size
    flat_tokens = voxels.reshape(token_count, model_width)
    normed = layer_norm(flat_tokens, norm_gain)
    group_rows = gathered_copies(qkv_weight, "owner", 0)
    columns = normed
    qkv = jnp.dot(
        columns,
        lax.all_gather(group_rows, "region", axis=0, tiled=True),
        preferred_element_type=jnp.float32,
    )
    qkv = qkv.astype(jnp.bfloat16)
    queries = qkv[:, :model_width].reshape(capacity, block_size, model_width)
    kv_pairs = qkv[:, model_width:].reshape(1, 1, capacity, block_size, 2 * model_width)
    extended = padded(kv_pairs, (("region", 0), ("owner", 1)), 1)
    extended = extended.reshape(9 * capacity * block_size, 2 * model_width)
    key_rows = extended[:, :model_width]
    value_rows = extended[:, model_width:]
    owner_count = lax.axis_size("owner")
    my_region = lax.axis_index("region")
    my_owner = lax.axis_index("owner")
    list_ids = neighbours.reshape(capacity, neighbours.shape[-1])
    far_region = list_ids // (owner_count * capacity)
    far_owner = list_ids // capacity % owner_count
    far_slot = list_ids % capacity
    local_ids = (
        (far_region - my_region + 1) * 3 + (far_owner - my_owner + 1)
    ) * capacity + far_slot
    local_ids = jnp.where(list_ids >= 0, local_ids, -1)
    slot_ids = jnp.arange(9 * capacity, dtype=jnp.int32)
    listed = jnp.any(local_ids[:, :, None] == slot_ids[None, None, :], axis=1)
    own_block = slot_ids[None, :] == (4 * capacity + jnp.arange(capacity, dtype=jnp.int32))[:, None]
    allowed = listed | own_block
    key_mask = jnp.repeat(allowed, block_size, axis=1)
    group_heads = 2
    group_cols = group_heads * HEAD_DIM
    group_count = model_width // group_cols
    score_scale = HEAD_DIM ** (-0.5)

    def attend_group(group_idx, buffer):
        offset = group_idx * group_cols
        query_part = lax.dynamic_slice_in_dim(queries, offset, group_cols, 2).reshape(
            capacity, block_size, group_heads, HEAD_DIM
        )
        key_part = lax.dynamic_slice_in_dim(key_rows, offset, group_cols, 1).reshape(
            -1, group_heads, HEAD_DIM
        )
        value_part = lax.dynamic_slice_in_dim(value_rows, offset, group_cols, 1).reshape(
            -1, group_heads, HEAD_DIM
        )
        scores = (
            jnp.einsum("cshd,khd->chsk", query_part, key_part, preferred_element_type=jnp.float32)
            * score_scale
        )
        scores = jnp.where(key_mask[:, None, None, :], scores, -1e30)
        row_max = jnp.max(scores, axis=-1, keepdims=True)
        shifted = jnp.exp(scores - row_max)
        attn_probs = (shifted / jnp.sum(shifted, axis=-1, keepdims=True)).astype(jnp.bfloat16)
        attended = jnp.einsum(
            "chsk,khd->cshd", attn_probs, value_part, preferred_element_type=jnp.float32
        )
        attended = attended.astype(jnp.bfloat16).reshape(capacity, block_size, group_cols)
        return lax.dynamic_update_slice_in_dim(buffer, attended, offset, 2)

    mixed = lax.fori_loop(
        0, group_count, attend_group, jnp.zeros((capacity, block_size, model_width), jnp.bfloat16)
    )
    mixed_rows = mixed.reshape(token_count, model_width)
    columns = mixed_rows
    projected = jnp.dot(
        columns,
        lax.all_gather(out_weight, ("region", "owner"), axis=0, tiled=True),
        preferred_element_type=jnp.float32,
    )
    result = flat_tokens.astype(jnp.float32) + projected
    return result.astype(jnp.bfloat16).reshape(voxels.shape)


def solution(mesh):
    return jax.shard_map(
        shards,
        mesh=mesh,
        in_specs=(
            P("region", "owner", None, None, None),
            P(),
            P(("region", "owner"), None),
            P(("region", "owner"), None),
            P("region", "owner", None, None),
        ),
        out_specs=P("region", "owner", None, None, None),
        check_vma=False,
    )
```

profile of v0, /device:TPU:1, one launch (start us, length us, event | category | flops | bytes accessed | tf_op | source)
XLA Modules:
  0.0 356.1 jit_solution(15957770580684786674)
XLA Ops:
  8.5 38.6 %all_to_all.5 = bf16[64,2,3072]{2,1,0:T(2,128)(2,1)S(1)} all-to-all(bf16[64,2,3072]{2,1,0:T(2,128)(2,1)S(1)} %broadcast_in_dim.53), channel_id=1, replica_groups=mesh['region'=8,'owner'=64] {'owner'}, dimensions={0} | all-to-all | bytes 1572864 | tf_op jit(solution)/shard_map/all_to_all | solution.py:17
  48.9 43.2 %all-gather.4.cloned.1.call-done = bf16[1024,3072]{1,0:T(8,128)(2,1)} async-done(((bf16[128,3072]{1,0:T(8,128)(2,1)}), bf16[1024,3072]{1,0:T(8,128)(2,1)}) %all-gather.4.cloned.1.call-update) | async-done | bytes 6291472 | tf_op jit(solution)/shard_map/all_gather | solution.py:57
  92.1 4.7 %convolution_convert_fusion = bf16[256,3072]{1,0:T(8,128)(2,1)S(1)} fusion(bf16[1024,3072]{1,0:T(8,128)(2,1)} %all-gather.4.cloned.1.call-done, bf16[1,1,1,256,1024]{4,3,2,1,0:T(8,128)(2,1)S(1)} %copy-done.2, f32[1024]{0:T(1024)S(1)} %copy-done.8, f32[256]{0:T(256)S(1)} %add_rsqrt_fusion, f32[256]{0:T(256)S(1)} %broadcast_multiply_fusion), kind=kOutput, calls=%fused_computation.17 | convolution fusion | flops 1612709888 | bytes 8394752 | tf_op jit(solution)/shard_map/dot_general | solution.py:55
  98.0 2.4 collective-permute-start
  102.4 9.7 %collective-permute-done = bf16[1,1,1,256,2048]{4,3,2,1,0:T(8,128)(2,1)S(1)} collective-permute-done((bf16[1,1,1,256,2048]{4,3,2,1,0:T(8,128)(2,1)S(1)}, bf16[1,1,1,256,2048]{4,3,2,1,0:T(8,128)(2,1)S(1)}, u32[]{:S(2)}, u32[]{:S(2)}) %collective-permute-start) | collective-permute-done | bytes 1048608 | tf_op jit(solution)/shard_map/ppermute | solution.py:33
  112.1 4.4 %collective-permute-done.1 = bf16[1,1,1,256,2048]{4,3,2,1,0:T(8,128)(2,1)S(1)} collective-permute-done((bf16[1,1,1,256,2048]{4,3,2,1,0:T(8,128)(2,1)S(1)}, bf16[1,1,1,256,2048]{4,3,2,1,0:T(8,128)(2,1)S(1)}, u32[]{:S(2)}, u32[]{:S(2)}) %collective-permute-start.1) | collective-permute-done | bytes 1048608 | tf_op jit(solution)/shard_map/ppermute | solution.py:34
  118.5 5.4 %collective-permute-start.2 = (bf16[3,1,1,256,2048]{4,3,2,1,0:T(8,128)(2,1)}, bf16[3,1,1,256,2048]{4,3,2,1,0:T(8,128)(2,1)}, u32[]{:S(2)}, u32[]{:S(2)}) collective-permute-start(bf16[3,1,1,256,2048]{4,3,2,1,0:T(8,128)(2,1)} %pad_maximum_fusion.1), channel_id=1, source_target_pairs={{0,1},{1,2},{2,3},{3,4},{4,5},{5,6},{6,7},{7,8},{8,9},{9,10},{10,1... | collective-permute-start | bytes 9437192 | tf_op jit(solution)/shard_map/ppermute | solution.py:33
  125.3 118.2 %all-gather.6.cloned.1.call-done = bf16[512,2,1024]{2,1,0:T(2,128)(2,1)} async-done(((bf16[1,2,1024]{2,1,0:T(2,128)(2,1)}), bf16[512,2,1024]{2,1,0:T(2,128)(2,1)}) %all-gather.6.cloned.1.call-update) | async-done | bytes 2097168 | tf_op jit(solution)/shard_map/all_gather | solution.py:120
  243.5 4.1 %reshape.300 = bf16[1024,1024]{1,0:T(8,128)(2,1)} reshape(bf16[512,2,1024]{2,1,0:T(2,128)(2,1)} %all-gather.6.cloned.1.call-done) | data formatting | bytes 4194304
  249.5 4.7 %pad_maximum_fusion = bf16[3,3,1,256,2048]{4,3,2,1,0:T(8,128)(2,1)S(1)} fusion(bf16[3,1,1,256,2048]{4,3,2,1,0:T(8,128)(2,1)} %collective-permute-done.3, bf16[1,1,1,256,2048]{4,3,2,1,0:T(8,128)(2,1)} %copy-done.5, bf16[1,1,1,256,2048]{4,3,2,1,0:T(8,128)(2,1)} %copy-done.1, bf16[1,1,1,256,2048]{4,3,2,1,0:T(8,128)(2,1)} %copy-done.4, ...), kind=kLoop, calls=%fused_computation.16 | loop fusion | flops 18874368 | bytes 18874368 | tf_op jit(solution)/shard_map/concatenate | solution.py:35
  254.2 4.8 %fusion.28 = (bf16[2304,1024]{1,0:T(8,128)(2,1)}, bf16[2304,1024]{1,0:T(8,128)(2,1)}) fusion(bf16[2304,2048]{1,0:T(8,128)(2,1)S(1)} %bitcast.105), kind=kLoop, calls=%fused_computation.51 | loop fusion | bytes 18874368 | tf_op jit(solution)/shard_map/slice | solution.py:65
  259.0 86.5 %while.14 = (s32[]{:T(128)}, bf16[1,256,1024]{1,2,0:T(8,128)(2,1)S(1)}, bf16[2304,1024]{1,0:T(8,128)(2,1)}, bf16[2304,1024]{1,0:T(8,128)(2,1)}, bf16[1,256,1024]...) while((s32[]{:T(128)}, ...), condition=%wide.region_6.7_spmd.clone, body=%wide.region_3.6_spmd.clone.sunk | while | flops 311458816 | bytes 39472324 | solution.py:113
  263.5 2.2 copy-done
  266.6 3.3 fusion.45
  274.3 2.2 copy-done
  277.4 3.3 fusion.45
  285.1 2.2 copy-done
  288.2 3.3 fusion.45
  299.0 3.3 fusion.45
  309.8 3.3 fusion.45
  320.6 3.3 fusion.45
  331.4 3.3 fusion.45
  342.2 3.3 fusion.45
  345.5 3.1 fusion.15
  (130 shorter events, 64.7 us)
Async XLA Ops:
  7.4 41.1 %copy-start.2 = (bf16[1,1,1,256,1024]{4,3,2,1,0:T(8,128)(2,1)S(1)}, bf16[1,1,1,256,1024]{4,3,2,1,0:T(8,128)(2,1)}, u32[]{:S(2)}) copy-start(bf16[1,1,1,256,1024]{4,3,2,1,0:T(8,128)(2,1)} %param.7) | copy-start | bytes 1572868
  7.4 84.7 %copy-start.8 = (f32[1024]{0:T(1024)S(1)}, f32[1024]{0:T(1024)}, u32[]{:S(2)}) copy-start(f32[1024]{0:T(1024)} %param.8) | copy-start | bytes 12292
  7.4 84.7 %all-gather.4.cloned.1.call-start = ((), (), s32[]{:S(2)}) async-start(), calls=%async_computation.1 | async-start | bytes 7077888 | tf_op jit(solution)/shard_map/all_gather | solution.py:57
  48.4 195.1 %all-gather.6.cloned.1.call-start = ((), (), s32[]{:S(2)}) async-start(), calls=%async_computation.2 | async-start | bytes 2101248 | tf_op jit(solution)/shard_map/all_gather | solution.py:120
  96.8 1.2 copy-start.6
  96.8 28.4 %copy-start.7 = (s32[1,1,1,8]{3,2,1,0:T(1,128)S(1)}, s32[1,1,1,8]{3,2,1,0:T(1,128)}, u32[]{:S(2)}) copy-start(s32[1,1,1,8]{3,2,1,0:T(1,128)} %param.11) | copy-start | bytes 100
  98.0 149.6 %copy-start.1 = (bf16[1,1,1,256,2048]{4,3,2,1,0:T(8,128)(2,1)}, bf16[1,1,1,256,2048]{4,3,2,1,0:T(8,128)(2,1)S(1)}, u32[]{:S(2)}) copy-start(bf16[1,1,1,256,2048]{4,3,2,1,0:T(8,128)(2,1)S(1)} %slice_bitcast_fusion) | copy-start | bytes 3145732
  98.0 14.1 %collective-permute-start = (bf16[1,1,1,256,2048]{4,3,2,1,0:T(8,128)(2,1)S(1)}, bf16[1,1,1,256,2048]{4,3,2,1,0:T(8,128)(2,1)S(1)}, u32[]{:S(2)}, u32[]{:S(2)}) collective-permute-start(bf16[1,1,1,256,2048]{4,3,2,1,0:T(8,128)(2,1)S(1)} %slice_bitcast_fusion), channel_id=1, source_target_pairs={{0,64},{64,128},{128,192},{192,256},{256,320},{320,384},{384,448},... | collective-permute-start | bytes 3145736 | tf_op jit(solution)/shard_map/ppermute | solution.py:33
  100.4 16.1 %collective-permute-start.1 = (bf16[1,1,1,256,2048]{4,3,2,1,0:T(8,128)(2,1)S(1)}, bf16[1,1,1,256,2048]{4,3,2,1,0:T(8,128)(2,1)S(1)}, u32[]{:S(2)}, u32[]{:S(2)}) collective-permute-start(bf16[1,1,1,256,2048]{4,3,2,1,0:T(8,128)(2,1)S(1)} %slice_bitcast_fusion), channel_id=1, source_target_pairs={{64,0},{128,64},{192,128},{256,192},{320,256},{384,320},{448,384},... | collective-permute-start | bytes 3145736 | tf_op jit(solution)/shard_map/ppermute | solution.py:34
  112.1 135.5 %copy-start.4 = (bf16[1,1,1,256,2048]{4,3,2,1,0:T(8,128)(2,1)}, bf16[1,1,1,256,2048]{4,3,2,1,0:T(8,128)(2,1)S(1)}, u32[]{:S(2)}) copy-start(bf16[1,1,1,256,2048]{4,3,2,1,0:T(8,128)(2,1)S(1)} %collective-permute-done) | copy-start | bytes 3145732
  116.5 131.1 %copy-start.5 = (bf16[1,1,1,256,2048]{4,3,2,1,0:T(8,128)(2,1)}, bf16[1,1,1,256,2048]{4,3,2,1,0:T(8,128)(2,1)S(1)}, u32[]{:S(2)}) copy-start(bf16[1,1,1,256,2048]{4,3,2,1,0:T(8,128)(2,1)S(1)} %collective-permute-done.1) | copy-start | bytes 3145732
  118.5 130.9 %collective-permute-start.2 = (bf16[3,1,1,256,2048]{4,3,2,1,0:T(8,128)(2,1)}, bf16[3,1,1,256,2048]{4,3,2,1,0:T(8,128)(2,1)}, u32[]{:S(2)}, u32[]{:S(2)}) collective-permute-start(bf16[3,1,1,256,2048]{4,3,2,1,0:T(8,128)(2,1)} %pad_maximum_fusion.1), channel_id=1, source_target_pairs={{0,1},{1,2},{2,3},{3,4},{4,5},{5,6},{6,7},{7,8},{8,9},{9,10},{10,1... | collective-permute-start | bytes 9437192 | tf_op jit(solution)/shard_map/ppermute | solution.py:33
  123.9 125.6 %collective-permute-start.3 = (bf16[3,1,1,256,2048]{4,3,2,1,0:T(8,128)(2,1)}, bf16[3,1,1,256,2048]{4,3,2,1,0:T(8,128)(2,1)}, u32[]{:S(2)}, u32[]{:S(2)}) collective-permute-start(bf16[3,1,1,256,2048]{4,3,2,1,0:T(8,128)(2,1)} %pad_maximum_fusion.1), channel_id=1, source_target_pairs={{1,0},{2,1},{3,2},{4,3},{5,4},{6,5},{7,6},{8,7},{9,8},{10,9},{11,1... | collective-permute-start | bytes 9437192 | tf_op jit(solution)/shard_map/ppermute | solution.py:34
  259.0 86.5 %copy-start.3 = (bf16[1,1,1,256,1024]{4,3,2,1,0:T(8,128)(2,1)S(1)}, bf16[1,1,1,256,1024]{4,3,2,1,0:T(8,128)(2,1)}, u32[]{:S(2)}) copy-start(bf16[1,1,1,256,1024]{4,3,2,1,0:T(8,128)(2,1)} %param.7) | copy-start | bytes 1572868
  263.4 2.2 copy-start
  274.3 2.2 copy-start
  285.1 2.2 copy-start
  295.9 2.2 copy-start
  306.7 2.2 copy-start
  317.5 2.2 copy-start
  328.3 2.2 copy-start
  339.1 2.2 copy-start
Sparse Core Ops, SparseCore 0:
  48.5 43.5 all-gather.3
Sparse Core Ops, SparseCore 1:
  102.5 140.9 all-gather.5
where the time goes:
time: 357 us; the launch traced here: 356 us
  waiting for transfers between devices  175 us (49%)
  local copies, waits for them, and re-layouts  55.3 us (15%)
  matrix products  47.8 us (13%)
  blocking collectives  38.6 us (11%)
  between operations  15 us (4%)
  other arithmetic  12.3 us (3%)
  starting transfers between devices  11.1 us (3%)
    all_gather x1, waiting for transfers between devices, shards(): lax.all_gather(out_weight, ('region', 'owner'), axis=0, tiled=True)  118 us
    all_gather x1, waiting for transfers between devices, shards(): lax.all_gather(group_rows, 'region', axis=0, tiled=True)  43.2 us
    all_to_all x1, blocking collectives, from_everyone(): lax.all_to_all(jnp.broadcast_to(value[None], (devices, *value.shape)), ax...  38.6 us
    dot_general x8, matrix products, attend_group(): jnp.einsum('chsk,khd->cshd', attn_probs, value_part, preferred_element_ty...  26.1 us
    while x16, local copies, waits for them, and re-layouts  17.8 us
    dot_general x8, matrix products, attend_group(): jnp.einsum('cshd,khd->chsk', query_part, key_part, preferred_element_type...  13.9 us
    dynamic_slice x16, local copies, waits for them, and re-layouts, attend_group(): lax.dynamic_slice_in_dim(key_rows, offset, group_cols, 1)  12.8 us
    ppermute x2, waiting for transfers between devices, padded(): before = lax.ppermute(last, axis, up)  9.66 us
  transfers between devices with their start and end apart: 6, of which 4 were waited for; matrix products, arithmetic and copies ran while one was open for 2% of the time, Pallas kernels for 0%

commit v1 on v0

v1 whole, which is shorter than its diff:
```python
import functools

import jax
import jax.numpy as jnp
from jax import lax
from jax.experimental import pallas as pl
from jax.experimental.pallas import tpu as pltpu
from jax.sharding import Mesh, PartitionSpec as P


HEAD_DIM = 64
LOG2E = 1.4426950408889634
LINE = ("x", "c")
PLANE = ("y", "z")
BF16 = jnp.bfloat16
F32 = jnp.float32


def norm_kernel(tokens_ref, gain_ref, out_ref):
    widened = tokens_ref[...].astype(F32)
    average = jnp.mean(widened, axis=-1, keepdims=True)
    centred = widened - average
    spread = jnp.mean(centred * centred, axis=-1, keepdims=True)
    out_ref[...] = (centred * lax.rsqrt(spread + 1e-06) * gain_ref[...]).astype(BF16)


def layer_norm(tokens, norm_gain):
    return pl.pallas_call(
        norm_kernel,
        grid=(2,),
        in_specs=[
            pl.BlockSpec((128, 1024), lambda i: (i, 0)),
            pl.BlockSpec((1, 1024), lambda i: (0, 0)),
        ],
        out_specs=pl.BlockSpec((128, 1024), lambda i: (i, 0)),
        out_shape=jax.ShapeDtypeStruct((256, 1024), BF16),
        name="layer_norm",
    )(tokens, norm_gain.reshape(1, 1024))


def shift(value, axis, step):
    n = lax.axis_size(axis)
    return lax.ppermute(value, axis, [(i, (i + step) % n) for i in range(n)])


def from_everyone(value, axes):
    n = lax.axis_size(axes)
    return lax.all_to_all(jnp.broadcast_to(value[None], (n, *value.shape)), axes, 0, 0, tiled=True)


def region_of(slot, x, c):
    parity, place = (slot // 4, slot % 4)
    step = jnp.where(place == 0, 0, jnp.where(place == 1, 3, place - 1))
    return 2 * ((x + step) % 4) + (c + parity) % 2


def slot_of(region, x, c):
    step = (region // 2 - x + 4) % 4
    place = jnp.where(step == 0, 0, jnp.where(step == 3, 1, step + 1))
    return 4 * ((region % 2 + c) % 2) + place


def qkv_kernel(mine_ref, other_ref, weight_ref, kv_ref, query_ref, value_weight):
    slot = pl.program_id(0)

    @pl.when(slot == 0)
    def _():
        value_weight[...] = weight_ref[:, 256:384].T

    def project(tokens):
        both = jnp.dot(tokens, weight_ref[:, :256], preferred_element_type=F32).astype(BF16)
        kv_ref[0, 0:256, :] = both[:, :128]
        query_ref[0] = both[:, 128:]
        values = lax.dot_general(
            value_weight[...], tokens, (((1,), (1,)), ((), ())), preferred_element_type=F32
        ).astype(BF16)
        kv_ref[0, 256:384, :] = values[:, :128]
        kv_ref[0, 384:512, :] = values[:, 128:]

    @pl.when(slot < 4)
    def _():
        project(mine_ref[...])

    @pl.when(slot >= 4)
    def _():
        project(other_ref[...])


def project_qkv(mine, other, weight):
    return pl.pallas_call(
        qkv_kernel,
        grid=(8,),
        in_specs=[
            pl.BlockSpec((256, 1024), lambda s: (jnp.minimum(s, 3), 0)),
            pl.BlockSpec((256, 1024), lambda s: (jnp.maximum(s - 4, 0), 0)),
            pl.BlockSpec((1024, 384), lambda s: (0, 0)),
        ],
        out_specs=[
            pl.BlockSpec((1, 512, 128), lambda s: (s, 0, 0)),
            pl.BlockSpec((1, 256, 128), lambda s: (s, 0, 0)),
        ],
        out_shape=[
            jax.ShapeDtypeStruct((8, 512, 128), BF16),
            jax.ShapeDtypeStruct((8, 256, 128), BF16),
        ],
        scratch_shapes=[pltpu.VMEM((128, 1024), BF16)],
        name="project_qkv",
    )(mine, other, weight)


FACTOR = HEAD_DIM ** (-0.5) * LOG2E


def near_places(table, refs):
    x, c = (table[72], table[73])
    region = region_of(pl.program_id(0), x, c)
    places = []
    for side, ref in refs:
        for step in range(3):
            near = jnp.clip(region + step - 1, 0, 7)
            flag = table[region * 9 + step * 3 + side]
            places.append((ref, slot_of(near, x, c), jnp.where(flag > 0, 0.0, 1e30).astype(F32)))
    return places


def score_places(places, query, cols, score_ref):
    tops = []
    for entry, (ref, slot, penalty) in enumerate(places):
        scores = lax.dot_general(
            ref[slot, 0:256, cols], query, (((1,), (1,)), ((), ())), preferred_element_type=F32
        )
        score_ref[entry] = scores
        tops.append(jnp.max(scores, axis=0, keepdims=True) - penalty)
    return functools.reduce(jnp.maximum, tops) * FACTOR


def mix_places(places, head, top, score_ref):
    ones = jnp.ones((16, 256), BF16)
    totals = []
    for entry, (ref, slot, penalty) in enumerate(places):
        weights = jnp.exp2(score_ref[entry] * FACTOR - (top + penalty)).astype(BF16)
        first = ref[slot, 256 + head * 64 : 320 + head * 64, :]
        second = ref[slot, 384 + head * 64 : 448 + head * 64, :]
        values = jnp.concatenate([jnp.concatenate([first, second], axis=1), ones], axis=0)
        totals.append(jnp.dot(values, weights, preferred_element_type=F32))
    return functools.reduce(jnp.add, totals)


def attend_own_kernel(table, query_ref, own_ref, total_ref, top_ref, score_ref):
    places = near_places(table, [(1, own_ref)])
    for head in range(2):
        cols = slice(head * 64, head * 64 + 64)
        top = score_places(places, query_ref[0, :, cols], cols, score_ref.at[head])
        total_ref[0, head] = mix_places(places, head, top, score_ref.at[head])
        top_ref[0, head] = jnp.broadcast_to(top, (8, 256))


def attend_own(table, queries, own):
    return pl.pallas_call(
        attend_own_kernel,
        grid_spec=pltpu.PrefetchScalarGridSpec(
            num_scalar_prefetch=1,
            grid=(8,),
            in_specs=[
                pl.BlockSpec((1, 256, 128), lambda s, t: (s, 0, 0)),
                pl.BlockSpec(memory_space=pltpu.VMEM),
            ],
            out_specs=[
                pl.BlockSpec((1, 2, 80, 256), lambda s, t: (s, 0, 0, 0)),
                pl.BlockSpec((1, 2, 8, 256), lambda s, t: (s, 0, 0, 0)),
            ],
            scratch_shapes=[pltpu.VMEM((2, 3, 256, 256), F32)],
        ),
        out_shape=[
            jax.ShapeDtypeStruct((8, 2, 80, 256), F32),
            jax.ShapeDtypeStruct((8, 2, 8, 256), F32),
        ],
        name="attend_own",
    )(table, queries, own)


def attend_kernel(
    table, query_ref, low_ref, high_ref, own_total_ref, own_top_ref, out_ref, score_ref
):
    places = near_places(table, [(0, low_ref), (2, high_ref)])
    for head in range(2):
        cols = slice(head * 64, head * 64 + 64)
        own_top = own_top_ref[0, head, 0:1]
        top = score_places(places, query_ref[0, :, cols], cols, score_ref.at[head])
        top = jnp.maximum(top, own_top)
        total = own_total_ref[0, head] * jnp.exp2(own_top - top)
        total += mix_places(places, head, top, score_ref.at[head])
        out_ref[0, cols, :] = (total[:64] / total[64:65]).astype(BF16)


def attend(table, queries, low, high, own_total, own_top):
    whole = pl.BlockSpec(memory_space=pltpu.VMEM)
    return pl.pallas_call(
        attend_kernel,
        grid_spec=pltpu.PrefetchScalarGridSpec(
            num_scalar_prefetch=1,
            grid=(8,),
            in_specs=[
                pl.BlockSpec((1, 256, 128), lambda s, t: (s, 0, 0)),
                whole,
                whole,
                pl.BlockSpec((1, 2, 80, 256), lambda s, t: (s, 0, 0, 0)),
                pl.BlockSpec((1, 2, 8, 256), lambda s, t: (s, 0, 0, 0)),
            ],
            out_specs=pl.BlockSpec(
                (1, 128, 256), lambda s, t: (region_of(s, t[72], t[73]), 0, 0)
            ),
            scratch_shapes=[pltpu.VMEM((2, 6, 256, 256), F32)],
        ),
        out_shape=jax.ShapeDtypeStruct((8, 128, 256), BF16),
        name="attend",
    )(table, queries, low, high, own_total, own_top)


def output_kernel(table, mixed_ref, mine_ref, other_ref, voxels_ref, out_ref):
    x, c = (table[72], table[73])
    total = voxels_ref[...].astype(F32)
    for slot in range(8):
        rows = (mine_ref, other_ref)[slot // 4][slot % 4 * 128 : slot % 4 * 128 + 128, :]
        heads = mixed_ref[region_of(slot, x, c)]
        total += lax.dot_general(
            heads, rows, (((0,), (0,)), ((), ())), preferred_element_type=F32
        )
    out_ref[...] = total.astype(BF16)


def project_out(table, mixed, mine, other, voxels):
    return pl.pallas_call(
        output_kernel,
        grid_spec=pltpu.PrefetchScalarGridSpec(
            num_scalar_prefetch=1,
            grid=(2,),
            in_specs=[
                pl.BlockSpec((8, 128, 256), lambda n, t: (0, 0, 0)),
                pl.BlockSpec((512, 512), lambda n, t: (0, n)),
                pl.BlockSpec((512, 512), lambda n, t: (0, n)),
                pl.BlockSpec((256, 512), lambda n, t: (0, n)),
            ],
            out_specs=pl.BlockSpec((256, 512), lambda n, t: (0, n)),
        ),
        out_shape=jax.ShapeDtypeStruct((256, 1024), BF16),
        name="project_out",
    )(table, mixed, mine, other, voxels)


def gathered_line(value):
    pieces = [value]
    for step in (1, -1, 2):
        pieces.append(shift(value, "x", step))
    mine = jnp.concatenate(pieces, axis=0)
    return (mine, shift(mine, "c", 1))


def layer(voxels, norm_gain, qkv_weight, out_weight, neighbours):
    x, c, y, z = (lax.axis_index(a) for a in ("x", "c", "y", "z"))
    region, owner = (2 * x + c, 8 * y + z)
    tokens = voxels.reshape(256, 1024)
    ids = neighbours.reshape(1, 8)
    entry = jnp.arange(128, dtype=jnp.int32)[:, None]
    near_region = region + entry // 3 - 1
    near_owner = owner + entry % 3 - 1
    inside = (
        (entry < 9) & (near_region >= 0) & (near_region < 8) & (near_owner >= 0) & (near_owner < 64)
    )
    listed = jnp.any((ids == near_region * 64 + near_owner) & inside, axis=1) | (entry[:, 0] == 4)

    normed = layer_norm(tokens, norm_gain)
    mine, other = gathered_line(normed)

    parts = qkv_weight.reshape(2, 3, 8, 128)
    parts = jnp.stack([parts[:, 1], parts[:, 0], parts[:, 2]], axis=2)
    parts = parts.transpose(1, 0, 2, 3).reshape(8, 2, 384)
    flags = jnp.broadcast_to(listed.astype(BF16)[None, None], (8, 2, 128))
    parts = jnp.concatenate([parts, flags], axis=2)
    swapped = lax.all_to_all(parts, LINE, 0, 0, tiled=True)
    table = jnp.concatenate([
        swapped[:, 0, 384:393].astype(jnp.int32).reshape(72),
        jnp.stack([x, c]).astype(jnp.int32),
    ])
    weight = from_everyone(swapped[:, :, :384].reshape(16, 384), PLANE)
    weight = weight.reshape(64, 8, 2, 384).transpose(1, 0, 2, 3).reshape(1024, 384)

    own, queries = project_qkv(mine, other, weight)
    line = [(i, i + 1) for i in range(63)]
    low = lax.ppermute(own, PLANE, line)
    high = lax.ppermute(own, PLANE, [(j, i) for i, j in line])
    own_total, own_top = attend_own(table, queries, own)

    out_rows, _ = lax.optimization_barrier((out_weight, queries))
    out_rows = from_everyone(out_rows, "z").reshape(16, 1024)
    out_rows = from_everyone(out_rows, "y").reshape(128, 1024)
    out_mine, out_other = gathered_line(out_rows)

    mixed = attend(table, queries, low, high, own_total, own_top)
    mixed = lax.all_to_all(mixed, LINE, 0, 0, tiled=True)
    result = project_out(table, mixed, out_mine, out_other, tokens)
    return result.reshape(voxels.shape)


def solution(mesh):
    fine = Mesh(mesh.devices.reshape(4, 2, 8, 8), ("x", "c", "y", "z"))
    return jax.shard_map(
        layer,
        mesh=fine,
        in_specs=(
            P(LINE, PLANE, None, None, None),
            P(),
            P((*LINE, *PLANE), None),
            P((*LINE, *PLANE), None),
            P(LINE, PLANE, None, None),
        ),
        out_specs=P(LINE, PLANE, None, None, None),
        check_vma=False,
    )
```

time: 357 us -> 194 us (0.54)
  waiting for transfers between devices: 175 us -> 31.4 us
  local copies, waits for them, and re-layouts: 55.3 us -> 5.21 us
  matrix products: 47.8 us -> 0 us
  Pallas kernels: 0 us -> 45.3 us
  blocking collectives: 38.6 us -> 71 us
  starting transfers between devices: 11.1 us -> 36.6 us
  between operations: 15 us -> 0.23 us
  other arithmetic: 12.3 us -> 2.92 us
    all_gather x2 -> x0, waiting for transfers between devices: 161 us -> none  [the longest x1 118 us: shards(): lax.all_gather(out_weight, ('region', 'owner'), axis=0, tiled=True)]
    dot_general x18 -> x0, matrix products: 47.8 us -> none  [the longest x8 26.1 us: attend_group(): jnp.einsum('chsk,khd->cshd', attn_probs, value_part, preferred_element_ty...]
    pallas_call x0 -> x5, Pallas kernels: none -> 45.3 us  [the longest x1 18.3 us: attend(): pl.pallas_call(attend_kernel, grid_spec=pltpu.PrefetchScalarGridSpec(num_...]
    all_to_all x1 -> x4, blocking collectives: 38.6 us -> 71 us  [the longest x2 49.9 us: from_everyone(): lax.all_to_all(jnp.broadcast_to(value[None], (n, *value.shape)), axes, 0,...]
    dynamic_slice x40 -> x0, local copies, waits for them, and re-layouts: 22.4 us -> none  [the longest x16 12.8 us: attend_group(): lax.dynamic_slice_in_dim(key_rows, offset, group_cols, 1)]
    ppermute x4 -> x10, starting transfers between devices: 11 us -> 33 us  [the longest x8 29.4 us: shift(): return lax.ppermute(value, axis, [(i, (i + step) % n) for i in range(n)])]
    while x16 -> x0, local copies, waits for them, and re-layouts: 17.8 us -> none
    ppermute x4 -> x10, waiting for transfers between devices: 14.1 us -> 25.5 us  [the longest x8 25.5 us: shift(): return lax.ppermute(value, axis, [(i, (i + step) % n) for i in range(n)])]
  transfers between devices with their start and end apart: 6 -> 11, of which waited for: 4 -> 7; matrix products, arithmetic and copies ran while one was open for 2% -> 2% of each run, Pallas kernels for 0% -> 16%
where the time goes in v1:
time: 194 us; the launch traced here: 193 us
  blocking collectives  71 us (37%)
  Pallas kernels  45.3 us (23%)
  starting transfers between devices  36.6 us (19%)
  waiting for transfers between devices  31.4 us (16%)
  local copies, waits for them, and re-layouts  5.21 us (3%)
  other arithmetic  2.92 us (2%)
    all_to_all x2, blocking collectives, from_everyone(): lax.all_to_all(jnp.broadcast_to(value[None], (n, *value.shape)), axes, 0,...  49.9 us
    ppermute x8, starting transfers between devices, shift(): return lax.ppermute(value, axis, [(i, (i + step) % n) for i in range(n)])  29.4 us
    ppermute x8, waiting for transfers between devices, shift(): return lax.ppermute(value, axis, [(i, (i + step) % n) for i in range(n)])  25.5 us
    pallas_call x1, Pallas kernels, attend(): pl.pallas_call(attend_kernel, grid_spec=pltpu.PrefetchScalarGridSpec(num_...  18.3 us
    all_to_all x1, blocking collectives, layer(): mixed = lax.all_to_all(mixed, LINE, 0, 0, tiled=True)  13.5 us
    pallas_call x1, Pallas kernels, attend_own(): pl.pallas_call(attend_own_kernel, grid_spec=pltpu.PrefetchScalarGridSpec(...  12.1 us
    pallas_call x1, Pallas kernels, project_qkv(): pl.pallas_call(qkv_kernel, grid=(8,), in_specs=[pl.BlockSpec((256, 1024),...  8.07 us
    all_to_all x1, blocking collectives, layer(): swapped = lax.all_to_all(parts, LINE, 0, 0, tiled=True)  7.67 us
  transfers between devices with their start and end apart: 11, of which 7 were waited for; matrix products, arithmetic and copies ran while one was open for 2% of the time, Pallas kernels for 16%

profile of v1, /device:TPU:1, one launch (start us, length us, event | category | flops | bytes accessed | tf_op | source)
XLA Modules:
  0.0 192.6 jit_solution(10455368829229451155)
XLA Ops:
  0.0 2.2 %layer_norm.1 = bf16[256,1024]{1,0:T(8,128)(2,1)} custom-call(bf16[256,1024]{1,0:T(8,128)(2,1)} %bitcast.28, f32[1,1024]{1,0:T(1,128)} %bitcast.36), custom_call_target="tpu_custom_call" | custom-call | tf_op jit(solution)/shard_map/layer_norm/pallas_call | solution.py:28
  2.2 5.5 %collective-permute-start.2 = (bf16[256,1024]{1,0:T(8,128)(2,1)}, bf16[256,1024]{1,0:T(8,128)(2,1)S(1)}, u32[]{:S(2)}, u32[]{:S(2)}) collective-permute-start(bf16[256,1024]{1,0:T(8,128)(2,1)} %layer_norm.1), channel_id=1, source_target_pairs={{0,256},{128,384},{256,0},{384,128},{1,257},{129,385},{257,1},{385... | collective-permute-start | bytes 1572872 | tf_op jit(solution)/shard_map/ppermute | solution.py:43
  7.6 2.8 %collective-permute-start.1 = (bf16[256,1024]{1,0:T(8,128)(2,1)}, bf16[256,1024]{1,0:T(8,128)(2,1)S(1)}, u32[]{:S(2)}, u32[]{:S(2)}) collective-permute-start(bf16[256,1024]{1,0:T(8,128)(2,1)} %layer_norm.1), channel_id=1, source_target_pairs={{0,384},{128,0},{256,128},{384,256},{1,385},{129,1},{257,129},{385... | collective-permute-start | bytes 1572872 | tf_op jit(solution)/shard_map/ppermute | solution.py:43
  10.4 2.5 %collective-permute-start = (bf16[256,1024]{1,0:T(8,128)(2,1)}, bf16[256,1024]{1,0:T(8,128)(2,1)}, u32[]{:S(2)}, u32[]{:S(2)}) collective-permute-start(bf16[256,1024]{1,0:T(8,128)(2,1)} %layer_norm.1), channel_id=1, source_target_pairs={{0,128},{128,256},{256,384},{384,0},{1,129},{129,257},{257,385},{3... | collective-permute-start | bytes 1572872 | tf_op jit(solution)/shard_map/ppermute | solution.py:43
  14.5 1.8 collective-permute-done.2
  16.3 14.6 %collective-permute-done.1 = bf16[256,1024]{1,0:T(8,128)(2,1)S(1)} collective-permute-done((bf16[256,1024]{1,0:T(8,128)(2,1)}, bf16[256,1024]{1,0:T(8,128)(2,1)S(1)}, u32[]{:S(2)}, u32[]{:S(2)}) %collective-permute-start.1) | collective-permute-done | bytes 524320 | tf_op jit(solution)/shard_map/ppermute | solution.py:43
  32.6 4.2 %collective-permute-start.3 = (bf16[1024,1024]{1,0:T(8,128)(2,1)S(1)}, bf16[1024,1024]{1,0:T(8,128)(2,1)}, u32[]{:S(2)}, u32[]{:S(2)}) collective-permute-start(bf16[1024,1024]{1,0:T(8,128)(2,1)S(1)} %pad_maximum_fusion.mine_ref), channel_id=1, source_target_pairs={{0,64},{64,0},{1,65},{65,1},{2,66},{66,2},{3,67},{67,3},{4,68},{68... | collective-permute-start | bytes 6291464 | tf_op jit(solution)/shard_map/ppermute | solution.py:43
  36.8 7.7 %all_to_all.25 = bf16[8,2,512]{2,1,0:T(2,128)(2,1)S(1)} all-to-all(bf16[8,2,512]{2,1,0:T(2,128)(2,1)S(1)} %copy.29), channel_id=1, replica_groups=mesh['x'=4,'c'=2,'y'=8,'z'=8] {'x','c'}, dimensions={0} | all-to-all | bytes 32768 | tf_op jit(solution)/shard_map/all_to_all | solution.py:280
  44.6 37.8 %all_to_all.26 = bf16[64,16,384]{2,1,0:T(8,128)(2,1)S(1)} all-to-all(bf16[64,16,384]{2,1,0:T(8,128)(2,1)S(1)} %broadcast_in_dim.14), channel_id=1, replica_groups=mesh['x'=4,'c'=2,'y'=8,'z'=8] {'y','z'}, dimensions={0} | all-to-all | bytes 1572864 | tf_op jit(solution)/shard_map/all_to_all | solution.py:48
  84.7 8.1 %project_qkv.1 = (bf16[8,512,128]{2,1,0:T(8,128)(2,1)}, bf16[8,256,128]{2,1,0:T(8,128)(2,1)}) custom-call(bf16[1024,1024]{1,0:T(8,128)(2,1)} %copy-done, bf16[1024,1024]{1,0:T(8,128)(2,1)} %collective-permute-done.3.other_ref, bf16[1024,384]{1,0:T(8,128)(2,1)} %reshape.113.weight_ref), custom_call_target="tpu_custom_call" | custom-call | tf_op jit(solution)/shard_map/project_qkv/pallas_call | solution.py:90
  92.8 12.1 %all_to_all.27 = bf16[8,2,1024]{2,1,0:T(2,128)(2,1)S(1)} all-to-all(bf16[8,2,1024]{2,1,0:T(2,128)(2,1)S(1)} %broadcast_in_dim.30), channel_id=1, replica_groups=mesh['x'=4,'c'=2,'y'=8,'z'=8] {'z'}, dimensions={0} | all-to-all | bytes 65536 | tf_op jit(solution)/shard_map/all_to_all | solution.py:48
  105.6 3.6 %all-to-all-start.4 = ((bf16[8,16,1024]{2,1,0:T(8,128)(2,1)}), bf16[8,16,1024]{2,1,0:T(8,128)(2,1)S(1)}, u32[]{:S(2)}, u32[]{:S(2)}) async-start(bf16[8,16,1024]{2,1,0:T(8,128)(2,1)} %broadcast_in_dim.32), calls=%async_computation.4 | async-start | bytes 524288 | tf_op jit(solution)/shard_map/all_to_all | solution.py:48
  109.2 2.2 %collective-permute-start.4 = (bf16[8,512,128]{2,1,0:T(8,128)(2,1)}, bf16[8,512,128]{2,1,0:T(8,128)(2,1)S(1)}, u32[]{:S(2)}, u32[]{:S(2)}) collective-permute-start(bf16[8,512,128]{2,1,0:T(8,128)(2,1)} %get-tuple-element.11.own_ref), channel_id=1, source_target_pairs={{0,1},{1,2},{2,3},{3,4},{4,5},{5,6},{6,7},{7,8},{8,9},{9,10},{10,1... | collective-permute-start | bytes 3145736 | tf_op jit(solution)/shard_map/ppermute | solution.py:290
  112.8 5.9 %all-to-all-done.4 = bf16[8,16,1024]{2,1,0:T(8,128)(2,1)S(1)} async-done(((bf16[8,16,1024]{2,1,0:T(8,128)(2,1)}), bf16[8,16,1024]{2,1,0:T(8,128)(2,1)S(1)}, u32[]{:S(2)}, u32[]{:S(2)}) %all-to-all-start.4) | async-done | bytes 262176 | tf_op jit(solution)/shard_map/all_to_all | solution.py:48
  118.7 2.7 %collective-permute-start.8 = (bf16[128,1024]{1,0:T(8,128)(2,1)S(1)}, bf16[128,1024]{1,0:T(8,128)(2,1)S(1)}, u32[]{:S(2)}, u32[]{:S(2)}) collective-permute-start(bf16[128,1024]{1,0:T(8,128)(2,1)S(1)} %bitcast.30), channel_id=1, source_target_pairs={{0,256},{128,384},{256,0},{384,128},{1,257},{129,385},{257,1},{385... | collective-permute-start | bytes 786440 | tf_op jit(solution)/shard_map/ppermute | solution.py:43
  121.4 3.7 %collective-permute-start.7 = (bf16[128,1024]{1,0:T(8,128)(2,1)S(1)}, bf16[128,1024]{1,0:T(8,128)(2,1)S(1)}, u32[]{:S(2)}, u32[]{:S(2)}) collective-permute-start(bf16[128,1024]{1,0:T(8,128)(2,1)S(1)} %bitcast.31), channel_id=1, source_target_pairs={{0,384},{128,0},{256,128},{384,256},{1,385},{129,1},{257,129},{385... | collective-permute-start | bytes 786440 | tf_op jit(solution)/shard_map/ppermute | solution.py:43
  125.1 1.9 collective-permute-start.6
  127.3 4.0 %collective-permute-done.7 = bf16[128,1024]{1,0:T(8,128)(2,1)S(1)} collective-permute-done((bf16[128,1024]{1,0:T(8,128)(2,1)S(1)}, bf16[128,1024]{1,0:T(8,128)(2,1)S(1)}, u32[]{:S(2)}, u32[]{:S(2)}) %collective-permute-start.7) | collective-permute-done | bytes 262176 | tf_op jit(solution)/shard_map/ppermute | solution.py:43
  131.2 4.5 %collective-permute-done.6 = bf16[128,1024]{1,0:T(8,128)(2,1)S(1)} collective-permute-done((bf16[128,1024]{1,0:T(8,128)(2,1)S(1)}, bf16[128,1024]{1,0:T(8,128)(2,1)S(1)}, u32[]{:S(2)}, u32[]{:S(2)}) %collective-permute-start.6) | collective-permute-done | bytes 262176 | tf_op jit(solution)/shard_map/ppermute | solution.py:43
  135.9 6.1 %collective-permute-start.9 = (bf16[512,1024]{1,0:T(8,128)(2,1)S(1)}, bf16[512,1024]{1,0:T(8,128)(2,1)}, u32[]{:S(2)}, u32[]{:S(2)}) collective-permute-start(bf16[512,1024]{1,0:T(8,128)(2,1)S(1)} %pad_maximum_fusion.1.mine_ref), channel_id=1, source_target_pairs={{0,64},{64,0},{1,65},{65,1},{2,66},{66,2},{3,67},{67,3},{4,68},{68... | collective-permute-start | bytes 3145736 | tf_op jit(solution)/shard_map/ppermute | solution.py:43
  142.8 12.1 %attend_own.1 = (f32[8,2,80,256]{3,2,1,0:T(8,128)}, f32[8,2,8,256]{3,2,1,0:T(8,128)}) custom-call(s32[74]{0:T(128)} %pad_add_fusion.table, bf16[8,256,128]{2,1,0:T(8,128)(2,1)} %get-tuple-element.10.query_ref, bf16[8,512,128]{2,1,0:T(8,128)(2,1)} %get-tuple-element.11.own_ref), custom_call_target="tpu_custom_call" | custom-call | tf_op jit(solution)/shard_map/attend_own/pallas_call | solution.py:159
  156.2 18.3 %attend.1 = bf16[8,128,256]{2,1,0:T(8,128)(2,1)} custom-call(s32[74]{0:T(128)} %pad_add_fusion.table, bf16[8,256,128]{2,1,0:T(8,128)(2,1)} %get-tuple-element.10.query_ref, bf16[8,512,128]{2,1,0:T(8,128)(2,1)} %copy-done.2, bf16[8,512,128]{2,1,0:T(8,128)(2,1)} %copy-done.3, f32[8,2,80,256]{3,2,1,0:T(8,128)} %get-tuple-element.12.own_total_ref, ...), custom_call_target="tpu_custom_call" | custom-call | tf_op jit(solution)/shard_map/attend/pallas_call | solution.py:198
  174.5 13.5 %all_to_all.28.mixed_ref = bf16[8,128,256]{2,1,0:T(8,128)(2,1)} all-to-all(bf16[8,128,256]{2,1,0:T(8,128)(2,1)} %attend.1), channel_id=1, replica_groups=mesh['x'=4,'c'=2,'y'=8,'z'=8] {'x','c'}, dimensions={0} | all-to-all | bytes 1048576 | tf_op jit(solution)/shard_map/all_to_all | solution.py:300
  188.0 4.6 %project_out.1 = bf16[256,1024]{1,0:T(8,128)(2,1)} custom-call(s32[74]{0:T(128)} %pad_add_fusion.table, bf16[8,128,256]{2,1,0:T(8,128)(2,1)} %all_to_all.28.mixed_ref, bf16[512,1024]{1,0:T(8,128)(2,1)} %copy-done.1, bf16[512,1024]{1,0:T(8,128)(2,1)} %collective-permute-done.9.other_ref, bf16[256,1024]{1,0:T(8,128)(2,1)} %bitcast.29), custom_call_target="tpu_custom_call" | custom-call | tf_op jit(solution)/shard_map/project_out/pallas_call | solution.py:233
  (41 shorter events, 9.9 us)
Async XLA Ops:
  2.2 14.1 %collective-permute-start.2 = (bf16[256,1024]{1,0:T(8,128)(2,1)}, bf16[256,1024]{1,0:T(8,128)(2,1)S(1)}, u32[]{:S(2)}, u32[]{:S(2)}) collective-permute-start(bf16[256,1024]{1,0:T(8,128)(2,1)} %layer_norm.1), channel_id=1, source_target_pairs={{0,256},{128,384},{256,0},{384,128},{1,257},{129,385},{257,1},{385... | collective-permute-start | bytes 1572872 | tf_op jit(solution)/shard_map/ppermute | solution.py:43
  7.6 23.2 %collective-permute-start.1 = (bf16[256,1024]{1,0:T(8,128)(2,1)}, bf16[256,1024]{1,0:T(8,128)(2,1)S(1)}, u32[]{:S(2)}, u32[]{:S(2)}) collective-permute-start(bf16[256,1024]{1,0:T(8,128)(2,1)} %layer_norm.1), channel_id=1, source_target_pairs={{0,384},{128,0},{256,128},{384,256},{1,385},{129,1},{257,129},{385... | collective-permute-start | bytes 1572872 | tf_op jit(solution)/shard_map/ppermute | solution.py:43
  10.4 20.8 %collective-permute-start = (bf16[256,1024]{1,0:T(8,128)(2,1)}, bf16[256,1024]{1,0:T(8,128)(2,1)}, u32[]{:S(2)}, u32[]{:S(2)}) collective-permute-start(bf16[256,1024]{1,0:T(8,128)(2,1)} %layer_norm.1), channel_id=1, source_target_pairs={{0,128},{128,256},{256,384},{384,0},{1,129},{129,257},{257,385},{3... | collective-permute-start | bytes 1572872 | tf_op jit(solution)/shard_map/ppermute | solution.py:43
  32.6 50.9 %copy-start = (bf16[1024,1024]{1,0:T(8,128)(2,1)}, bf16[1024,1024]{1,0:T(8,128)(2,1)S(1)}, u32[]{:S(2)}) copy-start(bf16[1024,1024]{1,0:T(8,128)(2,1)S(1)} %pad_maximum_fusion.mine_ref) | copy-start | bytes 6291460
  32.6 52.1 %collective-permute-start.3 = (bf16[1024,1024]{1,0:T(8,128)(2,1)S(1)}, bf16[1024,1024]{1,0:T(8,128)(2,1)}, u32[]{:S(2)}, u32[]{:S(2)}) collective-permute-start(bf16[1024,1024]{1,0:T(8,128)(2,1)S(1)} %pad_maximum_fusion.mine_ref), channel_id=1, source_target_pairs={{0,64},{64,0},{1,65},{65,1},{2,66},{66,2},{3,67},{67,3},{4,68},{68... | collective-permute-start | bytes 6291464 | tf_op jit(solution)/shard_map/ppermute | solution.py:43
  84.7 8.1 %copy-start.4 = (bf16[2,1024]{1,0:T(2,128)(2,1)S(1)}, bf16[2,1024]{1,0:T(2,128)(2,1)}, u32[]{:S(2)}) copy-start(bf16[2,1024]{1,0:T(2,128)(2,1)} %param.8) | copy-start | bytes 12292
  105.6 13.0 %all-to-all-start.4 = ((bf16[8,16,1024]{2,1,0:T(8,128)(2,1)}), bf16[8,16,1024]{2,1,0:T(8,128)(2,1)S(1)}, u32[]{:S(2)}, u32[]{:S(2)}) async-start(bf16[8,16,1024]{2,1,0:T(8,128)(2,1)} %broadcast_in_dim.32), calls=%async_computation.4 | async-start | bytes 524288 | tf_op jit(solution)/shard_map/all_to_all | solution.py:48
  109.2 45.7 %collective-permute-start.4 = (bf16[8,512,128]{2,1,0:T(8,128)(2,1)}, bf16[8,512,128]{2,1,0:T(8,128)(2,1)S(1)}, u32[]{:S(2)}, u32[]{:S(2)}) collective-permute-start(bf16[8,512,128]{2,1,0:T(8,128)(2,1)} %get-tuple-element.11.own_ref), channel_id=1, source_target_pairs={{0,1},{1,2},{2,3},{3,4},{4,5},{5,6},{6,7},{7,8},{8,9},{9,10},{10,1... | collective-permute-start | bytes 3145736 | tf_op jit(solution)/shard_map/ppermute | solution.py:290
  111.5 43.4 %collective-permute-start.5 = (bf16[8,512,128]{2,1,0:T(8,128)(2,1)}, bf16[8,512,128]{2,1,0:T(8,128)(2,1)S(1)}, u32[]{:S(2)}, u32[]{:S(2)}) collective-permute-start(bf16[8,512,128]{2,1,0:T(8,128)(2,1)} %get-tuple-element.11.own_ref), channel_id=1, source_target_pairs={{1,0},{2,1},{3,2},{4,3},{5,4},{6,5},{7,6},{8,7},{9,8},{10,9},{11,1... | collective-permute-start | bytes 3145736 | tf_op jit(solution)/shard_map/ppermute | solution.py:291
  118.7 8.6 %collective-permute-start.8 = (bf16[128,1024]{1,0:T(8,128)(2,1)S(1)}, bf16[128,1024]{1,0:T(8,128)(2,1)S(1)}, u32[]{:S(2)}, u32[]{:S(2)}) collective-permute-start(bf16[128,1024]{1,0:T(8,128)(2,1)S(1)} %bitcast.30), channel_id=1, source_target_pairs={{0,256},{128,384},{256,0},{384,128},{1,257},{129,385},{257,1},{385... | collective-permute-start | bytes 786440 | tf_op jit(solution)/shard_map/ppermute | solution.py:43
  121.4 9.9 %collective-permute-start.7 = (bf16[128,1024]{1,0:T(8,128)(2,1)S(1)}, bf16[128,1024]{1,0:T(8,128)(2,1)S(1)}, u32[]{:S(2)}, u32[]{:S(2)}) collective-permute-start(bf16[128,1024]{1,0:T(8,128)(2,1)S(1)} %bitcast.31), channel_id=1, source_target_pairs={{0,384},{128,0},{256,128},{384,256},{1,385},{129,1},{257,129},{385... | collective-permute-start | bytes 786440 | tf_op jit(solution)/shard_map/ppermute | solution.py:43
  125.1 10.7 %collective-permute-start.6 = (bf16[128,1024]{1,0:T(8,128)(2,1)S(1)}, bf16[128,1024]{1,0:T(8,128)(2,1)S(1)}, u32[]{:S(2)}, u32[]{:S(2)}) collective-permute-start(bf16[128,1024]{1,0:T(8,128)(2,1)S(1)} %bitcast.32), channel_id=1, source_target_pairs={{0,128},{128,256},{256,384},{384,0},{1,129},{129,257},{257,385},{3... | collective-permute-start | bytes 786440 | tf_op jit(solution)/shard_map/ppermute | solution.py:43
  135.9 38.7 %copy-start.1 = (bf16[512,1024]{1,0:T(8,128)(2,1)}, bf16[512,1024]{1,0:T(8,128)(2,1)S(1)}, u32[]{:S(2)}) copy-start(bf16[512,1024]{1,0:T(8,128)(2,1)S(1)} %pad_maximum_fusion.1.mine_ref) | copy-start | bytes 3145732
  135.9 52.1 %collective-permute-start.9 = (bf16[512,1024]{1,0:T(8,128)(2,1)S(1)}, bf16[512,1024]{1,0:T(8,128)(2,1)}, u32[]{:S(2)}, u32[]{:S(2)}) collective-permute-start(bf16[512,1024]{1,0:T(8,128)(2,1)S(1)} %pad_maximum_fusion.1.mine_ref), channel_id=1, source_target_pairs={{0,64},{64,0},{1,65},{65,1},{2,66},{66,2},{3,67},{67,3},{4,68},{68... | collective-permute-start | bytes 3145736 | tf_op jit(solution)/shard_map/ppermute | solution.py:43
  154.9 1.0 copy-start.2
  154.9 1.3 copy-start.3

commit v2 on v1

v2 whole, which is shorter than its diff:
```python
import functools

import jax
import jax.numpy as jnp
from jax import lax
from jax.experimental import pallas as pl
from jax.experimental.pallas import tpu as pltpu
from jax.sharding import Mesh, PartitionSpec as P


HEAD_DIM = 64
FACTOR = HEAD_DIM ** (-0.5) * 1.4426950408889634
LINE = ("x", "c")
PLANE = ("y", "z")
BF16 = jnp.bfloat16
F32 = jnp.float32


def norm_kernel(tokens_ref, gain_ref, out_ref):
    widened = tokens_ref[...].astype(F32)
    average = jnp.mean(widened, axis=-1, keepdims=True)
    centred = widened - average
    spread = jnp.mean(centred * centred, axis=-1, keepdims=True)
    out_ref[...] = (centred * lax.rsqrt(spread + 1e-06) * gain_ref[...]).astype(BF16)


def layer_norm(tokens, norm_gain):
    return pl.pallas_call(
        norm_kernel,
        grid=(2,),
        in_specs=[
            pl.BlockSpec((128, 1024), lambda i: (i, 0)),
            pl.BlockSpec((1, 1024), lambda i: (0, 0)),
        ],
        out_specs=pl.BlockSpec((128, 1024), lambda i: (i, 0)),
        out_shape=jax.ShapeDtypeStruct((256, 1024), BF16),
        name="layer_norm",
    )(tokens, norm_gain.reshape(1, 1024))


def shift(value, axis, step):
    n = lax.axis_size(axis)
    return lax.ppermute(value, axis, [(i, (i + step) % n) for i in range(n)])


def from_everyone(value, axes):
    n = lax.axis_size(axes)
    return lax.all_to_all(jnp.broadcast_to(value[None], (n, *value.shape)), axes, 0, 0, tiled=True)


def region_of(slot, x, c):
    parity, place = (slot // 4, slot % 4)
    step = jnp.where(place == 0, 0, jnp.where(place == 1, 3, place - 1))
    return 2 * ((x + step) % 4) + (c + parity) % 2


def slot_of(region, x, c):
    step = (region // 2 - x + 4) % 4
    place = jnp.where(step == 0, 0, jnp.where(step == 3, 1, step + 1))
    return 4 * ((region % 2 + c) % 2) + place


def qkv_kernel(mine_ref, other_ref, weight_ref, kv_ref, query_ref):
    def project(tokens_ref):
        projected = jnp.dot(tokens_ref[...], weight_ref[...], preferred_element_type=F32)
        for block in range(4):
            rows = slice(block * 256, block * 256 + 256)
            kv_ref[block, 0:256, :] = projected[rows, :128].astype(BF16)
            values = projected[rows, 128:256].astype(BF16).T
            kv_ref[block, 256:384, :] = values[:, :128]
            kv_ref[block, 384:512, :] = values[:, 128:]
            query_ref[block] = (projected[rows, 256:] * FACTOR).astype(BF16)

    @pl.when(pl.program_id(0) == 0)
    def _():
        project(mine_ref)

    @pl.when(pl.program_id(0) == 1)
    def _():
        project(other_ref)


def project_qkv(mine, other, weight):
    return pl.pallas_call(
        qkv_kernel,
        grid=(2,),
        in_specs=[
            pl.BlockSpec((1024, 1024), lambda s: (0, 0)),
            pl.BlockSpec((1024, 1024), lambda s: (0, 0)),
            pl.BlockSpec((1024, 384), lambda s: (0, 0)),
        ],
        out_specs=[
            pl.BlockSpec((4, 512, 128), lambda s: (s, 0, 0)),
            pl.BlockSpec((4, 256, 128), lambda s: (s, 0, 0)),
        ],
        out_shape=[
            jax.ShapeDtypeStruct((8, 512, 128), BF16),
            jax.ShapeDtypeStruct((8, 256, 128), BF16),
        ],
        name="project_qkv",
    )(mine, other, weight)


def near_places(table, slot, refs):
    x, c = (table[72], table[73])
    region = region_of(slot, x, c)
    places = []
    for side, ref in refs:
        for step in range(3):
            near = jnp.clip(region + step - 1, 0, 7)
            flag = table[region * 9 + step * 3 + side]
            places.append((ref, slot_of(near, x, c), jnp.where(flag > 0, 0.0, 1e30).astype(F32)))
    return places


def run_units(table, query_ref, refs, score_ref, weight_ref, known_top, finish):
    lanes = lax.broadcasted_iota(jnp.int32, (256, 128), 1)
    units = []
    for place in range(2):
        places = near_places(table, pl.program_id(0) * 2 + place, refs)
        for head in range(2):
            inside = (lanes >= head * 64) & (lanes < head * 64 + 64)
            query = jnp.where(inside, query_ref[place], jnp.zeros((), BF16))
            units.append((place, head, places, query))
    count = len(units[0][2])
    ones = jnp.ones((16, count * 256), BF16)
    tops = []
    for turn in range(5):
        column_tops = []
        for entry in range(count):
            rows = slice(entry * 256, entry * 256 + 256)
            if turn < 4:
                _, _, places, query = units[turn]
                ref, slot, penalty = places[entry]
                scores = lax.dot_general(
                    ref[slot, 0:256, :], query, (((1,), (1,)), ((), ())),
                    preferred_element_type=F32,
                )
                score_ref[turn % 2, rows] = scores
                column_tops.append(jnp.max(scores, axis=0, keepdims=True) - penalty)
            if turn > 0:
                penalty = units[turn - 1][2][entry][2]
                weight_ref[(turn - 1) % 2, rows] = jnp.exp2(
                    score_ref[(turn - 1) % 2, rows] - (tops[-1] + penalty)
                ).astype(BF16)
        if turn > 0:
            place, head, places, _ = units[turn - 1]
            halves = []
            for ref, slot, _ in places:
                halves.append(ref[slot, 256 + head * 64 : 320 + head * 64, :])
                halves.append(ref[slot, 384 + head * 64 : 448 + head * 64, :])
            values = jnp.concatenate([jnp.concatenate(halves, axis=1), ones], axis=0)
            total = jnp.dot(values, weight_ref[(turn - 1) % 2], preferred_element_type=F32)
            finish(place, head, tops[-1], total)
        if turn < 4:
            top = functools.reduce(jnp.maximum, column_tops)
            if known_top is not None:
                top = jnp.maximum(top, known_top(*units[turn][:2]))
            tops.append(top)


def attend_own_kernel(
    table, query_ref, own_ref, total_ref, top_ref, score_ref, weight_ref
):
    def finish(place, head, top, total):
        total_ref[place, head] = total
        top_ref[place, head] = jnp.broadcast_to(top, (8, 256))

    run_units(table, query_ref, [(1, own_ref)], score_ref, weight_ref, None, finish)


WHOLE = pl.BlockSpec((8, 512, 128), lambda s, t: (0, 0, 0), pipeline_mode=pl.Buffered(1))


def attend_own(table, queries, own):
    return pl.pallas_call(
        attend_own_kernel,
        grid_spec=pltpu.PrefetchScalarGridSpec(
            num_scalar_prefetch=1,
            grid=(4,),
            in_specs=[pl.BlockSpec((2, 256, 128), lambda s, t: (s, 0, 0)), WHOLE],
            out_specs=[
                pl.BlockSpec((2, 2, 80, 256), lambda s, t: (s, 0, 0, 0)),
                pl.BlockSpec((2, 2, 8, 256), lambda s, t: (s, 0, 0, 0)),
            ],
            scratch_shapes=[pltpu.VMEM((2, 768, 256), F32), pltpu.VMEM((2, 768, 256), BF16)],
        ),
        out_shape=[
            jax.ShapeDtypeStruct((8, 2, 80, 256), F32),
            jax.ShapeDtypeStruct((8, 2, 8, 256), F32),
        ],
        name="attend_own",
    )(table, queries, own)


def attend_kernel(
    table, query_ref, low_ref, high_ref, own_total_ref, own_top_ref, out_ref, score_ref, weight_ref
):
    def known_top(place, head):
        return own_top_ref[place, head, 0:1]

    def finish(place, head, top, total):
        total += own_total_ref[place, head] * jnp.exp2(known_top(place, head) - top)
        region = region_of(pl.program_id(0) * 2 + place, table[72], table[73])
        out_ref[region, head * 64 : head * 64 + 64, :] = (total[:64] / total[64:65]).astype(BF16)

    run_units(table, query_ref, [(0, low_ref), (2, high_ref)], score_ref, weight_ref, known_top, finish)


def attend(table, queries, low, high, own_total, own_top):
    return pl.pallas_call(
        attend_kernel,
        grid_spec=pltpu.PrefetchScalarGridSpec(
            num_scalar_prefetch=1,
            grid=(4,),
            in_specs=[
                pl.BlockSpec((2, 256, 128), lambda s, t: (s, 0, 0)),
                WHOLE,
                WHOLE,
                pl.BlockSpec((2, 2, 80, 256), lambda s, t: (s, 0, 0, 0)),
                pl.BlockSpec((2, 2, 8, 256), lambda s, t: (s, 0, 0, 0)),
            ],
            out_specs=pl.BlockSpec((8, 128, 256), lambda s, t: (0, 0, 0)),
            scratch_shapes=[pltpu.VMEM((2, 1536, 256), F32), pltpu.VMEM((2, 1536, 256), BF16)],
        ),
        out_shape=jax.ShapeDtypeStruct((8, 128, 256), BF16),
        name="attend",
    )(table, queries, low, high, own_total, own_top)


def output_kernel(table, mixed_ref, mine_ref, other_ref, voxels_ref, out_ref):
    mixed = mixed_ref[...].T
    for pair in range(4):
        ref = (mine_ref, other_ref)[pair // 2]
        slots = (2 * pair, 2 * pair + 1)
        weight = jnp.concatenate([ref[slot % 4] for slot in slots], axis=1)
        projected = jnp.dot(mixed, weight, preferred_element_type=F32)
        for place, slot in enumerate(slots):
            start = pl.multiple_of(region_of(slot, table[72], table[73]) * 128, 128)
            cols = pl.ds(start, 128)
            part = projected[:, place * 128 : place * 128 + 128]
            out_ref[:, cols] = (voxels_ref[:, cols].astype(F32) + part).astype(BF16)


def project_out(table, mixed, mine, other, voxels):
    return pl.pallas_call(
        output_kernel,
        grid_spec=pltpu.PrefetchScalarGridSpec(
            num_scalar_prefetch=1,
            grid=(1,),
            in_specs=[
                pl.BlockSpec((1024, 256), lambda n, t: (0, 0)),
                pl.BlockSpec((4, 1024, 128), lambda n, t: (0, 0, 0)),
                pl.BlockSpec((4, 1024, 128), lambda n, t: (0, 0, 0)),
                pl.BlockSpec((256, 1024), lambda n, t: (0, 0)),
            ],
            out_specs=pl.BlockSpec((256, 1024), lambda n, t: (0, 0)),
        ),
        out_shape=jax.ShapeDtypeStruct((256, 1024), BF16),
        name="project_out",
    )(table, mixed, mine, other, voxels)


def gathered_line(value):
    pieces = [value]
    for step in (1, -1, 2):
        pieces.append(shift(value, "x", step))
    mine = jnp.concatenate(pieces, axis=0)
    return (mine, shift(mine, "c", 1))


def layer(voxels, norm_gain, qkv_weight, out_weight, neighbours):
    x, c, y, z = (lax.axis_index(a) for a in ("x", "c", "y", "z"))
    region, owner = (2 * x + c, 8 * y + z)
    tokens = voxels.reshape(256, 1024)
    ids = neighbours.reshape(1, 8)
    entry = jnp.arange(128, dtype=jnp.int32)[:, None]
    near_region = region + entry // 3 - 1
    near_owner = owner + entry % 3 - 1
    inside = (
        (entry < 9) & (near_region >= 0) & (near_region < 8) & (near_owner >= 0) & (near_owner < 64)
    )
    listed = jnp.any((ids == near_region * 64 + near_owner) & inside, axis=1) | (entry[:, 0] == 4)

    normed = layer_norm(tokens, norm_gain)
    mine, other = gathered_line(normed)

    parts = qkv_weight.reshape(2, 3, 8, 128)
    flags = jnp.broadcast_to(listed.astype(BF16)[None, None], (2, 8, 128))
    parts = [parts[:, 1], parts[:, 2], parts[:, 0], out_weight.reshape(2, 8, 128), flags]
    parts = jnp.stack(parts, axis=2).transpose(1, 0, 2, 3).reshape(8, 2, 640)
    swapped = lax.all_to_all(parts, LINE, 0, 0, tiled=True)
    table = jnp.concatenate([
        swapped[:, 0, 512:521].astype(jnp.int32).reshape(72),
        jnp.stack([x, c]).astype(jnp.int32),
    ])

    def in_row_order(weight):
        width = weight.shape[-1]
        return weight.reshape(64, 8, 2, width).transpose(1, 0, 2, 3).reshape(1024, width)

    weight = from_everyone(swapped[:, :, :384].reshape(16, 384), PLANE)
    own, queries = project_qkv(mine, other, in_row_order(weight))
    line = [(i, i + 1) for i in range(63)]
    low = lax.ppermute(own, PLANE, line)
    high = lax.ppermute(own, PLANE, [(j, i) for i, j in line])

    out_part, _ = lax.optimization_barrier((swapped[:, :, 384:512], queries))
    out_part = from_everyone(out_part.reshape(16, 128), PLANE)
    own_total, own_top = attend_own(table, queries, own)
    out_part = in_row_order(out_part)
    out_mine, out_other = gathered_line(out_part)
    mixed = attend(table, queries, low, high, own_total, own_top)
    mixed = lax.all_to_all(mixed, LINE, 0, 0, tiled=True).reshape(1024, 256)
    out_mine, out_other = (part.reshape(4, 1024, 128) for part in (out_mine, out_other))
    result = project_out(table, mixed, out_mine, out_other, tokens)
    return result.reshape(voxels.shape)


def solution(mesh):
    fine = Mesh(mesh.devices.reshape(4, 2, 8, 8), ("x", "c", "y", "z"))
    return jax.shard_map(
        layer,
        mesh=fine,
        in_specs=(
            P(LINE, PLANE, None, None, None),
            P(),
            P((*LINE, *PLANE), None),
            P((*LINE, *PLANE), None),
            P(LINE, PLANE, None, None),
        ),
        out_specs=P(LINE, PLANE, None, None, None),
        check_vma=False,
    )
```

time: 194 us -> 184 us (0.948)
  blocking collectives: 71 us -> 47 us
  waiting for transfers between devices: 31.4 us -> 45 us
  starting transfers between devices: 36.6 us -> 49.7 us
  Pallas kernels: 45.3 us -> 32.8 us
    all_to_all x2 -> x1, blocking collectives: 49.9 us -> 20.7 us  [from_everyone(): lax.all_to_all(jnp.broadcast_to(value[None], (n, *value.shape)), axes, 0,...]
    all_to_all x1, waiting for transfers between devices: 5.89 us -> 21.7 us  [from_everyone(): lax.all_to_all(jnp.broadcast_to(value[None], (n, *value.shape)), axes, 0,...]
    all_to_all x1, starting transfers between devices: 3.59 us -> 16.3 us  [from_everyone(): lax.all_to_all(jnp.broadcast_to(value[None], (n, *value.shape)), axes, 0,...]
    pallas_call x1, Pallas kernels: 18.3 us -> 12.5 us  [attend(): pl.pallas_call(attend_kernel, grid_spec=pltpu.PrefetchScalarGridSpec(num_...]
    ppermute x8, waiting for transfers between devices: 25.5 us -> 20 us  [shift(): return lax.ppermute(value, axis, [(i, (i + step) % n) for i in range(n)])]
    all_to_all x1, blocking collectives: 13.5 us -> 18.5 us  [layer(): mixed = lax.all_to_all(mixed, LINE, 0, 0, tiled=True).reshape(1024, 256)]
    pallas_call x1, Pallas kernels: 12.1 us -> 7.98 us  [attend_own(): pl.pallas_call(attend_own_kernel, grid_spec=pltpu.PrefetchScalarGridSpec(...]
    ppermute x1, waiting for transfers between devices: 0.01 us -> 3.21 us  [layer(): high = lax.ppermute(own, PLANE, [(j, i) for i, j in line])]
  transfers between devices with their start and end apart: 11 -> 11, of which waited for: 7 -> 7; matrix products, arithmetic and copies ran while one was open for 2% -> 3% of each run, Pallas kernels for 16% -> 11%
where the time goes in v2:
time: 184 us; the launch traced here: 183 us
  starting transfers between devices  49.7 us (27%)
  blocking collectives  47 us (26%)
  waiting for transfers between devices  45 us (24%)
  Pallas kernels  32.8 us (18%)
  local copies, waits for them, and re-layouts  5.43 us (3%)
  other arithmetic  2.88 us (2%)
    ppermute x8, starting transfers between devices, shift(): return lax.ppermute(value, axis, [(i, (i + step) % n) for i in range(n)])  29.4 us
    all_to_all x1, waiting for transfers between devices, from_everyone(): lax.all_to_all(jnp.broadcast_to(value[None], (n, *value.shape)), axes, 0,...  21.7 us
    all_to_all x1, blocking collectives, from_everyone(): lax.all_to_all(jnp.broadcast_to(value[None], (n, *value.shape)), axes, 0,...  20.7 us
    ppermute x8, waiting for transfers between devices, shift(): return lax.ppermute(value, axis, [(i, (i + step) % n) for i in range(n)])  20 us
    all_to_all x1, blocking collectives, layer(): mixed = lax.all_to_all(mixed, LINE, 0, 0, tiled=True).reshape(1024, 256)  18.5 us
    all_to_all x1, starting transfers between devices, from_everyone(): lax.all_to_all(jnp.broadcast_to(value[None], (n, *value.shape)), axes, 0,...  16.3 us
    pallas_call x1, Pallas kernels, attend(): pl.pallas_call(attend_kernel, grid_spec=pltpu.PrefetchScalarGridSpec(num_...  12.5 us
    pallas_call x1, Pallas kernels, attend_own(): pl.pallas_call(attend_own_kernel, grid_spec=pltpu.PrefetchScalarGridSpec(...  7.98 us
  transfers between devices with their start and end apart: 11, of which 7 were waited for; matrix products, arithmetic and copies ran while one was open for 3% of the time, Pallas kernels for 11%

profile of v2, /device:TPU:1, one launch (start us, length us, event | category | flops | bytes accessed | tf_op | source)
XLA Modules:
  0.0 183.0 jit_solution(2143744294292185861)
XLA Ops:
  0.0 2.2 %layer_norm.1 = bf16[256,1024]{1,0:T(8,128)(2,1)} custom-call(bf16[256,1024]{1,0:T(8,128)(2,1)} %bitcast.42, f32[1,1024]{1,0:T(1,128)} %bitcast.56), custom_call_target="tpu_custom_call" | custom-call | tf_op jit(solution)/shard_map/layer_norm/pallas_call | solution.py:28
  2.2 5.5 %collective-permute-start.2 = (bf16[256,1024]{1,0:T(8,128)(2,1)}, bf16[256,1024]{1,0:T(8,128)(2,1)S(1)}, u32[]{:S(2)}, u32[]{:S(2)}) collective-permute-start(bf16[256,1024]{1,0:T(8,128)(2,1)} %layer_norm.1), channel_id=1, source_target_pairs={{0,256},{128,384},{256,0},{384,128},{1,257},{129,385},{257,1},{385... | collective-permute-start | bytes 1572872 | tf_op jit(solution)/shard_map/ppermute | solution.py:43
  7.6 2.8 %collective-permute-start.1 = (bf16[256,1024]{1,0:T(8,128)(2,1)}, bf16[256,1024]{1,0:T(8,128)(2,1)S(1)}, u32[]{:S(2)}, u32[]{:S(2)}) collective-permute-start(bf16[256,1024]{1,0:T(8,128)(2,1)} %layer_norm.1), channel_id=1, source_target_pairs={{0,384},{128,0},{256,128},{384,256},{1,385},{129,1},{257,129},{385... | collective-permute-start | bytes 1572872 | tf_op jit(solution)/shard_map/ppermute | solution.py:43
  10.4 2.5 %collective-permute-start = (bf16[256,1024]{1,0:T(8,128)(2,1)}, bf16[256,1024]{1,0:T(8,128)(2,1)}, u32[]{:S(2)}, u32[]{:S(2)}) collective-permute-start(bf16[256,1024]{1,0:T(8,128)(2,1)} %layer_norm.1), channel_id=1, source_target_pairs={{0,128},{128,256},{256,384},{384,0},{1,129},{129,257},{257,385},{3... | collective-permute-start | bytes 1572872 | tf_op jit(solution)/shard_map/ppermute | solution.py:43
  14.5 1.8 collective-permute-done.2
  16.3 14.6 %collective-permute-done.1 = bf16[256,1024]{1,0:T(8,128)(2,1)S(1)} collective-permute-done((bf16[256,1024]{1,0:T(8,128)(2,1)}, bf16[256,1024]{1,0:T(8,128)(2,1)S(1)}, u32[]{:S(2)}, u32[]{:S(2)}) %collective-permute-start.1) | collective-permute-done | bytes 524320 | tf_op jit(solution)/shard_map/ppermute | solution.py:43
  31.2 1.4 pad_maximum_fusion.mine_ref
  32.6 4.2 %collective-permute-start.3 = (bf16[1024,1024]{1,0:T(8,128)(2,1)S(1)}, bf16[1024,1024]{1,0:T(8,128)(2,1)}, u32[]{:S(2)}, u32[]{:S(2)}) collective-permute-start(bf16[1024,1024]{1,0:T(8,128)(2,1)S(1)} %pad_maximum_fusion.mine_ref), channel_id=1, source_target_pairs={{0,64},{64,0},{1,65},{65,1},{2,66},{66,2},{3,67},{67,3},{4,68},{68... | collective-permute-start | bytes 6291464 | tf_op jit(solution)/shard_map/ppermute | solution.py:43
  36.9 7.7 %all_to_all.20 = bf16[8,2,640]{2,1,0:T(2,128)(2,1)S(1)} all-to-all(bf16[8,2,640]{2,1,0:T(2,128)(2,1)S(1)} %reshape.131), channel_id=1, replica_groups=mesh['x'=4,'c'=2,'y'=8,'z'=8] {'x','c'}, dimensions={0} | all-to-all | bytes 40960 | tf_op jit(solution)/shard_map/all_to_all | solution.py:292
  45.5 16.3 %all-to-all-start.1 = ((bf16[64,16,384]{2,1,0:T(8,128)(2,1)}), bf16[64,16,384]{2,1,0:T(8,128)(2,1)S(1)}, u32[]{:S(2)}, u32[]{:S(2)}) async-start(bf16[64,16,384]{2,1,0:T(8,128)(2,1)} %broadcast_in_dim.17), calls=%async_computation.1 | async-start | bytes 1572864 | tf_op jit(solution)/shard_map/all_to_all | solution.py:48
  61.9 21.7 %all-to-all-done.1 = bf16[64,16,384]{2,1,0:T(8,128)(2,1)S(1)} async-done(((bf16[64,16,384]{2,1,0:T(8,128)(2,1)}), bf16[64,16,384]{2,1,0:T(8,128)(2,1)S(1)}, u32[]{:S(2)}, u32[]{:S(2)}) %all-to-all-start.1) | async-done | bytes 786464 | tf_op jit(solution)/shard_map/all_to_all | solution.py:48
  85.8 5.9 %project_qkv.1 = (bf16[8,512,128]{2,1,0:T(8,128)(2,1)}, bf16[8,256,128]{2,1,0:T(8,128)(2,1)}) custom-call(bf16[1024,1024]{1,0:T(8,128)(2,1)} %copy-done, bf16[1024,1024]{1,0:T(8,128)(2,1)} %collective-permute-done.3.other_ref, bf16[1024,384]{1,0:T(8,128)(2,1)} %reshape.123.weight_ref), custom_call_target="tpu_custom_call" | custom-call | tf_op jit(solution)/shard_map/project_qkv/pallas_call | solution.py:84
  91.8 20.7 %all_to_all.21 = bf16[64,16,128]{2,1,0:T(8,128)(2,1)S(1)} all-to-all(bf16[64,16,128]{2,1,0:T(8,128)(2,1)S(1)} %broadcast_in_dim.19), channel_id=1, replica_groups=mesh['x'=4,'c'=2,'y'=8,'z'=8] {'y','z'}, dimensions={0} | all-to-all | bytes 524288 | tf_op jit(solution)/shard_map/all_to_all | solution.py:48
  112.9 2.7 %collective-permute-start.8 = (bf16[1024,128]{1,0:T(8,128)(2,1)S(1)}, bf16[1024,128]{1,0:T(8,128)(2,1)S(1)}, u32[]{:S(2)}, u32[]{:S(2)}) collective-permute-start(bf16[1024,128]{1,0:T(8,128)(2,1)S(1)} %bitcast.46), channel_id=1, source_target_pairs={{0,256},{128,384},{256,0},{384,128},{1,257},{129,385},{257,1},{385... | collective-permute-start | bytes 786440 | tf_op jit(solution)/shard_map/ppermute | solution.py:43
  115.6 3.7 %collective-permute-start.7 = (bf16[1024,128]{1,0:T(8,128)(2,1)S(1)}, bf16[1024,128]{1,0:T(8,128)(2,1)S(1)}, u32[]{:S(2)}, u32[]{:S(2)}) collective-permute-start(bf16[1024,128]{1,0:T(8,128)(2,1)S(1)} %bitcast.47), channel_id=1, source_target_pairs={{0,384},{128,0},{256,128},{384,256},{1,385},{129,1},{257,129},{385... | collective-permute-start | bytes 786440 | tf_op jit(solution)/shard_map/ppermute | solution.py:43
  119.4 1.9 %collective-permute-start.6 = (bf16[1024,128]{1,0:T(8,128)(2,1)S(1)}, bf16[1024,128]{1,0:T(8,128)(2,1)S(1)}, u32[]{:S(2)}, u32[]{:S(2)}) collective-permute-start(bf16[1024,128]{1,0:T(8,128)(2,1)S(1)} %bitcast.48), channel_id=1, source_target_pairs={{0,128},{128,256},{256,384},{384,0},{1,129},{129,257},{257,385},{3... | collective-permute-start | bytes 786440 | tf_op jit(solution)/shard_map/ppermute | solution.py:43
  121.3 2.7 %collective-permute-start.4 = (bf16[8,512,128]{2,1,0:T(8,128)(2,1)}, bf16[8,512,128]{2,1,0:T(8,128)(2,1)S(1)}, u32[]{:S(2)}, u32[]{:S(2)}) collective-permute-start(bf16[8,512,128]{2,1,0:T(8,128)(2,1)} %get-tuple-element.11.own_ref), channel_id=1, source_target_pairs={{0,1},{1,2},{2,3},{3,4},{4,5},{5,6},{6,7},{7,8},{8,9},{9,10},{10,1... | collective-permute-start | bytes 3145736 | tf_op jit(solution)/shard_map/ppermute | solution.py:305
  125.8 2.8 %collective-permute-done.6 = bf16[1024,128]{1,0:T(8,128)(2,1)S(1)} collective-permute-done((bf16[1024,128]{1,0:T(8,128)(2,1)S(1)}, bf16[1024,128]{1,0:T(8,128)(2,1)S(1)}, u32[]{:S(2)}, u32[]{:S(2)}) %collective-permute-start.6) | collective-permute-done | bytes 262176 | tf_op jit(solution)/shard_map/ppermute | solution.py:43
  128.7 6.1 %collective-permute-start.9 = (bf16[4096,128]{1,0:T(8,128)(2,1)S(1)}, bf16[4096,128]{1,0:T(8,128)(2,1)}, u32[]{:S(2)}, u32[]{:S(2)}) collective-permute-start(bf16[4096,128]{1,0:T(8,128)(2,1)S(1)} %pad_maximum_fusion.1), channel_id=1, source_target_pairs={{0,64},{64,0},{1,65},{65,1},{2,66},{66,2},{3,67},{67,3},{4,68},{68... | collective-permute-start | bytes 3145736 | tf_op jit(solution)/shard_map/ppermute | solution.py:43
  135.6 8.0 %attend_own.1 = (f32[8,2,80,256]{3,2,1,0:T(8,128)}, f32[8,2,8,256]{3,2,1,0:T(8,128)}) custom-call(s32[74]{0:T(128)} %pad_add_fusion.table, bf16[8,256,128]{2,1,0:T(8,128)(2,1)} %get-tuple-element.10.query_ref, bf16[8,512,128]{2,1,0:T(8,128)(2,1)} %get-tuple-element.11.own_ref), custom_call_target="tpu_custom_call" | custom-call | tf_op jit(solution)/shard_map/attend_own/pallas_call | solution.py:176
  143.6 3.2 %collective-permute-done.5.high_ref = bf16[8,512,128]{2,1,0:T(8,128)(2,1)S(1)} collective-permute-done((bf16[8,512,128]{2,1,0:T(8,128)(2,1)}, bf16[8,512,128]{2,1,0:T(8,128)(2,1)S(1)}, u32[]{:S(2)}, u32[]{:S(2)}) %collective-permute-start.5) | collective-permute-done | bytes 1048608 | tf_op jit(solution)/shard_map/ppermute | solution.py:306
  147.8 12.5 %attend.1 = bf16[8,128,256]{2,1,0:T(8,128)(2,1)} custom-call(s32[74]{0:T(128)} %pad_add_fusion.table, bf16[8,256,128]{2,1,0:T(8,128)(2,1)} %get-tuple-element.10.query_ref, bf16[8,512,128]{2,1,0:T(8,128)(2,1)} %copy-done.2, bf16[8,512,128]{2,1,0:T(8,128)(2,1)} %copy-done.3, f32[8,2,80,256]{3,2,1,0:T(8,128)} %get-tuple-element.12.own_total_ref, ...), custom_call_target="tpu_custom_call" | custom-call | tf_op jit(solution)/shard_map/attend/pallas_call | solution.py:211
  160.3 18.5 %all_to_all.22 = bf16[8,128,256]{2,1,0:T(8,128)(2,1)} all-to-all(bf16[8,128,256]{2,1,0:T(8,128)(2,1)} %attend.1), channel_id=1, replica_groups=mesh['x'=4,'c'=2,'y'=8,'z'=8] {'x','c'}, dimensions={0} | all-to-all | bytes 1048576 | tf_op jit(solution)/shard_map/all_to_all | solution.py:314
  178.8 4.2 %project_out.1 = bf16[256,1024]{1,0:T(8,128)(2,1)} custom-call(s32[74]{0:T(128)} %pad_add_fusion.table, bf16[1024,256]{1,0:T(8,128)(2,1)} %bitcast.44, bf16[4,1024,128]{2,1,0:T(8,128)(2,1)} %bitcast.40, bf16[4,1024,128]{2,1,0:T(8,128)(2,1)} %bitcast.17.other_ref, bf16[256,1024]{1,0:T(8,128)(2,1)} %bitcast.43), custom_call_target="tpu_custom_call" | custom-call | tf_op jit(solution)/shard_map/project_out/pallas_call | solution.py:246
  (48 shorter events, 9.1 us)
Async XLA Ops:
  2.2 14.1 %collective-permute-start.2 = (bf16[256,1024]{1,0:T(8,128)(2,1)}, bf16[256,1024]{1,0:T(8,128)(2,1)S(1)}, u32[]{:S(2)}, u32[]{:S(2)}) collective-permute-start(bf16[256,1024]{1,0:T(8,128)(2,1)} %layer_norm.1), channel_id=1, source_target_pairs={{0,256},{128,384},{256,0},{384,128},{1,257},{129,385},{257,1},{385... | collective-permute-start | bytes 1572872 | tf_op jit(solution)/shard_map/ppermute | solution.py:43
  7.6 23.2 %collective-permute-start.1 = (bf16[256,1024]{1,0:T(8,128)(2,1)}, bf16[256,1024]{1,0:T(8,128)(2,1)S(1)}, u32[]{:S(2)}, u32[]{:S(2)}) collective-permute-start(bf16[256,1024]{1,0:T(8,128)(2,1)} %layer_norm.1), channel_id=1, source_target_pairs={{0,384},{128,0},{256,128},{384,256},{1,385},{129,1},{257,129},{385... | collective-permute-start | bytes 1572872 | tf_op jit(solution)/shard_map/ppermute | solution.py:43
  10.4 20.8 %collective-permute-start = (bf16[256,1024]{1,0:T(8,128)(2,1)}, bf16[256,1024]{1,0:T(8,128)(2,1)}, u32[]{:S(2)}, u32[]{:S(2)}) collective-permute-start(bf16[256,1024]{1,0:T(8,128)(2,1)} %layer_norm.1), channel_id=1, source_target_pairs={{0,128},{128,256},{256,384},{384,0},{1,129},{129,257},{257,385},{3... | collective-permute-start | bytes 1572872 | tf_op jit(solution)/shard_map/ppermute | solution.py:43
  14.5 22.3 %copy-start.6 = (bf16[2,1024]{1,0:T(2,128)(2,1)S(1)}, bf16[2,1024]{1,0:T(2,128)(2,1)}, u32[]{:S(2)}) copy-start(bf16[2,1024]{1,0:T(2,128)(2,1)} %param.8) | copy-start | bytes 12292
  32.6 52.0 %copy-start = (bf16[1024,1024]{1,0:T(8,128)(2,1)}, bf16[1024,1024]{1,0:T(8,128)(2,1)S(1)}, u32[]{:S(2)}) copy-start(bf16[1024,1024]{1,0:T(8,128)(2,1)S(1)} %pad_maximum_fusion.mine_ref) | copy-start | bytes 6291460
  32.6 53.2 %collective-permute-start.3 = (bf16[1024,1024]{1,0:T(8,128)(2,1)S(1)}, bf16[1024,1024]{1,0:T(8,128)(2,1)}, u32[]{:S(2)}, u32[]{:S(2)}) collective-permute-start(bf16[1024,1024]{1,0:T(8,128)(2,1)S(1)} %pad_maximum_fusion.mine_ref), channel_id=1, source_target_pairs={{0,64},{64,0},{1,65},{65,1},{2,66},{66,2},{3,67},{67,3},{4,68},{68... | collective-permute-start | bytes 6291464 | tf_op jit(solution)/shard_map/ppermute | solution.py:43
  44.5 40.0 %copy-start.4 = (bf16[8,2,640]{2,1,0:T(2,128)(2,1)}, bf16[8,2,640]{2,1,0:T(2,128)(2,1)S(1)}, u32[]{:S(2)}) copy-start(bf16[8,2,640]{2,1,0:T(2,128)(2,1)S(1)} %all_to_all.20) | copy-start | bytes 61444
  45.5 38.0 %all-to-all-start.1 = ((bf16[64,16,384]{2,1,0:T(8,128)(2,1)}), bf16[64,16,384]{2,1,0:T(8,128)(2,1)S(1)}, u32[]{:S(2)}, u32[]{:S(2)}) async-start(bf16[64,16,384]{2,1,0:T(8,128)(2,1)} %broadcast_in_dim.17), calls=%async_computation.1 | async-start | bytes 1572864 | tf_op jit(solution)/shard_map/all_to_all | solution.py:48
  85.8 5.9 %slice-start = ((bf16[8,2,640]{2,1,0:T(2,128)(2,1)}), bf16[8,2,128]{2,1,0:T(2,128)(2,1)S(1)}, s32[]{:S(2)}) async-start(bf16[8,2,640]{2,1,0:T(2,128)(2,1)} %copy-done.4), calls=%async_computation.4 | async-start | bytes 8192 | tf_op jit(solution)/shard_map/slice | solution.py:308
  91.7 43.1 %copy-start.5 = (bf16[8,2,640]{2,1,0:T(2,128)(2,1)S(1)}, bf16[8,2,640]{2,1,0:T(2,128)(2,1)}, u32[]{:S(2)}) copy-start(bf16[8,2,640]{2,1,0:T(2,128)(2,1)} %copy-done.4) | copy-start | bytes 61444
  112.9 12.4 %collective-permute-start.8 = (bf16[1024,128]{1,0:T(8,128)(2,1)S(1)}, bf16[1024,128]{1,0:T(8,128)(2,1)S(1)}, u32[]{:S(2)}, u32[]{:S(2)}) collective-permute-start(bf16[1024,128]{1,0:T(8,128)(2,1)S(1)} %bitcast.46), channel_id=1, source_target_pairs={{0,256},{128,384},{256,0},{384,128},{1,257},{129,385},{257,1},{385... | collective-permute-start | bytes 786440 | tf_op jit(solution)/shard_map/ppermute | solution.py:43
  115.6 10.2 %collective-permute-start.7 = (bf16[1024,128]{1,0:T(8,128)(2,1)S(1)}, bf16[1024,128]{1,0:T(8,128)(2,1)S(1)}, u32[]{:S(2)}, u32[]{:S(2)}) collective-permute-start(bf16[1024,128]{1,0:T(8,128)(2,1)S(1)} %bitcast.47), channel_id=1, source_target_pairs={{0,384},{128,0},{256,128},{384,256},{1,385},{129,1},{257,129},{385... | collective-permute-start | bytes 786440 | tf_op jit(solution)/shard_map/ppermute | solution.py:43
  119.4 9.3 %collective-permute-start.6 = (bf16[1024,128]{1,0:T(8,128)(2,1)S(1)}, bf16[1024,128]{1,0:T(8,128)(2,1)S(1)}, u32[]{:S(2)}, u32[]{:S(2)}) collective-permute-start(bf16[1024,128]{1,0:T(8,128)(2,1)S(1)} %bitcast.48), channel_id=1, source_target_pairs={{0,128},{128,256},{256,384},{384,0},{1,129},{129,257},{257,385},{3... | collective-permute-start | bytes 786440 | tf_op jit(solution)/shard_map/ppermute | solution.py:43
  121.3 22.3 %collective-permute-start.4 = (bf16[8,512,128]{2,1,0:T(8,128)(2,1)}, bf16[8,512,128]{2,1,0:T(8,128)(2,1)S(1)}, u32[]{:S(2)}, u32[]{:S(2)}) collective-permute-start(bf16[8,512,128]{2,1,0:T(8,128)(2,1)} %get-tuple-element.11.own_ref), channel_id=1, source_target_pairs={{0,1},{1,2},{2,3},{3,4},{4,5},{5,6},{6,7},{7,8},{8,9},{9,10},{10,1... | collective-permute-start | bytes 3145736 | tf_op jit(solution)/shard_map/ppermute | solution.py:305
  124.0 22.8 %collective-permute-start.5 = (bf16[8,512,128]{2,1,0:T(8,128)(2,1)}, bf16[8,512,128]{2,1,0:T(8,128)(2,1)S(1)}, u32[]{:S(2)}, u32[]{:S(2)}) collective-permute-start(bf16[8,512,128]{2,1,0:T(8,128)(2,1)} %get-tuple-element.11.own_ref), channel_id=1, source_target_pairs={{1,0},{2,1},{3,2},{4,3},{5,4},{6,5},{7,6},{8,7},{9,8},{10,9},{11,1... | collective-permute-start | bytes 3145736 | tf_op jit(solution)/shard_map/ppermute | solution.py:306
  128.7 31.6 %copy-start.1 = (bf16[4096,128]{1,0:T(8,128)(2,1)}, bf16[4096,128]{1,0:T(8,128)(2,1)S(1)}, u32[]{:S(2)}) copy-start(bf16[4096,128]{1,0:T(8,128)(2,1)S(1)} %pad_maximum_fusion.1) | copy-start | bytes 3145732
  128.7 50.1 %collective-permute-start.9 = (bf16[4096,128]{1,0:T(8,128)(2,1)S(1)}, bf16[4096,128]{1,0:T(8,128)(2,1)}, u32[]{:S(2)}, u32[]{:S(2)}) collective-permute-start(bf16[4096,128]{1,0:T(8,128)(2,1)S(1)} %pad_maximum_fusion.1), channel_id=1, source_target_pairs={{0,64},{64,0},{1,65},{65,1},{2,66},{66,2},{3,67},{67,3},{4,68},{68... | collective-permute-start | bytes 3145736 | tf_op jit(solution)/shard_map/ppermute | solution.py:43
  143.6 3.2 %copy-start.2 = (bf16[8,512,128]{2,1,0:T(8,128)(2,1)}, bf16[8,512,128]{2,1,0:T(8,128)(2,1)S(1)}, u32[]{:S(2)}) copy-start(bf16[8,512,128]{2,1,0:T(8,128)(2,1)S(1)} %collective-permute-done.4.low_ref) | copy-start | bytes 3145732
  146.8 1.0 copy-start.3

commit v3 on v2

--- a/solution.py
+++ b/solution.py
@@ -60,7 +60,14 @@
     return 4 * ((region % 2 + c) % 2) + place
 
 
-def qkv_kernel(mine_ref, other_ref, weight_ref, kv_ref, query_ref):
+WHOLE = pl.BlockSpec(memory_space=pltpu.VMEM)
+
+
+def on_chip(value):
+    return pltpu.with_memory_space_constraint(value, pltpu.VMEM)
+
+
+def qkv_kernel(mine_ref, other_ref, gathered_ref, kv_ref, query_ref, weight_ref):
     def project(tokens_ref):
         projected = jnp.dot(tokens_ref[...], weight_ref[...], preferred_element_type=F32)
         for block in range(4):
@@ -73,6 +80,10 @@
 
     @pl.when(pl.program_id(0) == 0)
     def _():
+        for region in range(8):
+            for y in range(8):
+                row = region * 128 + y * 16
+                weight_ref[row : row + 16] = gathered_ref[y, region * 16 : region * 16 + 16]
         project(mine_ref)
 
     @pl.when(pl.program_id(0) == 1)
@@ -85,9 +96,9 @@
         qkv_kernel,
         grid=(2,),
         in_specs=[
+            pl.BlockSpec(memory_space=pltpu.VMEM),
             pl.BlockSpec((1024, 1024), lambda s: (0, 0)),
-            pl.BlockSpec((1024, 1024), lambda s: (0, 0)),
-            pl.BlockSpec((1024, 384), lambda s: (0, 0)),
+            pl.BlockSpec(memory_space=pltpu.VMEM),
         ],
         out_specs=[
             pl.BlockSpec((4, 512, 128), lambda s: (s, 0, 0)),
@@ -97,8 +108,9 @@
             jax.ShapeDtypeStruct((8, 512, 128), BF16),
             jax.ShapeDtypeStruct((8, 256, 128), BF16),
         ],
+        scratch_shapes=[pltpu.VMEM((1024, 384), BF16)],
         name="project_qkv",
-    )(mine, other, weight)
+    )(on_chip(mine), other, on_chip(weight))
 
 
 def near_places(table, slot, refs):
@@ -169,9 +181,6 @@
     run_units(table, query_ref, [(1, own_ref)], score_ref, weight_ref, None, finish)
 
 
-WHOLE = pl.BlockSpec((8, 512, 128), lambda s, t: (0, 0, 0), pipeline_mode=pl.Buffered(1))
-
-
 def attend_own(table, queries, own):
     return pl.pallas_call(
         attend_own_kernel,
@@ -225,11 +234,12 @@
         ),
         out_shape=jax.ShapeDtypeStruct((8, 128, 256), BF16),
         name="attend",
-    )(table, queries, low, high, own_total, own_top)
+    )(table, queries, on_chip(low), on_chip(high), own_total, own_top)
 
 
 def output_kernel(table, mixed_ref, mine_ref, other_ref, voxels_ref, out_ref):
-    mixed = mixed_ref[...].T
+    rows = [r * 128 + y * 16 for y in range(8) for r in range(8)]
+    mixed = jnp.concatenate([mixed_ref[row : row + 16, :] for row in rows], axis=0).T
     for pair in range(4):
         ref = (mine_ref, other_ref)[pair // 2]
         slots = (2 * pair, 2 * pair + 1)
@@ -249,7 +259,7 @@
             num_scalar_prefetch=1,
             grid=(1,),
             in_specs=[
-                pl.BlockSpec((1024, 256), lambda n, t: (0, 0)),
+                pl.BlockSpec(memory_space=pltpu.VMEM),
                 pl.BlockSpec((4, 1024, 128), lambda n, t: (0, 0, 0)),
                 pl.BlockSpec((4, 1024, 128), lambda n, t: (0, 0, 0)),
                 pl.BlockSpec((256, 1024), lambda n, t: (0, 0)),
@@ -258,7 +268,7 @@
         ),
         out_shape=jax.ShapeDtypeStruct((256, 1024), BF16),
         name="project_out",
-    )(table, mixed, mine, other, voxels)
+    )(table, on_chip(mixed), mine, other, voxels)
 
 
 def gathered_line(value):
@@ -288,27 +298,25 @@
     parts = qkv_weight.reshape(2, 3, 8, 128)
     flags = jnp.broadcast_to(listed.astype(BF16)[None, None], (2, 8, 128))
     parts = [parts[:, 1], parts[:, 2], parts[:, 0], out_weight.reshape(2, 8, 128), flags]
-    parts = jnp.stack(parts, axis=2).transpose(1, 0, 2, 3).reshape(8, 2, 640)
-    swapped = lax.all_to_all(parts, LINE, 0, 0, tiled=True)
+    parts = jnp.stack(parts, axis=2).transpose(1, 0, 2, 3).reshape(8, 1, 2, 640)
+    parts = jnp.broadcast_to(parts, (8, 8, 2, 640)).reshape(64, 2, 640)
+    swapped = lax.all_to_all(parts, ("x", "c", "z"), 0, 0, tiled=True)
+    masks = lax.dynamic_index_in_dim(swapped.reshape(8, 8, 2, 640), z, 1, keepdims=False)
     table = jnp.concatenate([
-        swapped[:, 0, 512:521].astype(jnp.int32).reshape(72),
+        masks[:, 0, 512:521].astype(jnp.int32).reshape(72),
         jnp.stack([x, c]).astype(jnp.int32),
     ])
-
-    def in_row_order(weight):
-        width = weight.shape[-1]
-        return weight.reshape(64, 8, 2, width).transpose(1, 0, 2, 3).reshape(1024, width)
-
-    weight = from_everyone(swapped[:, :, :384].reshape(16, 384), PLANE)
-    own, queries = project_qkv(mine, other, in_row_order(weight))
+    swapped = swapped.reshape(128, 640)
+
+    weight = from_everyone(swapped[:, :384], "y")
+    own, queries = project_qkv(mine, other, weight)
     line = [(i, i + 1) for i in range(63)]
     low = lax.ppermute(own, PLANE, line)
     high = lax.ppermute(own, PLANE, [(j, i) for i, j in line])
 
-    out_part, _ = lax.optimization_barrier((swapped[:, :, 384:512], queries))
-    out_part = from_everyone(out_part.reshape(16, 128), PLANE)
+    out_part, _ = lax.optimization_barrier((swapped[:, 384:512], queries))
+    out_part = from_everyone(out_part, "y").reshape(1024, 128)
     own_total, own_top = attend_own(table, queries, own)
-    out_part = in_row_order(out_part)
     out_mine, out_other = gathered_line(out_part)
     mixed = attend(table, queries, low, high, own_total, own_top)
     mixed = lax.all_to_all(mixed, LINE, 0, 0, tiled=True).reshape(1024, 256)

time: 184 us -> 179 us (0.973)
  starting transfers between devices: 49.7 us -> 42.4 us
  waiting for transfers between devices: 45 us -> 49 us
  blocking collectives: 47 us -> 50.5 us
  local copies, waits for them, and re-layouts: 5.43 us -> 2.79 us
    all_to_all x1, blocking collectives: 7.68 us -> 22.4 us  [layer(): swapped = lax.all_to_all(parts, ('x', 'c', 'z'), 0, 0, tiled=True)]
    all_to_all x1, starting transfers between devices: 16.3 us -> 6.82 us  [from_everyone(): lax.all_to_all(jnp.broadcast_to(value[None], (n, *value.shape)), axes, 0,...]
    all_to_all x1, blocking collectives: 20.7 us -> 11.6 us  [from_everyone(): lax.all_to_all(jnp.broadcast_to(value[None], (n, *value.shape)), axes, 0,...]
    ppermute x1, waiting for transfers between devices: 0.01 us -> 4.16 us  [layer(): low = lax.ppermute(own, PLANE, line)]
    all_to_all x1, blocking collectives: 18.5 us -> 16.4 us  [layer(): mixed = lax.all_to_all(mixed, LINE, 0, 0, tiled=True).reshape(1024, 256)]
  transfers between devices with their start and end apart: 11 -> 11, of which waited for: 7 -> 7; matrix products, arithmetic and copies ran while one was open for 3% -> 2% of each run, Pallas kernels for 11% -> 11%
where the time goes in v3:
time: 179 us
  blocking collectives  50.5 us (28%)
  waiting for transfers between devices  49 us (27%)
  starting transfers between devices  42.4 us (24%)
  Pallas kernels  31 us (17%)
  other arithmetic  2.83 us (2%)
  local copies, waits for them, and re-layouts  2.79 us (2%)
    ppermute x8, starting transfers between devices, shift(): return lax.ppermute(value, axis, [(i, (i + step) % n) for i in range(n)])  30.9 us
    all_to_all x1, blocking collectives, layer(): swapped = lax.all_to_all(parts, ('x', 'c', 'z'), 0, 0, tiled=True)  22.4 us
    all_to_all x1, waiting for transfers between devices, from_everyone(): lax.all_to_all(jnp.broadcast_to(value[None], (n, *value.shape)), axes, 0,...  22.1 us
    ppermute x8, waiting for transfers between devices, shift(): return lax.ppermute(value, axis, [(i, (i + step) % n) for i in range(n)])  18.9 us
    all_to_all x1, blocking collectives, layer(): mixed = lax.all_to_all(mixed, LINE, 0, 0, tiled=True).reshape(1024, 256)  16.4 us
    pallas_call x1, Pallas kernels, attend(): pl.pallas_call(attend_kernel, grid_spec=pltpu.PrefetchScalarGridSpec(num_...  11.7 us
    all_to_all x1, blocking collectives, from_everyone(): lax.all_to_all(jnp.broadcast_to(value[None], (n, *value.shape)), axes, 0,...  11.6 us
    pallas_call x1, Pallas kernels, attend_own(): pl.pallas_call(attend_own_kernel, grid_spec=pltpu.PrefetchScalarGridSpec(...  7.98 us
  transfers between devices with their start and end apart: 11, of which 7 were waited for; matrix products, arithmetic and copies ran while one was open for 2% of the time, Pallas kernels for 11%

profile of v3, /device:TPU:1, one launch (start us, length us, event | category | flops | bytes accessed | tf_op | source)
XLA Modules:
  0.0 178.7 jit_solution(13801819877144071856)
XLA Ops:
  0.0 2.2 %layer_norm.1 = bf16[256,1024]{1,0:T(8,128)(2,1)} custom-call(bf16[256,1024]{1,0:T(8,128)(2,1)} %bitcast.44, f32[1,1024]{1,0:T(1,128)} %bitcast.58), custom_call_target="tpu_custom_call" | custom-call | tf_op jit(solution)/shard_map/layer_norm/pallas_call | solution.py:28
  2.2 5.5 %collective-permute-start.2 = (bf16[256,1024]{1,0:T(8,128)(2,1)}, bf16[256,1024]{1,0:T(8,128)(2,1)S(1)}, u32[]{:S(2)}, u32[]{:S(2)}) collective-permute-start(bf16[256,1024]{1,0:T(8,128)(2,1)} %layer_norm.1), channel_id=1, source_target_pairs={{0,256},{128,384},{256,0},{384,128},{1,257},{129,385},{257,1},{385... | collective-permute-start | bytes 1572872 | tf_op jit(solution)/shard_map/ppermute | solution.py:43
  7.6 2.8 %collective-permute-start.1 = (bf16[256,1024]{1,0:T(8,128)(2,1)}, bf16[256,1024]{1,0:T(8,128)(2,1)S(1)}, u32[]{:S(2)}, u32[]{:S(2)}) collective-permute-start(bf16[256,1024]{1,0:T(8,128)(2,1)} %layer_norm.1), channel_id=1, source_target_pairs={{0,384},{128,0},{256,128},{384,256},{1,385},{129,1},{257,129},{385... | collective-permute-start | bytes 1572872 | tf_op jit(solution)/shard_map/ppermute | solution.py:43
  10.4 2.5 %collective-permute-start = (bf16[256,1024]{1,0:T(8,128)(2,1)}, bf16[256,1024]{1,0:T(8,128)(2,1)}, u32[]{:S(2)}, u32[]{:S(2)}) collective-permute-start(bf16[256,1024]{1,0:T(8,128)(2,1)} %layer_norm.1), channel_id=1, source_target_pairs={{0,128},{128,256},{256,384},{384,0},{1,129},{129,257},{257,385},{3... | collective-permute-start | bytes 1572872 | tf_op jit(solution)/shard_map/ppermute | solution.py:43
  16.3 14.6 %collective-permute-done.1 = bf16[256,1024]{1,0:T(8,128)(2,1)S(1)} collective-permute-done((bf16[256,1024]{1,0:T(8,128)(2,1)}, bf16[256,1024]{1,0:T(8,128)(2,1)S(1)}, u32[]{:S(2)}, u32[]{:S(2)}) %collective-permute-start.1) | collective-permute-done | bytes 524320 | tf_op jit(solution)/shard_map/ppermute | solution.py:43
  31.2 1.4 pad_maximum_fusion.mine_ref
  32.6 4.2 %collective-permute-start.3 = (bf16[1024,1024]{1,0:T(8,128)(2,1)S(1)}, bf16[1024,1024]{1,0:T(8,128)(2,1)}, u32[]{:S(2)}, u32[]{:S(2)}) collective-permute-start(bf16[1024,1024]{1,0:T(8,128)(2,1)S(1)} %pad_maximum_fusion.mine_ref), channel_id=1, source_target_pairs={{0,64},{64,0},{1,65},{65,1},{2,66},{66,2},{3,67},{67,3},{4,68},{68... | collective-permute-start | bytes 6291464 | tf_op jit(solution)/shard_map/ppermute | solution.py:43
  36.9 22.4 %all_to_all.20 = bf16[64,2,640]{2,1,0:T(2,128)(2,1)S(1)} all-to-all(bf16[64,2,640]{2,1,0:T(2,128)(2,1)S(1)} %bitcast.50), channel_id=1, replica_groups=mesh['x'=4,'c'=2,'y'=8,'z'=8] {'x','c','z'}, dimensions={0} | all-to-all | bytes 327680 | tf_op jit(solution)/shard_map/all_to_all | solution.py:303
  60.4 6.8 %all-to-all-start.1 = ((bf16[8,128,384]{2,1,0:T(8,128)(2,1)}), bf16[8,128,384]{2,1,0:T(8,128)(2,1)S(1)}, u32[]{:S(2)}, u32[]{:S(2)}) async-start(bf16[8,128,384]{2,1,0:T(8,128)(2,1)} %broadcast_in_dim.10), calls=%async_computation.1 | async-start | bytes 1572864 | tf_op jit(solution)/shard_map/all_to_all | solution.py:48
  67.2 22.1 %all-to-all-done.1.gathered_ref = bf16[8,128,384]{2,1,0:T(8,128)(2,1)S(1)} async-done(((bf16[8,128,384]{2,1,0:T(8,128)(2,1)}), bf16[8,128,384]{2,1,0:T(8,128)(2,1)S(1)}, u32[]{:S(2)}, u32[]{:S(2)}) %all-to-all-start.1) | async-done | bytes 786464 | tf_op jit(solution)/shard_map/all_to_all | solution.py:48
  89.3 5.1 %project_qkv.1 = (bf16[8,512,128]{2,1,0:T(8,128)(2,1)}, bf16[8,256,128]{2,1,0:T(8,128)(2,1)}) custom-call(bf16[1024,1024]{1,0:T(8,128)(2,1)S(1)} %pad_maximum_fusion.mine_ref, bf16[1024,1024]{1,0:T(8,128)(2,1)} %collective-permute-done.3.other_ref, bf16[8,128,384]{2,1,0:T(8,128)(2,1)S(1)} %all-to-all-done.1.gathered_ref), custom_call_target="tpu_custom_call" | custom-call | tf_op jit(solution)/shard_map/project_qkv/pallas_call | solution.py:95
  94.5 11.6 %all_to_all.21 = bf16[8,128,128]{2,1,0:T(8,128)(2,1)S(1)} all-to-all(bf16[8,128,128]{2,1,0:T(8,128)(2,1)S(1)} %broadcast_in_dim.11), channel_id=1, replica_groups=mesh['x'=4,'c'=2,'y'=8,'z'=8] {'y'}, dimensions={0} | all-to-all | bytes 524288 | tf_op jit(solution)/shard_map/all_to_all | solution.py:48
  106.1 4.6 %collective-permute-start.8 = (bf16[1024,128]{1,0:T(8,128)(2,1)S(1)}, bf16[1024,128]{1,0:T(8,128)(2,1)S(1)}, u32[]{:S(2)}, u32[]{:S(2)}) collective-permute-start(bf16[1024,128]{1,0:T(8,128)(2,1)S(1)} %bitcast.46), channel_id=1, source_target_pairs={{0,256},{128,384},{256,0},{384,128},{1,257},{129,385},{257,1},{385... | collective-permute-start | bytes 786440 | tf_op jit(solution)/shard_map/ppermute | solution.py:43
  110.7 5.3 %collective-permute-start.7 = (bf16[1024,128]{1,0:T(8,128)(2,1)S(1)}, bf16[1024,128]{1,0:T(8,128)(2,1)S(1)}, u32[]{:S(2)}, u32[]{:S(2)}) collective-permute-start(bf16[1024,128]{1,0:T(8,128)(2,1)S(1)} %bitcast.47), channel_id=1, source_target_pairs={{0,384},{128,0},{256,128},{384,256},{1,385},{129,1},{257,129},{385... | collective-permute-start | bytes 786440 | tf_op jit(solution)/shard_map/ppermute | solution.py:43
  116.0 2.5 %collective-permute-start.6 = (bf16[1024,128]{1,0:T(8,128)(2,1)S(1)}, bf16[1024,128]{1,0:T(8,128)(2,1)S(1)}, u32[]{:S(2)}, u32[]{:S(2)}) collective-permute-start(bf16[1024,128]{1,0:T(8,128)(2,1)S(1)} %bitcast.48), channel_id=1, source_target_pairs={{0,128},{128,256},{256,384},{384,0},{1,129},{129,257},{257,385},{3... | collective-permute-start | bytes 786440 | tf_op jit(solution)/shard_map/ppermute | solution.py:43
  118.5 3.3 %collective-permute-start.4 = (bf16[8,512,128]{2,1,0:T(8,128)(2,1)}, bf16[8,512,128]{2,1,0:T(8,128)(2,1)S(1)}, u32[]{:S(2)}, u32[]{:S(2)}) collective-permute-start(bf16[8,512,128]{2,1,0:T(8,128)(2,1)} %get-tuple-element.11.own_ref), channel_id=1, source_target_pairs={{0,1},{1,2},{2,3},{3,4},{4,5},{5,6},{6,7},{7,8},{8,9},{9,10},{10,1... | collective-permute-start | bytes 3145736 | tf_op jit(solution)/shard_map/ppermute | solution.py:314
  123.2 2.9 %collective-permute-done.7 = bf16[1024,128]{1,0:T(8,128)(2,1)S(1)} collective-permute-done((bf16[1024,128]{1,0:T(8,128)(2,1)S(1)}, bf16[1024,128]{1,0:T(8,128)(2,1)S(1)}, u32[]{:S(2)}, u32[]{:S(2)}) %collective-permute-start.7) | collective-permute-done | bytes 262176 | tf_op jit(solution)/shard_map/ppermute | solution.py:43
  126.2 3.7 %collective-permute-start.9 = (bf16[4096,128]{1,0:T(8,128)(2,1)S(1)}, bf16[4096,128]{1,0:T(8,128)(2,1)}, u32[]{:S(2)}, u32[]{:S(2)}) collective-permute-start(bf16[4096,128]{1,0:T(8,128)(2,1)S(1)} %pad_maximum_fusion.1), channel_id=1, source_target_pairs={{0,64},{64,0},{1,65},{65,1},{2,66},{66,2},{3,67},{67,3},{4,68},{68... | collective-permute-start | bytes 3145736 | tf_op jit(solution)/shard_map/ppermute | solution.py:43
  130.6 8.0 %attend_own.1 = (f32[8,2,80,256]{3,2,1,0:T(8,128)}, f32[8,2,8,256]{3,2,1,0:T(8,128)}) custom-call(s32[74]{0:T(128)} %pad_add_fusion.table, bf16[8,256,128]{2,1,0:T(8,128)(2,1)} %get-tuple-element.10.query_ref, bf16[8,512,128]{2,1,0:T(8,128)(2,1)} %get-tuple-element.11.own_ref), custom_call_target="tpu_custom_call" | custom-call | tf_op jit(solution)/shard_map/attend_own/pallas_call | solution.py:185
  138.6 4.2 %collective-permute-done.4.low_ref = bf16[8,512,128]{2,1,0:T(8,128)(2,1)S(1)} collective-permute-done((bf16[8,512,128]{2,1,0:T(8,128)(2,1)}, bf16[8,512,128]{2,1,0:T(8,128)(2,1)S(1)}, u32[]{:S(2)}, u32[]{:S(2)}) %collective-permute-start.4) | collective-permute-done | bytes 1048608 | tf_op jit(solution)/shard_map/ppermute | solution.py:314
  142.8 3.8 %collective-permute-done.5.high_ref = bf16[8,512,128]{2,1,0:T(8,128)(2,1)S(1)} collective-permute-done((bf16[8,512,128]{2,1,0:T(8,128)(2,1)}, bf16[8,512,128]{2,1,0:T(8,128)(2,1)S(1)}, u32[]{:S(2)}, u32[]{:S(2)}) %collective-permute-start.5) | collective-permute-done | bytes 1048608 | tf_op jit(solution)/shard_map/ppermute | solution.py:315
  146.6 11.7 %attend.1 = bf16[8,128,256]{2,1,0:T(8,128)(2,1)} custom-call(s32[74]{0:T(128)} %pad_add_fusion.table, bf16[8,256,128]{2,1,0:T(8,128)(2,1)} %get-tuple-element.10.query_ref, bf16[8,512,128]{2,1,0:T(8,128)(2,1)S(1)} %collective-permute-done.4.low_ref, bf16[8,512,128]{2,1,0:T(8,128)(2,1)S(1)} %collective-permute-done.5.high_ref, ...), custom_call_target="tpu_custom_call" | custom-call | tf_op jit(solution)/shard_map/attend/pallas_call | solution.py:220
  158.2 16.4 %all_to_all.22 = bf16[8,128,256]{2,1,0:T(8,128)(2,1)S(1)} all-to-all(bf16[8,128,256]{2,1,0:T(8,128)(2,1)} %attend.1), channel_id=1, replica_groups=mesh['x'=4,'c'=2,'y'=8,'z'=8] {'x','c'}, dimensions={0} | all-to-all | bytes 1048576 | tf_op jit(solution)/shard_map/all_to_all | solution.py:322
  174.7 4.0 %project_out.1 = bf16[256,1024]{1,0:T(8,128)(2,1)} custom-call(s32[74]{0:T(128)} %pad_add_fusion.table, bf16[1024,256]{1,0:T(8,128)(2,1)S(1)} %bitcast.42, bf16[4,1024,128]{2,1,0:T(8,128)(2,1)} %bitcast.43, bf16[4,1024,128]{2,1,0:T(8,128)(2,1)} %bitcast.14.other_ref, bf16[256,1024]{1,0:T(8,128)(2,1)} %bitcast.45), custom_call_target="tpu_custom_call" | custom-call | tf_op jit(solution)/shard_map/project_out/pallas_call | solution.py:256
  (34 shorter events, 7.0 us)
Async XLA Ops:
  2.2 14.1 %collective-permute-start.2 = (bf16[256,1024]{1,0:T(8,128)(2,1)}, bf16[256,1024]{1,0:T(8,128)(2,1)S(1)}, u32[]{:S(2)}, u32[]{:S(2)}) collective-permute-start(bf16[256,1024]{1,0:T(8,128)(2,1)} %layer_norm.1), channel_id=1, source_target_pairs={{0,256},{128,384},{256,0},{384,128},{1,257},{129,385},{257,1},{385... | collective-permute-start | bytes 1572872 | tf_op jit(solution)/shard_map/ppermute | solution.py:43
  7.6 23.2 %collective-permute-start.1 = (bf16[256,1024]{1,0:T(8,128)(2,1)}, bf16[256,1024]{1,0:T(8,128)(2,1)S(1)}, u32[]{:S(2)}, u32[]{:S(2)}) collective-permute-start(bf16[256,1024]{1,0:T(8,128)(2,1)} %layer_norm.1), channel_id=1, source_target_pairs={{0,384},{128,0},{256,128},{384,256},{1,385},{129,1},{257,129},{385... | collective-permute-start | bytes 1572872 | tf_op jit(solution)/shard_map/ppermute | solution.py:43
  10.4 20.8 %collective-permute-start = (bf16[256,1024]{1,0:T(8,128)(2,1)}, bf16[256,1024]{1,0:T(8,128)(2,1)}, u32[]{:S(2)}, u32[]{:S(2)}) collective-permute-start(bf16[256,1024]{1,0:T(8,128)(2,1)} %layer_norm.1), channel_id=1, source_target_pairs={{0,128},{128,256},{256,384},{384,0},{1,129},{129,257},{257,385},{3... | collective-permute-start | bytes 1572872 | tf_op jit(solution)/shard_map/ppermute | solution.py:43
  32.6 56.8 %collective-permute-start.3 = (bf16[1024,1024]{1,0:T(8,128)(2,1)S(1)}, bf16[1024,1024]{1,0:T(8,128)(2,1)}, u32[]{:S(2)}, u32[]{:S(2)}) collective-permute-start(bf16[1024,1024]{1,0:T(8,128)(2,1)S(1)} %pad_maximum_fusion.mine_ref), channel_id=1, source_target_pairs={{0,64},{64,0},{1,65},{65,1},{2,66},{66,2},{3,67},{67,3},{4,68},{68... | collective-permute-start | bytes 6291464 | tf_op jit(solution)/shard_map/ppermute | solution.py:43
  60.4 28.9 %all-to-all-start.1 = ((bf16[8,128,384]{2,1,0:T(8,128)(2,1)}), bf16[8,128,384]{2,1,0:T(8,128)(2,1)S(1)}, u32[]{:S(2)}, u32[]{:S(2)}) async-start(bf16[8,128,384]{2,1,0:T(8,128)(2,1)} %broadcast_in_dim.10), calls=%async_computation.1 | async-start | bytes 1572864 | tf_op jit(solution)/shard_map/all_to_all | solution.py:48
  106.1 17.0 %collective-permute-start.8 = (bf16[1024,128]{1,0:T(8,128)(2,1)S(1)}, bf16[1024,128]{1,0:T(8,128)(2,1)S(1)}, u32[]{:S(2)}, u32[]{:S(2)}) collective-permute-start(bf16[1024,128]{1,0:T(8,128)(2,1)S(1)} %bitcast.46), channel_id=1, source_target_pairs={{0,256},{128,384},{256,0},{384,128},{1,257},{129,385},{257,1},{385... | collective-permute-start | bytes 786440 | tf_op jit(solution)/shard_map/ppermute | solution.py:43
  110.7 15.3 %collective-permute-start.7 = (bf16[1024,128]{1,0:T(8,128)(2,1)S(1)}, bf16[1024,128]{1,0:T(8,128)(2,1)S(1)}, u32[]{:S(2)}, u32[]{:S(2)}) collective-permute-start(bf16[1024,128]{1,0:T(8,128)(2,1)S(1)} %bitcast.47), channel_id=1, source_target_pairs={{0,384},{128,0},{256,128},{384,256},{1,385},{129,1},{257,129},{385... | collective-permute-start | bytes 786440 | tf_op jit(solution)/shard_map/ppermute | solution.py:43
  116.0 10.1 %collective-permute-start.6 = (bf16[1024,128]{1,0:T(8,128)(2,1)S(1)}, bf16[1024,128]{1,0:T(8,128)(2,1)S(1)}, u32[]{:S(2)}, u32[]{:S(2)}) collective-permute-start(bf16[1024,128]{1,0:T(8,128)(2,1)S(1)} %bitcast.48), channel_id=1, source_target_pairs={{0,128},{128,256},{256,384},{384,0},{1,129},{129,257},{257,385},{3... | collective-permute-start | bytes 786440 | tf_op jit(solution)/shard_map/ppermute | solution.py:43
  118.5 24.3 %collective-permute-start.4 = (bf16[8,512,128]{2,1,0:T(8,128)(2,1)}, bf16[8,512,128]{2,1,0:T(8,128)(2,1)S(1)}, u32[]{:S(2)}, u32[]{:S(2)}) collective-permute-start(bf16[8,512,128]{2,1,0:T(8,128)(2,1)} %get-tuple-element.11.own_ref), channel_id=1, source_target_pairs={{0,1},{1,2},{2,3},{3,4},{4,5},{5,6},{6,7},{7,8},{8,9},{9,10},{10,1... | collective-permute-start | bytes 3145736 | tf_op jit(solution)/shard_map/ppermute | solution.py:314
  121.9 24.7 %collective-permute-start.5 = (bf16[8,512,128]{2,1,0:T(8,128)(2,1)}, bf16[8,512,128]{2,1,0:T(8,128)(2,1)S(1)}, u32[]{:S(2)}, u32[]{:S(2)}) collective-permute-start(bf16[8,512,128]{2,1,0:T(8,128)(2,1)} %get-tuple-element.11.own_ref), channel_id=1, source_target_pairs={{1,0},{2,1},{3,2},{4,3},{5,4},{6,5},{7,6},{8,7},{9,8},{10,9},{11,1... | collective-permute-start | bytes 3145736 | tf_op jit(solution)/shard_map/ppermute | solution.py:315
  126.1 32.1 %copy-start = (bf16[4096,128]{1,0:T(8,128)(2,1)}, bf16[4096,128]{1,0:T(8,128)(2,1)S(1)}, u32[]{:S(2)}) copy-start(bf16[4096,128]{1,0:T(8,128)(2,1)S(1)} %pad_maximum_fusion.1) | copy-start | bytes 3145732
  126.2 48.5 %collective-permute-start.9 = (bf16[4096,128]{1,0:T(8,128)(2,1)S(1)}, bf16[4096,128]{1,0:T(8,128)(2,1)}, u32[]{:S(2)}, u32[]{:S(2)}) collective-permute-start(bf16[4096,128]{1,0:T(8,128)(2,1)S(1)} %pad_maximum_fusion.1), channel_id=1, source_target_pairs={{0,64},{64,0},{1,65},{65,1},{2,66},{66,2},{3,67},{67,3},{4,68},{68... | collective-permute-start | bytes 3145736 | tf_op jit(solution)/shard_map/ppermute | solution.py:43

commit v4 on v3

--- a/solution.py
+++ b/solution.py
@@ -38,6 +38,43 @@
     )(tokens, norm_gain.reshape(1, 1024))
 
 
+def message_kernel(lists_ref, weight_ref, out_weight_ref, out_ref):
+    region = 2 * lax.axis_index("x") + lax.axis_index("c")
+    owner = 8 * lax.axis_index("y") + lax.axis_index("z")
+    lanes = lax.broadcasted_iota(jnp.int32, (2, 128), 1)
+    flags = jnp.where(lanes == 4, 1.0, 0.0)
+    for entry in (0, 1, 2, 3, 5, 6, 7, 8):
+        near_region = region + entry // 3 - 1
+        near_owner = owner + entry % 3 - 1
+        inside = (
+            (near_region >= 0) & (near_region < 8) & (near_owner >= 0) & (near_owner < 64)
+        )
+        number = jnp.where(inside, near_region * 64 + near_owner, -2)
+        listed = functools.reduce(jnp.logical_or, [lists_ref[0, i] == number for i in range(8)])
+        flags = jnp.where((lanes == entry) & listed, 1.0, flags)
+    flags = flags.astype(BF16)
+    for head_pair in range(8):
+        start = head_pair * 128
+        parts = [weight_ref[:, base + start : base + start + 128] for base in (1024, 2048, 0)]
+        parts += [out_weight_ref[:, start : start + 128], flags]
+        message = jnp.concatenate(parts, axis=1)
+        for z in range(8):
+            out_ref[head_pair * 8 + z] = message
+
+
+def messages(lists, weight, out_weight):
+    return pl.pallas_call(
+        message_kernel,
+        in_specs=[
+            pl.BlockSpec(memory_space=pltpu.SMEM),
+            pl.BlockSpec(memory_space=pltpu.VMEM),
+            pl.BlockSpec(memory_space=pltpu.VMEM),
+        ],
+        out_shape=jax.ShapeDtypeStruct((64, 2, 640), BF16),
+        name="messages",
+    )(lists, weight, out_weight)
+
+
 def shift(value, axis, step):
     n = lax.axis_size(axis)
     return lax.ppermute(value, axis, [(i, (i + step) % n) for i in range(n)])
@@ -67,50 +104,56 @@
     return pltpu.with_memory_space_constraint(value, pltpu.VMEM)
 
 
-def qkv_kernel(mine_ref, other_ref, gathered_ref, kv_ref, query_ref, weight_ref):
-    def project(tokens_ref):
-        projected = jnp.dot(tokens_ref[...], weight_ref[...], preferred_element_type=F32)
-        for block in range(4):
-            rows = slice(block * 256, block * 256 + 256)
-            kv_ref[block, 0:256, :] = projected[rows, :128].astype(BF16)
-            values = projected[rows, 128:256].astype(BF16).T
-            kv_ref[block, 256:384, :] = values[:, :128]
-            kv_ref[block, 384:512, :] = values[:, 128:]
-            query_ref[block] = (projected[rows, 256:] * FACTOR).astype(BF16)
-
+def project_tokens(tokens, weight, kv_ref, query_ref):
+    projected = jnp.dot(tokens, weight, preferred_element_type=F32)
+    for block in range(2):
+        rows = slice(block * 256, block * 256 + 256)
+        kv_ref[block, 0:256, :] = projected[rows, :128].astype(BF16)
+        values = projected[rows, 128:256].astype(BF16).T
+        kv_ref[block, 256:384, :] = values[:, :128]
+        kv_ref[block, 384:512, :] = values[:, 128:]
+        query_ref[block] = (projected[rows, 256:] * FACTOR).astype(BF16)
+
+
+def mine_kernel(tokens_ref, gathered_ref, kv_ref, query_ref, weight_ref):
     @pl.when(pl.program_id(0) == 0)
     def _():
         for region in range(8):
             for y in range(8):
                 row = region * 128 + y * 16
                 weight_ref[row : row + 16] = gathered_ref[y, region * 16 : region * 16 + 16]
-        project(mine_ref)
-
-    @pl.when(pl.program_id(0) == 1)
-    def _():
-        project(other_ref)
-
-
-def project_qkv(mine, other, weight):
-    return pl.pallas_call(
-        qkv_kernel,
+
+    project_tokens(tokens_ref[...], weight_ref[...], kv_ref, query_ref)
+
+
+def other_kernel(tokens_ref, weight_ref, _, __, kv_ref, query_ref):
+    rows = pl.ds(pl.multiple_of(pl.program_id(0) * 512, 512), 512)
+    project_tokens(tokens_ref[rows, :], weight_ref[...], kv_ref, query_ref)
+
+
+def project_call(kernel, first, weight_out, aliased):
+    whole = pl.BlockSpec((1024, 384), lambda s: (0, 0))
+    on_chip_spec = pl.BlockSpec(memory_space=pltpu.VMEM)
+    return pl.pallas_call(
+        kernel,
         grid=(2,),
         in_specs=[
-            pl.BlockSpec(memory_space=pltpu.VMEM),
-            pl.BlockSpec((1024, 1024), lambda s: (0, 0)),
-            pl.BlockSpec(memory_space=pltpu.VMEM),
+            pl.BlockSpec((512, 1024), lambda s: (s, 0)) if weight_out else on_chip_spec,
+            on_chip_spec if weight_out else whole,
+            *[pl.BlockSpec(memory_space=pl.ANY)] * aliased,
         ],
         out_specs=[
-            pl.BlockSpec((4, 512, 128), lambda s: (s, 0, 0)),
-            pl.BlockSpec((4, 256, 128), lambda s: (s, 0, 0)),
+            pl.BlockSpec((2, 512, 128), lambda s: (2 * first + s, 0, 0)),
+            pl.BlockSpec((2, 256, 128), lambda s: (2 * first + s, 0, 0)),
+            *[whole] * weight_out,
         ],
         out_shape=[
             jax.ShapeDtypeStruct((8, 512, 128), BF16),
             jax.ShapeDtypeStruct((8, 256, 128), BF16),
-        ],
-        scratch_shapes=[pltpu.VMEM((1024, 384), BF16)],
-        name="project_qkv",
-    )(on_chip(mine), other, on_chip(weight))
+            *[jax.ShapeDtypeStruct((1024, 384), BF16)] * weight_out,
+        ],
+        input_output_aliases={2: 0, 3: 1} if aliased else {},
+    )
 
 
 def near_places(table, slot, refs):
@@ -237,19 +280,20 @@
     )(table, queries, on_chip(low), on_chip(high), own_total, own_top)
 
 
-def output_kernel(table, mixed_ref, mine_ref, other_ref, voxels_ref, out_ref):
-    rows = [r * 128 + y * 16 for y in range(8) for r in range(8)]
-    mixed = jnp.concatenate([mixed_ref[row : row + 16, :] for row in rows], axis=0).T
-    for pair in range(4):
-        ref = (mine_ref, other_ref)[pair // 2]
-        slots = (2 * pair, 2 * pair + 1)
-        weight = jnp.concatenate([ref[slot % 4] for slot in slots], axis=1)
-        projected = jnp.dot(mixed, weight, preferred_element_type=F32)
-        for place, slot in enumerate(slots):
-            start = pl.multiple_of(region_of(slot, table[72], table[73]) * 128, 128)
-            cols = pl.ds(start, 128)
-            part = projected[:, place * 128 : place * 128 + 128]
-            out_ref[:, cols] = (voxels_ref[:, cols].astype(F32) + part).astype(BF16)
+def output_kernel(table, mixed_ref, mine_ref, other_ref, voxels_ref, out_ref, turned_ref):
+    @pl.when(pl.program_id(0) == 0)
+    def _():
+        rows = [r * 128 + y * 16 for y in range(8) for r in range(8)]
+        mixed = jnp.concatenate([mixed_ref[row : row + 16, :] for row in rows], axis=0)
+        turned_ref[...] = mixed.T
+
+    weight = jnp.concatenate([mine_ref[0], other_ref[0]], axis=1)
+    projected = jnp.dot(turned_ref[...], weight, preferred_element_type=F32)
+    c = table[73]
+    for place, parity in enumerate((c, 1 - c)):
+        cols = pl.ds(pl.multiple_of(parity * 128, 128), 128)
+        part = projected[:, place * 128 : place * 128 + 128]
+        out_ref[:, cols] = (voxels_ref[:, cols].astype(F32) + part).astype(BF16)
 
 
 def project_out(table, mixed, mine, other, voxels):
@@ -257,14 +301,15 @@
         output_kernel,
         grid_spec=pltpu.PrefetchScalarGridSpec(
             num_scalar_prefetch=1,
-            grid=(1,),
+            grid=(4,),
             in_specs=[
                 pl.BlockSpec(memory_space=pltpu.VMEM),
-                pl.BlockSpec((4, 1024, 128), lambda n, t: (0, 0, 0)),
-                pl.BlockSpec((4, 1024, 128), lambda n, t: (0, 0, 0)),
-                pl.BlockSpec((256, 1024), lambda n, t: (0, 0)),
+                pl.BlockSpec((1, 1024, 128), lambda n, t: (n, 0, 0)),
+                pl.BlockSpec((1, 1024, 128), lambda n, t: (n, 0, 0)),
+                pl.BlockSpec((256, 256), lambda n, t: (0, n)),
             ],
-            out_specs=pl.BlockSpec((256, 1024), lambda n, t: (0, 0)),
+            out_specs=pl.BlockSpec((256, 256), lambda n, t: (0, n)),
+            scratch_shapes=[pltpu.VMEM((256, 1024), BF16)],
         ),
         out_shape=jax.ShapeDtypeStruct((256, 1024), BF16),
         name="project_out",
@@ -280,26 +325,12 @@
 
 
 def layer(voxels, norm_gain, qkv_weight, out_weight, neighbours):
-    x, c, y, z = (lax.axis_index(a) for a in ("x", "c", "y", "z"))
-    region, owner = (2 * x + c, 8 * y + z)
+    x, c, z = (lax.axis_index(a) for a in ("x", "c", "z"))
     tokens = voxels.reshape(256, 1024)
-    ids = neighbours.reshape(1, 8)
-    entry = jnp.arange(128, dtype=jnp.int32)[:, None]
-    near_region = region + entry // 3 - 1
-    near_owner = owner + entry % 3 - 1
-    inside = (
-        (entry < 9) & (near_region >= 0) & (near_region < 8) & (near_owner >= 0) & (near_owner < 64)
-    )
-    listed = jnp.any((ids == near_region * 64 + near_owner) & inside, axis=1) | (entry[:, 0] == 4)
-
     normed = layer_norm(tokens, norm_gain)
     mine, other = gathered_line(normed)
 
-    parts = qkv_weight.reshape(2, 3, 8, 128)
-    flags = jnp.broadcast_to(listed.astype(BF16)[None, None], (2, 8, 128))
-    parts = [parts[:, 1], parts[:, 2], parts[:, 0], out_weight.reshape(2, 8, 128), flags]
-    parts = jnp.stack(parts, axis=2).transpose(1, 0, 2, 3).reshape(8, 1, 2, 640)
-    parts = jnp.broadcast_to(parts, (8, 8, 2, 640)).reshape(64, 2, 640)
+    parts = messages(neighbours.reshape(1, 8), qkv_weight, out_weight)
     swapped = lax.all_to_all(parts, ("x", "c", "z"), 0, 0, tiled=True)
     masks = lax.dynamic_index_in_dim(swapped.reshape(8, 8, 2, 640), z, 1, keepdims=False)
     table = jnp.concatenate([
@@ -309,7 +340,8 @@
     swapped = swapped.reshape(128, 640)
 
     weight = from_everyone(swapped[:, :384], "y")
-    own, queries = project_qkv(mine, other, weight)
+    own, queries, weight = project_call(mine_kernel, 0, 1, 0)(mine, on_chip(weight))
+    own, queries = project_call(other_kernel, 1, 0, 2)(on_chip(other), weight, own, queries)
     line = [(i, i + 1) for i in range(63)]
     low = lax.ppermute(own, PLANE, line)
     high = lax.ppermute(own, PLANE, [(j, i) for i, j in line])
@@ -317,10 +349,10 @@
     out_part, _ = lax.optimization_barrier((swapped[:, 384:512], queries))
     out_part = from_everyone(out_part, "y").reshape(1024, 128)
     own_total, own_top = attend_own(table, queries, own)
-    out_mine, out_other = gathered_line(out_part)
+    out_mine = from_everyone(out_part, "x")
+    out_other = shift(out_mine, "c", 1)
     mixed = attend(table, queries, low, high, own_total, own_top)
     mixed = lax.all_to_all(mixed, LINE, 0, 0, tiled=True).reshape(1024, 256)
-    out_mine, out_other = (part.reshape(4, 1024, 128) for part in (out_mine, out_other))
     result = project_out(table, mixed, out_mine, out_other, tokens)
     return result.reshape(voxels.shape)
 

time: 179 us -> 184 us (1.028)
  Pallas kernels: 31 us -> 36 us
  starting transfers between devices: 42.4 us -> 37.5 us
  waiting for transfers between devices: 49 us -> 52.8 us
    ppermute x8 -> x5, starting transfers between devices: 30.9 us -> 19.3 us  [shift(): return lax.ppermute(value, axis, [(i, (i + step) % n) for i in range(n)])]
    all_to_all x1 -> x2, waiting for transfers between devices: 22.1 us -> 32.4 us  [from_everyone(): lax.all_to_all(jnp.broadcast_to(value[None], (n, *value.shape)), axes, 0,...]
    all_to_all x1 -> x2, starting transfers between devices: 6.82 us -> 14.1 us  [from_everyone(): lax.all_to_all(jnp.broadcast_to(value[None], (n, *value.shape)), axes, 0,...]
    ppermute x1, waiting for transfers between devices: 4.16 us -> 0.01 us  [layer(): low = lax.ppermute(own, PLANE, line)]
    pallas_call x1 -> x3, Pallas kernels: 5.13 us -> 9.18 us  [the longest x1 4.05 us: layer(): project_call(other_kernel, 1, 0, 2)(on_chip(other), weight, own, queries)]
    ppermute x8 -> x5, waiting for transfers between devices: 18.9 us -> 17.9 us  [shift(): return lax.ppermute(value, axis, [(i, (i + step) % n) for i in range(n)])]
  transfers between devices with their start and end apart: 11 -> 9, of which waited for: 7 -> 6; matrix products, arithmetic and copies ran while one was open for 2% -> 1% of each run, Pallas kernels for 11% -> 14%
where the time goes in v4:
time: 184 us; the launch traced here: 183 us
  waiting for transfers between devices  52.8 us (29%)
  blocking collectives  50.8 us (28%)
  starting transfers between devices  37.5 us (20%)
  Pallas kernels  36 us (20%)
  other arithmetic  3.13 us (2%)
  local copies, waits for them, and re-layouts  2.31 us (1%)
    all_to_all x2, waiting for transfers between devices, from_everyone(): lax.all_to_all(jnp.broadcast_to(value[None], (n, *value.shape)), axes, 0,...  32.4 us
    all_to_all x1, blocking collectives, layer(): swapped = lax.all_to_all(parts, ('x', 'c', 'z'), 0, 0, tiled=True)  23.7 us
    ppermute x5, starting transfers between devices, shift(): return lax.ppermute(value, axis, [(i, (i + step) % n) for i in range(n)])  19.3 us
    ppermute x5, waiting for transfers between devices, shift(): return lax.ppermute(value, axis, [(i, (i + step) % n) for i in range(n)])  17.9 us
    all_to_all x1, blocking collectives, layer(): mixed = lax.all_to_all(mixed, LINE, 0, 0, tiled=True).reshape(1024, 256)  15.3 us
    all_to_all x2, starting transfers between devices, from_everyone(): lax.all_to_all(jnp.broadcast_to(value[None], (n, *value.shape)), axes, 0,...  14.1 us
    all_to_all x1, blocking collectives, from_everyone(): lax.all_to_all(jnp.broadcast_to(value[None], (n, *value.shape)), axes, 0,...  11.8 us
    pallas_call x1, Pallas kernels, attend(): pl.pallas_call(attend_kernel, grid_spec=pltpu.PrefetchScalarGridSpec(num_...  11.6 us
  transfers between devices with their start and end apart: 9, of which 6 were waited for; matrix products, arithmetic and copies ran while one was open for 1% of the time, Pallas kernels for 14%

profile of v4, /device:TPU:1, one launch (start us, length us, event | category | flops | bytes accessed | tf_op | source)
XLA Modules:
  0.0 182.6 jit_solution(6333121670844700335)
XLA Ops:
  0.0 2.2 %layer_norm.1 = bf16[256,1024]{1,0:T(8,128)(2,1)} custom-call(bf16[256,1024]{1,0:T(8,128)(2,1)} %bitcast.15, f32[1,1024]{1,0:T(1,128)} %bitcast.20), custom_call_target="tpu_custom_call" | custom-call | tf_op jit(solution)/shard_map/layer_norm/pallas_call | solution.py:28
  2.2 3.9 %collective-permute-start = (bf16[256,1024]{1,0:T(8,128)(2,1)}, bf16[256,1024]{1,0:T(8,128)(2,1)S(1)}, u32[]{:S(2)}, u32[]{:S(2)}) collective-permute-start(bf16[256,1024]{1,0:T(8,128)(2,1)} %layer_norm.1), channel_id=1, source_target_pairs={{0,128},{128,256},{256,384},{384,0},{1,129},{129,257},{257,385},{3... | collective-permute-start | bytes 1572872 | tf_op jit(solution)/shard_map/ppermute | solution.py:80
  6.1 3.2 %collective-permute-start.1 = (bf16[256,1024]{1,0:T(8,128)(2,1)}, bf16[256,1024]{1,0:T(8,128)(2,1)S(1)}, u32[]{:S(2)}, u32[]{:S(2)}) collective-permute-start(bf16[256,1024]{1,0:T(8,128)(2,1)} %layer_norm.1), channel_id=1, source_target_pairs={{0,384},{128,0},{256,128},{384,256},{1,385},{129,1},{257,129},{385... | collective-permute-start | bytes 1572872 | tf_op jit(solution)/shard_map/ppermute | solution.py:80
  9.3 3.6 %collective-permute-start.2 = (bf16[256,1024]{1,0:T(8,128)(2,1)}, bf16[256,1024]{1,0:T(8,128)(2,1)S(1)}, u32[]{:S(2)}, u32[]{:S(2)}) collective-permute-start(bf16[256,1024]{1,0:T(8,128)(2,1)} %layer_norm.1), channel_id=1, source_target_pairs={{0,256},{128,384},{256,0},{384,128},{1,257},{129,385},{257,1},{385... | collective-permute-start | bytes 1572872 | tf_op jit(solution)/shard_map/ppermute | solution.py:80
  14.1 2.7 %collective-permute-done.1 = bf16[256,1024]{1,0:T(8,128)(2,1)S(1)} collective-permute-done((bf16[256,1024]{1,0:T(8,128)(2,1)}, bf16[256,1024]{1,0:T(8,128)(2,1)S(1)}, u32[]{:S(2)}, u32[]{:S(2)}) %collective-permute-start.1) | collective-permute-done | bytes 524320 | tf_op jit(solution)/shard_map/ppermute | solution.py:80
  16.9 14.0 %collective-permute-done.2 = bf16[256,1024]{1,0:T(8,128)(2,1)S(1)} collective-permute-done((bf16[256,1024]{1,0:T(8,128)(2,1)}, bf16[256,1024]{1,0:T(8,128)(2,1)S(1)}, u32[]{:S(2)}, u32[]{:S(2)}) %collective-permute-start.2) | collective-permute-done | bytes 524320 | tf_op jit(solution)/shard_map/ppermute | solution.py:80
  30.8 2.5 %pad_maximum_fusion.tokens_ref = bf16[1024,1024]{1,0:T(8,128)(2,1)} fusion(bf16[256,1024]{1,0:T(8,128)(2,1)S(1)} %collective-permute-done.2, bf16[256,1024]{1,0:T(8,128)(2,1)S(1)} %collective-permute-done.1, bf16[256,1024]{1,0:T(8,128)(2,1)S(1)} %collective-permute-done, bf16[256,1024]{1,0:T(8,128)(2,1)} %layer_norm.1), kind=kLoop, calls=%fused_computation | loop fusion | flops 8388608 | bytes 4194304 | tf_op jit(solution)/shard_map/concatenate | solution.py:323
  33.4 4.9 %collective-permute-start.3 = (bf16[1024,1024]{1,0:T(8,128)(2,1)}, bf16[1024,1024]{1,0:T(8,128)(2,1)}, u32[]{:S(2)}, u32[]{:S(2)}) collective-permute-start(bf16[1024,1024]{1,0:T(8,128)(2,1)} %pad_maximum_fusion.tokens_ref), channel_id=1, source_target_pairs={{0,64},{64,0},{1,65},{65,1},{2,66},{66,2},{3,67},{67,3},{4,68},{68... | collective-permute-start | bytes 6291464 | tf_op jit(solution)/shard_map/ppermute | solution.py:80
  38.2 1.5 messages.1
  39.7 23.7 %all_to_all.25 = bf16[64,2,640]{2,1,0:T(2,128)(2,1)S(1)} all-to-all(bf16[64,2,640]{2,1,0:T(2,128)(2,1)} %messages.1), channel_id=1, replica_groups=mesh['x'=4,'c'=2,'y'=8,'z'=8] {'x','c','z'}, dimensions={0} | all-to-all | bytes 327680 | tf_op jit(solution)/shard_map/all_to_all | solution.py:334
  64.5 6.8 %all-to-all-start.1 = ((bf16[8,128,384]{2,1,0:T(8,128)(2,1)}), bf16[8,128,384]{2,1,0:T(8,128)(2,1)S(1)}, u32[]{:S(2)}, u32[]{:S(2)}) async-start(bf16[8,128,384]{2,1,0:T(8,128)(2,1)} %broadcast_in_dim.8), calls=%async_computation.1 | async-start | bytes 1572864 | tf_op jit(solution)/shard_map/all_to_all | solution.py:85
  71.3 22.1 %all-to-all-done.1.gathered_ref = bf16[8,128,384]{2,1,0:T(8,128)(2,1)S(1)} async-done(((bf16[8,128,384]{2,1,0:T(8,128)(2,1)}), bf16[8,128,384]{2,1,0:T(8,128)(2,1)S(1)}, u32[]{:S(2)}, u32[]{:S(2)}) %all-to-all-start.1) | async-done | bytes 786464 | tf_op jit(solution)/shard_map/all_to_all | solution.py:85
  93.5 3.6 %shard_map.55 = (bf16[8,512,128]{2,1,0:T(8,128)(2,1)}, bf16[8,256,128]{2,1,0:T(8,128)(2,1)}, bf16[1024,384]{1,0:T(8,128)(2,1)}) custom-call(bf16[1024,1024]{1,0:T(8,128)(2,1)} %pad_maximum_fusion.tokens_ref, bf16[8,128,384]{2,1,0:T(8,128)(2,1)S(1)} %all-to-all-done.1.gathered_ref), custom_call_target="tpu_custom_call" | custom-call | tf_op jit(solution)/shard_map/pallas_call | solution.py:343
  97.1 4.1 %shard_map.56 = (bf16[8,512,128]{2,1,0:T(8,128)(2,1)}, bf16[8,256,128]{2,1,0:T(8,128)(2,1)}) custom-call(bf16[1024,1024]{1,0:T(8,128)(2,1)} %collective-permute-done.3.tokens_ref, bf16[1024,384]{1,0:T(8,128)(2,1)} %get-tuple-element.13.weight_ref, bf16[8,512,128]{2,1,0:T(8,128)(2,1)} %get-tuple-element.14._, ...), custom_call_target="tpu_custom_call", output_to_operand_aliasing={{0}: (2, {}), {1}: (3, {})} | custom-call | tf_op jit(solution)/shard_map/pallas_call | solution.py:344
  101.2 11.8 %all_to_all.26 = bf16[8,128,128]{2,1,0:T(8,128)(2,1)S(1)} all-to-all(bf16[8,128,128]{2,1,0:T(8,128)(2,1)S(1)} %broadcast_in_dim.9), channel_id=1, replica_groups=mesh['x'=4,'c'=2,'y'=8,'z'=8] {'y'}, dimensions={0} | all-to-all | bytes 524288 | tf_op jit(solution)/shard_map/all_to_all | solution.py:85
  114.1 7.3 %all-to-all-start.4 = ((bf16[4,1024,128]{2,1,0:T(8,128)(2,1)}), bf16[4,1024,128]{2,1,0:T(8,128)(2,1)}, u32[]{:S(2)}, u32[]{:S(2)}) async-start(bf16[4,1024,128]{2,1,0:T(8,128)(2,1)} %broadcast_in_dim.22), calls=%async_computation.4 | async-start | bytes 2097152 | tf_op jit(solution)/shard_map/all_to_all | solution.py:85
  121.4 2.8 %collective-permute-start.4 = (bf16[8,512,128]{2,1,0:T(8,128)(2,1)S(1)}, bf16[8,512,128]{2,1,0:T(8,128)(2,1)S(1)}, u32[]{:S(2)}, u32[]{:S(2)}) collective-permute-start(bf16[8,512,128]{2,1,0:T(8,128)(2,1)S(1)} %copy-done), channel_id=1, source_target_pairs={{0,1},{1,2},{2,3},{3,4},{4,5},{5,6},{6,7},{7,8},{8,9},{9,10},{10,1... | collective-permute-start | bytes 3145736 | tf_op jit(solution)/shard_map/ppermute | solution.py:346
  125.6 10.3 %all-to-all-done.4.mine_ref = bf16[4,1024,128]{2,1,0:T(8,128)(2,1)} async-done(((bf16[4,1024,128]{2,1,0:T(8,128)(2,1)}), bf16[4,1024,128]{2,1,0:T(8,128)(2,1)}, u32[]{:S(2)}, u32[]{:S(2)}) %all-to-all-start.4) | async-done | bytes 1048608 | tf_op jit(solution)/shard_map/all_to_all | solution.py:85
  135.8 3.7 %collective-permute-start.6 = (bf16[4,1024,128]{2,1,0:T(8,128)(2,1)}, bf16[4,1024,128]{2,1,0:T(8,128)(2,1)}, u32[]{:S(2)}, u32[]{:S(2)}) collective-permute-start(bf16[4,1024,128]{2,1,0:T(8,128)(2,1)} %all-to-all-done.4.mine_ref), channel_id=1, source_target_pairs={{0,64},{64,0},{1,65},{65,1},{2,66},{66,2},{3,67},{67,3},{4,68},{68... | collective-permute-start | bytes 3145736 | tf_op jit(solution)/shard_map/ppermute | solution.py:80
  140.2 8.0 %attend_own.1 = (f32[8,2,80,256]{3,2,1,0:T(8,128)}, f32[8,2,8,256]{3,2,1,0:T(8,128)}) custom-call(s32[74]{0:T(128)} %pad_add_fusion.table, bf16[8,256,128]{2,1,0:T(8,128)(2,1)} %get-tuple-element.16.query_ref, bf16[8,512,128]{2,1,0:T(8,128)(2,1)} %get-tuple-element.17.own_ref), custom_call_target="tpu_custom_call" | custom-call | tf_op jit(solution)/shard_map/attend_own/pallas_call | solution.py:228
  148.2 2.5 %collective-permute-done.5.high_ref = bf16[8,512,128]{2,1,0:T(8,128)(2,1)S(1)} collective-permute-done((bf16[8,512,128]{2,1,0:T(8,128)(2,1)S(1)}, bf16[8,512,128]{2,1,0:T(8,128)(2,1)S(1)}, u32[]{:S(2)}, u32[]{:S(2)}) %collective-permute-start.5) | collective-permute-done | bytes 1048608 | tf_op jit(solution)/shard_map/ppermute | solution.py:347
  150.7 11.6 %attend.1 = bf16[8,128,256]{2,1,0:T(8,128)(2,1)} custom-call(s32[74]{0:T(128)} %pad_add_fusion.table, bf16[8,256,128]{2,1,0:T(8,128)(2,1)} %get-tuple-element.16.query_ref, bf16[8,512,128]{2,1,0:T(8,128)(2,1)S(1)} %collective-permute-done.4.low_ref, bf16[8,512,128]{2,1,0:T(8,128)(2,1)S(1)} %collective-permute-done.5.high_ref, ...), custom_call_target="tpu_custom_call" | custom-call | tf_op jit(solution)/shard_map/attend/pallas_call | solution.py:263
  162.3 15.3 %all_to_all.27 = bf16[8,128,256]{2,1,0:T(8,128)(2,1)S(1)} all-to-all(bf16[8,128,256]{2,1,0:T(8,128)(2,1)} %attend.1), channel_id=1, replica_groups=mesh['x'=4,'c'=2,'y'=8,'z'=8] {'x','c'}, dimensions={0} | all-to-all | bytes 1048576 | tf_op jit(solution)/shard_map/all_to_all | solution.py:355
  177.7 5.0 %project_out.1 = bf16[256,1024]{1,0:T(8,128)(2,1)} custom-call(s32[74]{0:T(128)} %pad_add_fusion.table, bf16[1024,256]{1,0:T(8,128)(2,1)S(1)} %bitcast.14, bf16[4,1024,128]{2,1,0:T(8,128)(2,1)} %all-to-all-done.4.mine_ref, bf16[4,1024,128]{2,1,0:T(8,128)(2,1)} %collective-permute-done.6.other_ref, bf16[256,1024]{1,0:T(8,128)(2,1)} %bitcast.16), custom_call_target="tpu_custom_call" | custom-call | tf_op jit(solution)/shard_map/project_out/pallas_call | solution.py:300
  (21 shorter events, 5.4 us)
Async XLA Ops:
  2.2 12.0 %collective-permute-start = (bf16[256,1024]{1,0:T(8,128)(2,1)}, bf16[256,1024]{1,0:T(8,128)(2,1)S(1)}, u32[]{:S(2)}, u32[]{:S(2)}) collective-permute-start(bf16[256,1024]{1,0:T(8,128)(2,1)} %layer_norm.1), channel_id=1, source_target_pairs={{0,128},{128,256},{256,384},{384,0},{1,129},{129,257},{257,385},{3... | collective-permute-start | bytes 1572872 | tf_op jit(solution)/shard_map/ppermute | solution.py:80
  6.1 10.8 %collective-permute-start.1 = (bf16[256,1024]{1,0:T(8,128)(2,1)}, bf16[256,1024]{1,0:T(8,128)(2,1)S(1)}, u32[]{:S(2)}, u32[]{:S(2)}) collective-permute-start(bf16[256,1024]{1,0:T(8,128)(2,1)} %layer_norm.1), channel_id=1, source_target_pairs={{0,384},{128,0},{256,128},{384,256},{1,385},{129,1},{257,129},{385... | collective-permute-start | bytes 1572872 | tf_op jit(solution)/shard_map/ppermute | solution.py:80
  9.3 21.5 %collective-permute-start.2 = (bf16[256,1024]{1,0:T(8,128)(2,1)}, bf16[256,1024]{1,0:T(8,128)(2,1)S(1)}, u32[]{:S(2)}, u32[]{:S(2)}) collective-permute-start(bf16[256,1024]{1,0:T(8,128)(2,1)} %layer_norm.1), channel_id=1, source_target_pairs={{0,256},{128,384},{256,0},{384,128},{1,257},{129,385},{257,1},{385... | collective-permute-start | bytes 1572872 | tf_op jit(solution)/shard_map/ppermute | solution.py:80
  33.4 63.7 %collective-permute-start.3 = (bf16[1024,1024]{1,0:T(8,128)(2,1)}, bf16[1024,1024]{1,0:T(8,128)(2,1)}, u32[]{:S(2)}, u32[]{:S(2)}) collective-permute-start(bf16[1024,1024]{1,0:T(8,128)(2,1)} %pad_maximum_fusion.tokens_ref), channel_id=1, source_target_pairs={{0,64},{64,0},{1,65},{65,1},{2,66},{66,2},{3,67},{67,3},{4,68},{68... | collective-permute-start | bytes 6291464 | tf_op jit(solution)/shard_map/ppermute | solution.py:80
  63.5 33.6 %copy-start.1 = (bf16[128,640]{1,0:T(8,128)(2,1)}, bf16[128,640]{1,0:T(8,128)(2,1)S(1)}, u32[]{:S(2)}) copy-start(bf16[128,640]{1,0:T(8,128)(2,1)S(1)} %reshape.32) | copy-start | bytes 491524
  64.5 28.9 %all-to-all-start.1 = ((bf16[8,128,384]{2,1,0:T(8,128)(2,1)}), bf16[8,128,384]{2,1,0:T(8,128)(2,1)S(1)}, u32[]{:S(2)}, u32[]{:S(2)}) async-start(bf16[8,128,384]{2,1,0:T(8,128)(2,1)} %broadcast_in_dim.8), calls=%async_computation.1 | async-start | bytes 1572864 | tf_op jit(solution)/shard_map/all_to_all | solution.py:85
  97.1 4.1 %slice-start = ((bf16[128,640]{1,0:T(8,128)(2,1)}), bf16[128,128]{1,0:T(8,128)(2,1)S(1)}, s32[]{:S(2)}) async-start(bf16[128,640]{1,0:T(8,128)(2,1)} %copy-done.1), calls=%async_computation.5 | async-start | bytes 65536 | tf_op jit(solution)/shard_map/slice | solution.py:349
  101.2 20.3 %copy-start = (bf16[8,512,128]{2,1,0:T(8,128)(2,1)S(1)}, bf16[8,512,128]{2,1,0:T(8,128)(2,1)}, u32[]{:S(2)}) copy-start(bf16[8,512,128]{2,1,0:T(8,128)(2,1)} %get-tuple-element.17.own_ref) | copy-start | bytes 3145732
  114.1 21.7 %all-to-all-start.4 = ((bf16[4,1024,128]{2,1,0:T(8,128)(2,1)}), bf16[4,1024,128]{2,1,0:T(8,128)(2,1)}, u32[]{:S(2)}, u32[]{:S(2)}) async-start(bf16[4,1024,128]{2,1,0:T(8,128)(2,1)} %broadcast_in_dim.22), calls=%async_computation.4 | async-start | bytes 2097152 | tf_op jit(solution)/shard_map/all_to_all | solution.py:85
  121.4 26.8 %collective-permute-start.4 = (bf16[8,512,128]{2,1,0:T(8,128)(2,1)S(1)}, bf16[8,512,128]{2,1,0:T(8,128)(2,1)S(1)}, u32[]{:S(2)}, u32[]{:S(2)}) collective-permute-start(bf16[8,512,128]{2,1,0:T(8,128)(2,1)S(1)} %copy-done), channel_id=1, source_target_pairs={{0,1},{1,2},{2,3},{3,4},{4,5},{5,6},{6,7},{7,8},{8,9},{9,10},{10,1... | collective-permute-start | bytes 3145736 | tf_op jit(solution)/shard_map/ppermute | solution.py:346
  124.3 26.4 %collective-permute-start.5 = (bf16[8,512,128]{2,1,0:T(8,128)(2,1)S(1)}, bf16[8,512,128]{2,1,0:T(8,128)(2,1)S(1)}, u32[]{:S(2)}, u32[]{:S(2)}) collective-permute-start(bf16[8,512,128]{2,1,0:T(8,128)(2,1)S(1)} %copy-done), channel_id=1, source_target_pairs={{1,0},{2,1},{3,2},{4,3},{5,4},{6,5},{7,6},{8,7},{9,8},{10,9},{11,1... | collective-permute-start | bytes 3145736 | tf_op jit(solution)/shard_map/ppermute | solution.py:347
  135.8 41.8 %collective-permute-start.6 = (bf16[4,1024,128]{2,1,0:T(8,128)(2,1)}, bf16[4,1024,128]{2,1,0:T(8,128)(2,1)}, u32[]{:S(2)}, u32[]{:S(2)}) collective-permute-start(bf16[4,1024,128]{2,1,0:T(8,128)(2,1)} %all-to-all-done.4.mine_ref), channel_id=1, source_target_pairs={{0,64},{64,0},{1,65},{65,1},{2,66},{66,2},{3,67},{67,3},{4,68},{68... | collective-permute-start | bytes 3145736 | tf_op jit(solution)/shard_map/ppermute | solution.py:80

commit v5 on v4

--- a/solution.py
+++ b/solution.py
@@ -104,18 +104,7 @@
     return pltpu.with_memory_space_constraint(value, pltpu.VMEM)
 
 
-def project_tokens(tokens, weight, kv_ref, query_ref):
-    projected = jnp.dot(tokens, weight, preferred_element_type=F32)
-    for block in range(2):
-        rows = slice(block * 256, block * 256 + 256)
-        kv_ref[block, 0:256, :] = projected[rows, :128].astype(BF16)
-        values = projected[rows, 128:256].astype(BF16).T
-        kv_ref[block, 256:384, :] = values[:, :128]
-        kv_ref[block, 384:512, :] = values[:, 128:]
-        query_ref[block] = (projected[rows, 256:] * FACTOR).astype(BF16)
-
-
-def mine_kernel(tokens_ref, gathered_ref, kv_ref, query_ref, weight_ref):
+def qkv_kernel(mine_ref, other_ref, gathered_ref, kv_ref, query_ref, weight_ref):
     @pl.when(pl.program_id(0) == 0)
     def _():
         for region in range(8):
@@ -123,37 +112,45 @@
                 row = region * 128 + y * 16
                 weight_ref[row : row + 16] = gathered_ref[y, region * 16 : region * 16 + 16]
 
-    project_tokens(tokens_ref[...], weight_ref[...], kv_ref, query_ref)
-
-
-def other_kernel(tokens_ref, weight_ref, _, __, kv_ref, query_ref):
-    rows = pl.ds(pl.multiple_of(pl.program_id(0) * 512, 512), 512)
-    project_tokens(tokens_ref[rows, :], weight_ref[...], kv_ref, query_ref)
-
-
-def project_call(kernel, first, weight_out, aliased):
-    whole = pl.BlockSpec((1024, 384), lambda s: (0, 0))
-    on_chip_spec = pl.BlockSpec(memory_space=pltpu.VMEM)
-    return pl.pallas_call(
-        kernel,
-        grid=(2,),
+    def project(tokens):
+        projected = jnp.dot(tokens, weight_ref[...], preferred_element_type=F32)
+        for block in range(2):
+            rows = slice(block * 256, block * 256 + 256)
+            kv_ref[block, 0:256, :] = projected[rows, :128].astype(BF16)
+            values = projected[rows, 128:256].astype(BF16).T
+            kv_ref[block, 256:384, :] = values[:, :128]
+            kv_ref[block, 384:512, :] = values[:, 128:]
+            query_ref[block] = (projected[rows, 256:] * FACTOR).astype(BF16)
+
+    @pl.when(pl.program_id(0) < 2)
+    def _():
+        project(mine_ref[...])
+
+    @pl.when(pl.program_id(0) >= 2)
+    def _():
+        project(other_ref[...])
+
+
+def project_qkv(mine, other, weight):
+    return pl.pallas_call(
+        qkv_kernel,
+        grid=(4,),
         in_specs=[
-            pl.BlockSpec((512, 1024), lambda s: (s, 0)) if weight_out else on_chip_spec,
-            on_chip_spec if weight_out else whole,
-            *[pl.BlockSpec(memory_space=pl.ANY)] * aliased,
+            pl.BlockSpec((512, 1024), lambda s: (jnp.minimum(s, 1), 0)),
+            pl.BlockSpec((512, 1024), lambda s: (jnp.maximum(s - 2, 0), 0)),
+            pl.BlockSpec(memory_space=pltpu.VMEM),
         ],
         out_specs=[
-            pl.BlockSpec((2, 512, 128), lambda s: (2 * first + s, 0, 0)),
-            pl.BlockSpec((2, 256, 128), lambda s: (2 * first + s, 0, 0)),
-            *[whole] * weight_out,
+            pl.BlockSpec((2, 512, 128), lambda s: (s, 0, 0)),
+            pl.BlockSpec((2, 256, 128), lambda s: (s, 0, 0)),
         ],
         out_shape=[
             jax.ShapeDtypeStruct((8, 512, 128), BF16),
             jax.ShapeDtypeStruct((8, 256, 128), BF16),
-            *[jax.ShapeDtypeStruct((1024, 384), BF16)] * weight_out,
-        ],
-        input_output_aliases={2: 0, 3: 1} if aliased else {},
-    )
+        ],
+        scratch_shapes=[pltpu.VMEM((1024, 384), BF16)],
+        name="project_qkv",
+    )(mine, other, on_chip(weight))
 
 
 def near_places(table, slot, refs):
@@ -287,7 +284,7 @@
         mixed = jnp.concatenate([mixed_ref[row : row + 16, :] for row in rows], axis=0)
         turned_ref[...] = mixed.T
 
-    weight = jnp.concatenate([mine_ref[0], other_ref[0]], axis=1)
+    weight = jnp.concatenate([mine_ref[0], other_ref[pl.program_id(0)]], axis=1)
     projected = jnp.dot(turned_ref[...], weight, preferred_element_type=F32)
     c = table[73]
     for place, parity in enumerate((c, 1 - c)):
@@ -305,7 +302,7 @@
             in_specs=[
                 pl.BlockSpec(memory_space=pltpu.VMEM),
                 pl.BlockSpec((1, 1024, 128), lambda n, t: (n, 0, 0)),
-                pl.BlockSpec((1, 1024, 128), lambda n, t: (n, 0, 0)),
+                pl.BlockSpec(memory_space=pltpu.VMEM),
                 pl.BlockSpec((256, 256), lambda n, t: (0, n)),
             ],
             out_specs=pl.BlockSpec((256, 256), lambda n, t: (0, n)),
@@ -313,7 +310,7 @@
         ),
         out_shape=jax.ShapeDtypeStruct((256, 1024), BF16),
         name="project_out",
-    )(table, on_chip(mixed), mine, other, voxels)
+    )(table, on_chip(mixed), mine, on_chip(other), voxels)
 
 
 def gathered_line(value):
@@ -340,8 +337,7 @@
     swapped = swapped.reshape(128, 640)
 
     weight = from_everyone(swapped[:, :384], "y")
-    own, queries, weight = project_call(mine_kernel, 0, 1, 0)(mine, on_chip(weight))
-    own, queries = project_call(other_kernel, 1, 0, 2)(on_chip(other), weight, own, queries)
+    own, queries = project_qkv(mine, other, weight)
     line = [(i, i + 1) for i in range(63)]
     low = lax.ppermute(own, PLANE, line)
     high = lax.ppermute(own, PLANE, [(j, i) for i, j in line])

time: 184 us -> 182 us (0.989)
    pallas_call x2 -> x1, Pallas kernels: 7.69 us -> 6.08 us  [project_qkv(): pl.pallas_call(qkv_kernel, grid=(4,), in_specs=[pl.BlockSpec((512, 1024),...]
  transfers between devices with their start and end apart: 9 -> 9, of which waited for: 6 -> 6; matrix products, arithmetic and copies ran while one was open for 1% -> 1% of each run, Pallas kernels for 14% -> 12%
where the time goes in v5:
time: 182 us; the launch traced here: 181 us
  waiting for transfers between devices  53.1 us (29%)
  blocking collectives  49.6 us (27%)
  starting transfers between devices  36.8 us (20%)
  Pallas kernels  34.2 us (19%)
  local copies, waits for them, and re-layouts  3.6 us (2%)
  other arithmetic  3.21 us (2%)
    all_to_all x2, waiting for transfers between devices, from_everyone(): lax.all_to_all(jnp.broadcast_to(value[None], (n, *value.shape)), axes, 0,...  32.4 us
    all_to_all x1, blocking collectives, layer(): swapped = lax.all_to_all(parts, ('x', 'c', 'z'), 0, 0, tiled=True)  22.6 us
    ppermute x5, starting transfers between devices, shift(): return lax.ppermute(value, axis, [(i, (i + step) % n) for i in range(n)])  18.6 us
    ppermute x5, waiting for transfers between devices, shift(): return lax.ppermute(value, axis, [(i, (i + step) % n) for i in range(n)])  18.2 us
    all_to_all x1, blocking collectives, layer(): mixed = lax.all_to_all(mixed, LINE, 0, 0, tiled=True).reshape(1024, 256)  15.3 us
    all_to_all x2, starting transfers between devices, from_everyone(): lax.all_to_all(jnp.broadcast_to(value[None], (n, *value.shape)), axes, 0,...  14.1 us
    pallas_call x1, Pallas kernels, attend(): pl.pallas_call(attend_kernel, grid_spec=pltpu.PrefetchScalarGridSpec(num_...  11.7 us
    all_to_all x1, blocking collectives, from_everyone(): lax.all_to_all(jnp.broadcast_to(value[None], (n, *value.shape)), axes, 0,...  11.6 us
  transfers between devices with their start and end apart: 9, of which 6 were waited for; matrix products, arithmetic and copies ran while one was open for 1% of the time, Pallas kernels for 12%

profile of v5, /device:TPU:1, one launch (start us, length us, event | category | flops | bytes accessed | tf_op | source)
XLA Modules:
  0.0 180.6 jit_solution(5990221350620502920)
XLA Ops:
  0.0 2.2 %layer_norm.1 = bf16[256,1024]{1,0:T(8,128)(2,1)} custom-call(bf16[256,1024]{1,0:T(8,128)(2,1)} %bitcast.15, f32[1,1024]{1,0:T(1,128)} %bitcast.20), custom_call_target="tpu_custom_call" | custom-call | tf_op jit(solution)/shard_map/layer_norm/pallas_call | solution.py:28
  2.2 5.5 %collective-permute-start.2 = (bf16[256,1024]{1,0:T(8,128)(2,1)}, bf16[256,1024]{1,0:T(8,128)(2,1)S(1)}, u32[]{:S(2)}, u32[]{:S(2)}) collective-permute-start(bf16[256,1024]{1,0:T(8,128)(2,1)} %layer_norm.1), channel_id=1, source_target_pairs={{0,256},{128,384},{256,0},{384,128},{1,257},{129,385},{257,1},{385... | collective-permute-start | bytes 1572872 | tf_op jit(solution)/shard_map/ppermute | solution.py:80
  7.6 2.8 %collective-permute-start.1 = (bf16[256,1024]{1,0:T(8,128)(2,1)}, bf16[256,1024]{1,0:T(8,128)(2,1)S(1)}, u32[]{:S(2)}, u32[]{:S(2)}) collective-permute-start(bf16[256,1024]{1,0:T(8,128)(2,1)} %layer_norm.1), channel_id=1, source_target_pairs={{0,384},{128,0},{256,128},{384,256},{1,385},{129,1},{257,129},{385... | collective-permute-start | bytes 1572872 | tf_op jit(solution)/shard_map/ppermute | solution.py:80
  10.4 2.5 %collective-permute-start = (bf16[256,1024]{1,0:T(8,128)(2,1)}, bf16[256,1024]{1,0:T(8,128)(2,1)S(1)}, u32[]{:S(2)}, u32[]{:S(2)}) collective-permute-start(bf16[256,1024]{1,0:T(8,128)(2,1)} %layer_norm.1), channel_id=1, source_target_pairs={{0,128},{128,256},{256,384},{384,0},{1,129},{129,257},{257,385},{3... | collective-permute-start | bytes 1572872 | tf_op jit(solution)/shard_map/ppermute | solution.py:80
  12.9 3.3 %collective-permute-done.2 = bf16[256,1024]{1,0:T(8,128)(2,1)S(1)} collective-permute-done((bf16[256,1024]{1,0:T(8,128)(2,1)}, bf16[256,1024]{1,0:T(8,128)(2,1)S(1)}, u32[]{:S(2)}, u32[]{:S(2)}) %collective-permute-start.2) | collective-permute-done | bytes 524320 | tf_op jit(solution)/shard_map/ppermute | solution.py:80
  16.3 14.6 %collective-permute-done.1 = bf16[256,1024]{1,0:T(8,128)(2,1)S(1)} collective-permute-done((bf16[256,1024]{1,0:T(8,128)(2,1)}, bf16[256,1024]{1,0:T(8,128)(2,1)S(1)}, u32[]{:S(2)}, u32[]{:S(2)}) %collective-permute-start.1) | collective-permute-done | bytes 524320 | tf_op jit(solution)/shard_map/ppermute | solution.py:80
  31.1 2.5 %pad_maximum_fusion.mine_ref = bf16[1024,1024]{1,0:T(8,128)(2,1)} fusion(bf16[256,1024]{1,0:T(8,128)(2,1)S(1)} %collective-permute-done.2, bf16[256,1024]{1,0:T(8,128)(2,1)S(1)} %collective-permute-done.1, bf16[256,1024]{1,0:T(8,128)(2,1)S(1)} %collective-permute-done, bf16[256,1024]{1,0:T(8,128)(2,1)} %layer_norm.1), kind=kLoop, calls=%fused_computation | loop fusion | flops 8388608 | bytes 4194304 | tf_op jit(solution)/shard_map/concatenate | solution.py:320
  33.6 4.2 %collective-permute-start.3 = (bf16[1024,1024]{1,0:T(8,128)(2,1)}, bf16[1024,1024]{1,0:T(8,128)(2,1)S(1)}, u32[]{:S(2)}, u32[]{:S(2)}) collective-permute-start(bf16[1024,1024]{1,0:T(8,128)(2,1)} %pad_maximum_fusion.mine_ref), channel_id=1, source_target_pairs={{0,64},{64,0},{1,65},{65,1},{2,66},{66,2},{3,67},{67,3},{4,68},{68... | collective-permute-start | bytes 6291464 | tf_op jit(solution)/shard_map/ppermute | solution.py:80
  37.8 1.5 messages.1
  39.3 22.6 %all_to_all.25 = bf16[64,2,640]{2,1,0:T(2,128)(2,1)S(1)} all-to-all(bf16[64,2,640]{2,1,0:T(2,128)(2,1)} %messages.1), channel_id=1, replica_groups=mesh['x'=4,'c'=2,'y'=8,'z'=8] {'x','c','z'}, dimensions={0} | all-to-all | bytes 327680 | tf_op jit(solution)/shard_map/all_to_all | solution.py:331
  62.9 6.8 %all-to-all-start.1 = ((bf16[8,128,384]{2,1,0:T(8,128)(2,1)}), bf16[8,128,384]{2,1,0:T(8,128)(2,1)S(1)}, u32[]{:S(2)}, u32[]{:S(2)}) async-start(bf16[8,128,384]{2,1,0:T(8,128)(2,1)} %broadcast_in_dim.8), calls=%async_computation.1 | async-start | bytes 1572864 | tf_op jit(solution)/shard_map/all_to_all | solution.py:85
  69.8 22.1 %all-to-all-done.1.gathered_ref = bf16[8,128,384]{2,1,0:T(8,128)(2,1)S(1)} async-done(((bf16[8,128,384]{2,1,0:T(8,128)(2,1)}), bf16[8,128,384]{2,1,0:T(8,128)(2,1)S(1)}, u32[]{:S(2)}, u32[]{:S(2)}) %all-to-all-start.1) | async-done | bytes 786464 | tf_op jit(solution)/shard_map/all_to_all | solution.py:85
  91.9 1.3 copy-done
  93.2 6.1 %project_qkv.1 = (bf16[8,512,128]{2,1,0:T(8,128)(2,1)}, bf16[8,256,128]{2,1,0:T(8,128)(2,1)}) custom-call(bf16[1024,1024]{1,0:T(8,128)(2,1)} %pad_maximum_fusion.mine_ref, bf16[1024,1024]{1,0:T(8,128)(2,1)} %copy-done, bf16[8,128,384]{2,1,0:T(8,128)(2,1)S(1)} %all-to-all-done.1.gathered_ref), custom_call_target="tpu_custom_call" | custom-call | tf_op jit(solution)/shard_map/project_qkv/pallas_call | solution.py:135
  99.3 11.6 %all_to_all.26 = bf16[8,128,128]{2,1,0:T(8,128)(2,1)S(1)} all-to-all(bf16[8,128,128]{2,1,0:T(8,128)(2,1)S(1)} %broadcast_in_dim.9), channel_id=1, replica_groups=mesh['x'=4,'c'=2,'y'=8,'z'=8] {'y'}, dimensions={0} | all-to-all | bytes 524288 | tf_op jit(solution)/shard_map/all_to_all | solution.py:85
  112.1 7.3 %all-to-all-start.4 = ((bf16[4,1024,128]{2,1,0:T(8,128)(2,1)}), bf16[4,1024,128]{2,1,0:T(8,128)(2,1)}, u32[]{:S(2)}, u32[]{:S(2)}) async-start(bf16[4,1024,128]{2,1,0:T(8,128)(2,1)} %broadcast_in_dim.22), calls=%async_computation.4 | async-start | bytes 2097152 | tf_op jit(solution)/shard_map/all_to_all | solution.py:85
  119.4 2.8 %collective-permute-start.4 = (bf16[8,512,128]{2,1,0:T(8,128)(2,1)}, bf16[8,512,128]{2,1,0:T(8,128)(2,1)S(1)}, u32[]{:S(2)}, u32[]{:S(2)}) collective-permute-start(bf16[8,512,128]{2,1,0:T(8,128)(2,1)} %get-tuple-element.11.own_ref), channel_id=1, source_target_pairs={{0,1},{1,2},{2,3},{3,4},{4,5},{5,6},{6,7},{7,8},{8,9},{9,10},{10,1... | collective-permute-start | bytes 3145736 | tf_op jit(solution)/shard_map/ppermute | solution.py:342
  123.5 10.3 %all-to-all-done.4.mine_ref = bf16[4,1024,128]{2,1,0:T(8,128)(2,1)} async-done(((bf16[4,1024,128]{2,1,0:T(8,128)(2,1)}), bf16[4,1024,128]{2,1,0:T(8,128)(2,1)}, u32[]{:S(2)}, u32[]{:S(2)}) %all-to-all-start.4) | async-done | bytes 1048608 | tf_op jit(solution)/shard_map/all_to_all | solution.py:85
  133.8 3.7 %collective-permute-start.6 = (bf16[4,1024,128]{2,1,0:T(8,128)(2,1)}, bf16[4,1024,128]{2,1,0:T(8,128)(2,1)S(1)}, u32[]{:S(2)}, u32[]{:S(2)}) collective-permute-start(bf16[4,1024,128]{2,1,0:T(8,128)(2,1)} %all-to-all-done.4.mine_ref), channel_id=1, source_target_pairs={{0,64},{64,0},{1,65},{65,1},{2,66},{66,2},{3,67},{67,3},{4,68},{68... | collective-permute-start | bytes 3145736 | tf_op jit(solution)/shard_map/ppermute | solution.py:80
  138.2 8.0 %attend_own.1 = (f32[8,2,80,256]{3,2,1,0:T(8,128)}, f32[8,2,8,256]{3,2,1,0:T(8,128)}) custom-call(s32[74]{0:T(128)} %pad_add_fusion.table, bf16[8,256,128]{2,1,0:T(8,128)(2,1)} %get-tuple-element.10.query_ref, bf16[8,512,128]{2,1,0:T(8,128)(2,1)} %get-tuple-element.11.own_ref), custom_call_target="tpu_custom_call" | custom-call | tf_op jit(solution)/shard_map/attend_own/pallas_call | solution.py:225
  146.2 2.6 %collective-permute-done.5.high_ref = bf16[8,512,128]{2,1,0:T(8,128)(2,1)S(1)} collective-permute-done((bf16[8,512,128]{2,1,0:T(8,128)(2,1)}, bf16[8,512,128]{2,1,0:T(8,128)(2,1)S(1)}, u32[]{:S(2)}, u32[]{:S(2)}) %collective-permute-start.5) | collective-permute-done | bytes 1048608 | tf_op jit(solution)/shard_map/ppermute | solution.py:343
  148.8 11.7 %attend.1 = bf16[8,128,256]{2,1,0:T(8,128)(2,1)} custom-call(s32[74]{0:T(128)} %pad_add_fusion.table, bf16[8,256,128]{2,1,0:T(8,128)(2,1)} %get-tuple-element.10.query_ref, bf16[8,512,128]{2,1,0:T(8,128)(2,1)S(1)} %collective-permute-done.4.low_ref, bf16[8,512,128]{2,1,0:T(8,128)(2,1)S(1)} %collective-permute-done.5.high_ref, ...), custom_call_target="tpu_custom_call" | custom-call | tf_op jit(solution)/shard_map/attend/pallas_call | solution.py:260
  160.5 15.3 %all_to_all.27 = bf16[8,128,256]{2,1,0:T(8,128)(2,1)S(1)} all-to-all(bf16[8,128,256]{2,1,0:T(8,128)(2,1)} %attend.1), channel_id=1, replica_groups=mesh['x'=4,'c'=2,'y'=8,'z'=8] {'x','c'}, dimensions={0} | all-to-all | bytes 1048576 | tf_op jit(solution)/shard_map/all_to_all | solution.py:351
  175.8 4.8 %project_out.1 = bf16[256,1024]{1,0:T(8,128)(2,1)} custom-call(s32[74]{0:T(128)} %pad_add_fusion.table, bf16[1024,256]{1,0:T(8,128)(2,1)S(1)} %bitcast.14, bf16[4,1024,128]{2,1,0:T(8,128)(2,1)} %all-to-all-done.4.mine_ref, bf16[4,1024,128]{2,1,0:T(8,128)(2,1)S(1)} %collective-permute-done.6.other_ref, bf16[256,1024]{1,0:T(8,128)(2,1)} %bitcast.16), custom_call_target="tpu_custom_call" | custom-call | tf_op jit(solution)/shard_map/project_out/pallas_call | solution.py:297
  (17 shorter events, 4.5 us)
Async XLA Ops:
  2.2 14.1 %collective-permute-start.2 = (bf16[256,1024]{1,0:T(8,128)(2,1)}, bf16[256,1024]{1,0:T(8,128)(2,1)S(1)}, u32[]{:S(2)}, u32[]{:S(2)}) collective-permute-start(bf16[256,1024]{1,0:T(8,128)(2,1)} %layer_norm.1), channel_id=1, source_target_pairs={{0,256},{128,384},{256,0},{384,128},{1,257},{129,385},{257,1},{385... | collective-permute-start | bytes 1572872 | tf_op jit(solution)/shard_map/ppermute | solution.py:80
  7.6 23.2 %collective-permute-start.1 = (bf16[256,1024]{1,0:T(8,128)(2,1)}, bf16[256,1024]{1,0:T(8,128)(2,1)S(1)}, u32[]{:S(2)}, u32[]{:S(2)}) collective-permute-start(bf16[256,1024]{1,0:T(8,128)(2,1)} %layer_norm.1), channel_id=1, source_target_pairs={{0,384},{128,0},{256,128},{384,256},{1,385},{129,1},{257,129},{385... | collective-permute-start | bytes 1572872 | tf_op jit(solution)/shard_map/ppermute | solution.py:80
  10.4 20.7 %collective-permute-start = (bf16[256,1024]{1,0:T(8,128)(2,1)}, bf16[256,1024]{1,0:T(8,128)(2,1)S(1)}, u32[]{:S(2)}, u32[]{:S(2)}) collective-permute-start(bf16[256,1024]{1,0:T(8,128)(2,1)} %layer_norm.1), channel_id=1, source_target_pairs={{0,128},{128,256},{256,384},{384,0},{1,129},{129,257},{257,385},{3... | collective-permute-start | bytes 1572872 | tf_op jit(solution)/shard_map/ppermute | solution.py:80
  33.6 58.3 %collective-permute-start.3 = (bf16[1024,1024]{1,0:T(8,128)(2,1)}, bf16[1024,1024]{1,0:T(8,128)(2,1)S(1)}, u32[]{:S(2)}, u32[]{:S(2)}) collective-permute-start(bf16[1024,1024]{1,0:T(8,128)(2,1)} %pad_maximum_fusion.mine_ref), channel_id=1, source_target_pairs={{0,64},{64,0},{1,65},{65,1},{2,66},{66,2},{3,67},{67,3},{4,68},{68... | collective-permute-start | bytes 6291464 | tf_op jit(solution)/shard_map/ppermute | solution.py:80
  62.9 28.9 %all-to-all-start.1 = ((bf16[8,128,384]{2,1,0:T(8,128)(2,1)}), bf16[8,128,384]{2,1,0:T(8,128)(2,1)S(1)}, u32[]{:S(2)}, u32[]{:S(2)}) async-start(bf16[8,128,384]{2,1,0:T(8,128)(2,1)} %broadcast_in_dim.8), calls=%async_computation.1 | async-start | bytes 1572864 | tf_op jit(solution)/shard_map/all_to_all | solution.py:85
  91.9 1.3 copy-start
  112.1 21.7 %all-to-all-start.4 = ((bf16[4,1024,128]{2,1,0:T(8,128)(2,1)}), bf16[4,1024,128]{2,1,0:T(8,128)(2,1)}, u32[]{:S(2)}, u32[]{:S(2)}) async-start(bf16[4,1024,128]{2,1,0:T(8,128)(2,1)} %broadcast_in_dim.22), calls=%async_computation.4 | async-start | bytes 2097152 | tf_op jit(solution)/shard_map/all_to_all | solution.py:85
  119.4 26.8 %collective-permute-start.4 = (bf16[8,512,128]{2,1,0:T(8,128)(2,1)}, bf16[8,512,128]{2,1,0:T(8,128)(2,1)S(1)}, u32[]{:S(2)}, u32[]{:S(2)}) collective-permute-start(bf16[8,512,128]{2,1,0:T(8,128)(2,1)} %get-tuple-element.11.own_ref), channel_id=1, source_target_pairs={{0,1},{1,2},{2,3},{3,4},{4,5},{5,6},{6,7},{7,8},{8,9},{9,10},{10,1... | collective-permute-start | bytes 3145736 | tf_op jit(solution)/shard_map/ppermute | solution.py:342
  122.2 26.6 %collective-permute-start.5 = (bf16[8,512,128]{2,1,0:T(8,128)(2,1)}, bf16[8,512,128]{2,1,0:T(8,128)(2,1)S(1)}, u32[]{:S(2)}, u32[]{:S(2)}) collective-permute-start(bf16[8,512,128]{2,1,0:T(8,128)(2,1)} %get-tuple-element.11.own_ref), channel_id=1, source_target_pairs={{1,0},{2,1},{3,2},{4,3},{5,4},{6,5},{7,6},{8,7},{9,8},{10,9},{11,1... | collective-permute-start | bytes 3145736 | tf_op jit(solution)/shard_map/ppermute | solution.py:343
  133.8 42.1 %collective-permute-start.6 = (bf16[4,1024,128]{2,1,0:T(8,128)(2,1)}, bf16[4,1024,128]{2,1,0:T(8,128)(2,1)S(1)}, u32[]{:S(2)}, u32[]{:S(2)}) collective-permute-start(bf16[4,1024,128]{2,1,0:T(8,128)(2,1)} %all-to-all-done.4.mine_ref), channel_id=1, source_target_pairs={{0,64},{64,0},{1,65},{65,1},{2,66},{66,2},{3,67},{67,3},{4,68},{68... | collective-permute-start | bytes 3145736 | tf_op jit(solution)/shard_map/ppermute | solution.py:80

commit v6 on v5

--- a/solution.py
+++ b/solution.py
@@ -16,7 +16,7 @@
 F32 = jnp.float32
 
 
-def norm_kernel(tokens_ref, gain_ref, out_ref):
+def norm(tokens_ref, gain_ref, out_ref):
     widened = tokens_ref[...].astype(F32)
     average = jnp.mean(widened, axis=-1, keepdims=True)
     centred = widened - average
@@ -24,21 +24,17 @@
     out_ref[...] = (centred * lax.rsqrt(spread + 1e-06) * gain_ref[...]).astype(BF16)
 
 
-def layer_norm(tokens, norm_gain):
-    return pl.pallas_call(
-        norm_kernel,
-        grid=(2,),
-        in_specs=[
-            pl.BlockSpec((128, 1024), lambda i: (i, 0)),
-            pl.BlockSpec((1, 1024), lambda i: (0, 0)),
-        ],
-        out_specs=pl.BlockSpec((128, 1024), lambda i: (i, 0)),
-        out_shape=jax.ShapeDtypeStruct((256, 1024), BF16),
-        name="layer_norm",
-    )(tokens, norm_gain.reshape(1, 1024))
-
-
-def message_kernel(lists_ref, weight_ref, out_weight_ref, out_ref):
+def prepare_kernel(
+    lists_ref, tokens_ref, gain_ref, weight_ref, out_weight_ref, normed_ref, messages_ref
+):
+    norm(tokens_ref, gain_ref, normed_ref)
+
+    @pl.when(pl.program_id(0) == 0)
+    def _():
+        write_messages(lists_ref, weight_ref, out_weight_ref, messages_ref)
+
+
+def write_messages(lists_ref, weight_ref, out_weight_ref, out_ref):
     region = 2 * lax.axis_index("x") + lax.axis_index("c")
     owner = 8 * lax.axis_index("y") + lax.axis_index("z")
     lanes = lax.broadcasted_iota(jnp.int32, (2, 128), 1)
@@ -62,17 +58,27 @@
             out_ref[head_pair * 8 + z] = message
 
 
-def messages(lists, weight, out_weight):
-    return pl.pallas_call(
-        message_kernel,
+def prepare(lists, tokens, gain, weight, out_weight):
+    return pl.pallas_call(
+        prepare_kernel,
+        grid=(2,),
         in_specs=[
             pl.BlockSpec(memory_space=pltpu.SMEM),
-            pl.BlockSpec(memory_space=pltpu.VMEM),
-            pl.BlockSpec(memory_space=pltpu.VMEM),
-        ],
-        out_shape=jax.ShapeDtypeStruct((64, 2, 640), BF16),
-        name="messages",
-    )(lists, weight, out_weight)
+            pl.BlockSpec((128, 1024), lambda i: (i, 0)),
+            pl.BlockSpec((1, 1024), lambda i: (0, 0)),
+            pl.BlockSpec((2, 3072), lambda i: (0, 0)),
+            pl.BlockSpec((2, 1024), lambda i: (0, 0)),
+        ],
+        out_specs=[
+            pl.BlockSpec((128, 1024), lambda i: (i, 0)),
+            pl.BlockSpec((64, 2, 640), lambda i: (0, 0, 0)),
+        ],
+        out_shape=[
+            jax.ShapeDtypeStruct((256, 1024), BF16),
+            jax.ShapeDtypeStruct((64, 2, 640), BF16),
+        ],
+        name="prepare",
+    )(lists, tokens, gain, weight, out_weight)
 
 
 def shift(value, axis, step):
@@ -151,6 +157,21 @@
         scratch_shapes=[pltpu.VMEM((1024, 384), BF16)],
         name="project_qkv",
     )(mine, other, on_chip(weight))
+
+
+def settle_kernel(in_ref, out_ref):
+    out_ref[...] = in_ref[...]
+
+
+def settle(value):
+    return pl.pallas_call(
+        settle_kernel,
+        grid=(4,),
+        in_specs=[pl.BlockSpec((256, 1024), lambda i: (i, 0))],
+        out_specs=pl.BlockSpec((256, 1024), lambda i: (i, 0)),
+        out_shape=jax.ShapeDtypeStruct((1024, 1024), BF16),
+        name="settle",
+    )(value)
 
 
 def near_places(table, slot, refs):
@@ -277,20 +298,17 @@
     )(table, queries, on_chip(low), on_chip(high), own_total, own_top)
 
 
-def output_kernel(table, mixed_ref, mine_ref, other_ref, voxels_ref, out_ref, turned_ref):
-    @pl.when(pl.program_id(0) == 0)
-    def _():
-        rows = [r * 128 + y * 16 for y in range(8) for r in range(8)]
-        mixed = jnp.concatenate([mixed_ref[row : row + 16, :] for row in rows], axis=0)
-        turned_ref[...] = mixed.T
-
-    weight = jnp.concatenate([mine_ref[0], other_ref[pl.program_id(0)]], axis=1)
-    projected = jnp.dot(turned_ref[...], weight, preferred_element_type=F32)
+def output_kernel(table, mixed_ref, mine_ref, other_ref, voxels_ref, out_ref):
+    rows = [r * 128 + y * 16 for y in range(8) for r in range(8)]
+    mixed = jnp.concatenate([mixed_ref[row : row + 16, :] for row in rows], axis=0).T
     c = table[73]
-    for place, parity in enumerate((c, 1 - c)):
-        cols = pl.ds(pl.multiple_of(parity * 128, 128), 128)
-        part = projected[:, place * 128 : place * 128 + 128]
-        out_ref[:, cols] = (voxels_ref[:, cols].astype(F32) + part).astype(BF16)
+    for chip in range(4):
+        weight = jnp.concatenate([mine_ref[chip], other_ref[chip]], axis=1)
+        projected = jnp.dot(mixed, weight, preferred_element_type=F32)
+        for place, parity in enumerate((c, 1 - c)):
+            cols = pl.ds(pl.multiple_of(chip * 256 + parity * 128, 128), 128)
+            part = projected[:, place * 128 : place * 128 + 128]
+            out_ref[:, cols] = (voxels_ref[:, cols].astype(F32) + part).astype(BF16)
 
 
 def project_out(table, mixed, mine, other, voxels):
@@ -298,15 +316,14 @@
         output_kernel,
         grid_spec=pltpu.PrefetchScalarGridSpec(
             num_scalar_prefetch=1,
-            grid=(4,),
+            grid=(1,),
             in_specs=[
                 pl.BlockSpec(memory_space=pltpu.VMEM),
-                pl.BlockSpec((1, 1024, 128), lambda n, t: (n, 0, 0)),
+                pl.BlockSpec((4, 1024, 128), lambda n, t: (0, 0, 0)),
                 pl.BlockSpec(memory_space=pltpu.VMEM),
-                pl.BlockSpec((256, 256), lambda n, t: (0, n)),
+                pl.BlockSpec((256, 1024), lambda n, t: (0, 0)),
             ],
-            out_specs=pl.BlockSpec((256, 256), lambda n, t: (0, n)),
-            scratch_shapes=[pltpu.VMEM((256, 1024), BF16)],
+            out_specs=pl.BlockSpec((256, 1024), lambda n, t: (0, 0)),
         ),
         out_shape=jax.ShapeDtypeStruct((256, 1024), BF16),
         name="project_out",
@@ -324,10 +341,12 @@
 def layer(voxels, norm_gain, qkv_weight, out_weight, neighbours):
     x, c, z = (lax.axis_index(a) for a in ("x", "c", "z"))
     tokens = voxels.reshape(256, 1024)
-    normed = layer_norm(tokens, norm_gain)
+    normed, parts = prepare(
+        neighbours.reshape(1, 8), tokens, norm_gain.reshape(1, 1024), qkv_weight, out_weight
+    )
     mine, other = gathered_line(normed)
-
-    parts = messages(neighbours.reshape(1, 8), qkv_weight, out_weight)
+    other = settle(other)
+
     swapped = lax.all_to_all(parts, ("x", "c", "z"), 0, 0, tiled=True)
     masks = lax.dynamic_index_in_dim(swapped.reshape(8, 8, 2, 640), z, 1, keepdims=False)
     table = jnp.concatenate([

time: 182 us -> 178 us (0.978)
  waiting for transfers between devices: 53.1 us -> 44.2 us
  local copies, waits for them, and re-layouts: 3.6 us -> 8.07 us
  other arithmetic: 3.21 us -> 0.59 us
    all_to_all x2, waiting for transfers between devices: 32.4 us -> 27.2 us  [from_everyone(): lax.all_to_all(jnp.broadcast_to(value[None], (n, *value.shape)), axes, 0,...]
    ppermute x5, waiting for transfers between devices: 18.2 us -> 14.3 us  [shift(): return lax.ppermute(value, axis, [(i, (i + step) % n) for i in range(n)])]
    unnamed x2 -> x9, local copies, waits for them, and re-layouts: 1.31 us -> 4.92 us
    concatenate x1 -> x0, other arithmetic: 2.54 us -> none  [gathered_line(): mine = jnp.concatenate(pieces, axis=0)]
    pallas_call x2, Pallas kernels: 3.67 us -> 6.18 us  [the longest x1 3.81 us: settle(): pl.pallas_call(settle_kernel, grid=(4,), in_specs=[pl.BlockSpec((256, 102...]
  transfers between devices with their start and end apart: 9 -> 9, of which waited for: 6 -> 5; matrix products, arithmetic and copies ran while one was open for 1% -> 3% of each run, Pallas kernels for 12% -> 13%
where the time goes in v6:
time: 178 us
  blocking collectives  50.5 us (28%)
  waiting for transfers between devices  44.2 us (25%)
  starting transfers between devices  38.5 us (22%)
  Pallas kernels  35.6 us (20%)
  local copies, waits for them, and re-layouts  8.07 us (5%)
    all_to_all x2, waiting for transfers between devices, from_everyone(): lax.all_to_all(jnp.broadcast_to(value[None], (n, *value.shape)), axes, 0,...  27.2 us
    all_to_all x1, blocking collectives, layer(): swapped = lax.all_to_all(parts, ('x', 'c', 'z'), 0, 0, tiled=True)  23.5 us
    ppermute x5, starting transfers between devices, shift(): return lax.ppermute(value, axis, [(i, (i + step) % n) for i in range(n)])  20.2 us
    all_to_all x1, blocking collectives, layer(): mixed = lax.all_to_all(mixed, LINE, 0, 0, tiled=True).reshape(1024, 256)  15.3 us
    ppermute x5, waiting for transfers between devices, shift(): return lax.ppermute(value, axis, [(i, (i + step) % n) for i in range(n)])  14.3 us
    all_to_all x2, starting transfers between devices, from_everyone(): lax.all_to_all(jnp.broadcast_to(value[None], (n, *value.shape)), axes, 0,...  14.1 us
    pallas_call x1, Pallas kernels, attend(): pl.pallas_call(attend_kernel, grid_spec=pltpu.PrefetchScalarGridSpec(num_...  11.7 us
    all_to_all x1, blocking collectives, from_everyone(): lax.all_to_all(jnp.broadcast_to(value[None], (n, *value.shape)), axes, 0,...  11.6 us
  transfers between devices with their start and end apart: 9, of which 5 were waited for; matrix products, arithmetic and copies ran while one was open for 3% of the time, Pallas kernels for 13%

profile of v6, /device:TPU:1, one launch (start us, length us, event | category | flops | bytes accessed | tf_op | source)
XLA Modules:
  0.0 177.6 jit_solution(1428883079018539220)
XLA Ops:
  0.0 2.4 %prepare.1 = (bf16[256,1024]{1,0:T(8,128)(2,1)}, bf16[64,2,640]{2,1,0:T(2,128)(2,1)}) custom-call(s32[1,8]{1,0:T(1,128)} %bitcast.21, bf16[256,1024]{1,0:T(8,128)(2,1)} %bitcast.15, f32[1,1024]{1,0:T(1,128)} %bitcast.20, bf16[2,3072]{1,0:T(2,128)(2,1)} %weight_ref.1, bf16[2,1024]{1,0:T(2,128)(2,1)} %out_weight_ref.1), custom_call_target="tpu_custom_call" | custom-call | tf_op jit(solution)/shard_map/prepare/pallas_call | solution.py:62
  2.4 4.1 %collective-permute-start = (bf16[256,1024]{1,0:T(8,128)(2,1)}, bf16[256,1024]{1,0:T(8,128)(2,1)S(1)}, u32[]{:S(2)}, u32[]{:S(2)}) collective-permute-start(bf16[256,1024]{1,0:T(8,128)(2,1)} %get-tuple-element.13), channel_id=1, source_target_pairs={{0,128},{128,256},{256,384},{384,0},{1,129},{129,257},{257,385},{3... | collective-permute-start | bytes 1572872 | tf_op jit(solution)/shard_map/ppermute | solution.py:86
  6.4 3.2 %collective-permute-start.1 = (bf16[256,1024]{1,0:T(8,128)(2,1)}, bf16[256,1024]{1,0:T(8,128)(2,1)S(1)}, u32[]{:S(2)}, u32[]{:S(2)}) collective-permute-start(bf16[256,1024]{1,0:T(8,128)(2,1)} %get-tuple-element.13), channel_id=1, source_target_pairs={{0,384},{128,0},{256,128},{384,256},{1,385},{129,1},{257,129},{385... | collective-permute-start | bytes 1572872 | tf_op jit(solution)/shard_map/ppermute | solution.py:86
  9.6 3.6 %collective-permute-start.2 = (bf16[256,1024]{1,0:T(8,128)(2,1)}, bf16[256,1024]{1,0:T(8,128)(2,1)S(1)}, u32[]{:S(2)}, u32[]{:S(2)}) collective-permute-start(bf16[256,1024]{1,0:T(8,128)(2,1)} %get-tuple-element.13), channel_id=1, source_target_pairs={{0,256},{128,384},{256,0},{384,128},{1,257},{129,385},{257,1},{385... | collective-permute-start | bytes 1572872 | tf_op jit(solution)/shard_map/ppermute | solution.py:86
  13.3 1.9 %constant_dynamic-update-slice_fusion.3 = bf16[1024,1024]{1,0:T(8,128)(2,1)} fusion(bf16[256,1024]{1,0:T(8,128)(2,1)} %get-tuple-element.13), kind=kLoop, calls=%fused_computation.4 | loop fusion | bytes 1048576
  18.0 13.1 %collective-permute-done.2 = bf16[256,1024]{1,0:T(8,128)(2,1)S(1)} collective-permute-done((bf16[256,1024]{1,0:T(8,128)(2,1)}, bf16[256,1024]{1,0:T(8,128)(2,1)S(1)}, u32[]{:S(2)}, u32[]{:S(2)}) %collective-permute-start.2) | collective-permute-done | bytes 524320 | tf_op jit(solution)/shard_map/ppermute | solution.py:86
  32.0 5.7 %collective-permute-start.3 = (bf16[1024,1024]{1,0:T(8,128)(2,1)}, bf16[1024,1024]{1,0:T(8,128)(2,1)S(1)}, u32[]{:S(2)}, u32[]{:S(2)}) collective-permute-start(bf16[1024,1024]{1,0:T(8,128)(2,1)} %constant_dynamic-update-slice_fusion.mine_ref), channel_id=1, source_target_pairs={{0,64},{64,0},{1,65},{65,1},{2,66},{66,2},{3,67},{67,3},{4,68},{68... | collective-permute-start | bytes 6291464 | tf_op jit(solution)/shard_map/ppermute | solution.py:86
  37.7 23.5 %all_to_all.25 = bf16[64,2,640]{2,1,0:T(2,128)(2,1)S(1)} all-to-all(bf16[64,2,640]{2,1,0:T(2,128)(2,1)S(1)} %copy-done.2), channel_id=1, replica_groups=mesh['x'=4,'c'=2,'y'=8,'z'=8] {'x','c','z'}, dimensions={0} | all-to-all | bytes 327680 | tf_op jit(solution)/shard_map/all_to_all | solution.py:350
  62.3 6.8 %all-to-all-start.1 = ((bf16[8,128,384]{2,1,0:T(8,128)(2,1)}), bf16[8,128,384]{2,1,0:T(8,128)(2,1)S(1)}, u32[]{:S(2)}, u32[]{:S(2)}) async-start(bf16[8,128,384]{2,1,0:T(8,128)(2,1)} %broadcast_in_dim.8), calls=%async_computation.1 | async-start | bytes 1572864 | tf_op jit(solution)/shard_map/all_to_all | solution.py:91
  69.1 1.4 copy-done
  70.5 3.8 %settle.1.other_ref = bf16[1024,1024]{1,0:T(8,128)(2,1)} custom-call(bf16[1024,1024]{1,0:T(8,128)(2,1)} %copy-done), custom_call_target="tpu_custom_call" | custom-call | tf_op jit(solution)/shard_map/settle/pallas_call | solution.py:167
  74.3 16.9 %all-to-all-done.1.gathered_ref = bf16[8,128,384]{2,1,0:T(8,128)(2,1)S(1)} async-done(((bf16[8,128,384]{2,1,0:T(8,128)(2,1)}), bf16[8,128,384]{2,1,0:T(8,128)(2,1)S(1)}, u32[]{:S(2)}, u32[]{:S(2)}) %all-to-all-start.1) | async-done | bytes 786464 | tf_op jit(solution)/shard_map/all_to_all | solution.py:91
  91.3 6.1 %project_qkv.1 = (bf16[8,512,128]{2,1,0:T(8,128)(2,1)}, bf16[8,256,128]{2,1,0:T(8,128)(2,1)}) custom-call(bf16[1024,1024]{1,0:T(8,128)(2,1)} %constant_dynamic-update-slice_fusion.mine_ref, bf16[1024,1024]{1,0:T(8,128)(2,1)} %settle.1.other_ref, bf16[8,128,384]{2,1,0:T(8,128)(2,1)S(1)} %all-to-all-done.1.gathered_ref), custom_call_target="tpu_custom_call" | custom-call | tf_op jit(solution)/shard_map/project_qkv/pallas_call | solution.py:141
  97.4 11.6 %all_to_all.26 = bf16[8,128,128]{2,1,0:T(8,128)(2,1)S(1)} all-to-all(bf16[8,128,128]{2,1,0:T(8,128)(2,1)S(1)} %broadcast_in_dim.9), channel_id=1, replica_groups=mesh['x'=4,'c'=2,'y'=8,'z'=8] {'y'}, dimensions={0} | all-to-all | bytes 524288 | tf_op jit(solution)/shard_map/all_to_all | solution.py:91
  110.2 7.3 %all-to-all-start.4 = ((bf16[4,1024,128]{2,1,0:T(8,128)(2,1)}), bf16[4,1024,128]{2,1,0:T(8,128)(2,1)}, u32[]{:S(2)}, u32[]{:S(2)}) async-start(bf16[4,1024,128]{2,1,0:T(8,128)(2,1)} %broadcast_in_dim.22), calls=%async_computation.4 | async-start | bytes 2097152 | tf_op jit(solution)/shard_map/all_to_all | solution.py:91
  117.5 2.8 %collective-permute-start.4 = (bf16[8,512,128]{2,1,0:T(8,128)(2,1)}, bf16[8,512,128]{2,1,0:T(8,128)(2,1)S(1)}, u32[]{:S(2)}, u32[]{:S(2)}) collective-permute-start(bf16[8,512,128]{2,1,0:T(8,128)(2,1)} %get-tuple-element.15.own_ref), channel_id=1, source_target_pairs={{0,1},{1,2},{2,3},{3,4},{4,5},{5,6},{6,7},{7,8},{8,9},{9,10},{10,1... | collective-permute-start | bytes 3145736 | tf_op jit(solution)/shard_map/ppermute | solution.py:361
  120.3 1.3 collective-permute-start.5
  121.6 10.3 %all-to-all-done.4.mine_ref = bf16[4,1024,128]{2,1,0:T(8,128)(2,1)} async-done(((bf16[4,1024,128]{2,1,0:T(8,128)(2,1)}), bf16[4,1024,128]{2,1,0:T(8,128)(2,1)}, u32[]{:S(2)}, u32[]{:S(2)}) %all-to-all-start.4) | async-done | bytes 1048608 | tf_op jit(solution)/shard_map/all_to_all | solution.py:91
  131.9 3.7 %collective-permute-start.6 = (bf16[4,1024,128]{2,1,0:T(8,128)(2,1)}, bf16[4,1024,128]{2,1,0:T(8,128)(2,1)S(1)}, u32[]{:S(2)}, u32[]{:S(2)}) collective-permute-start(bf16[4,1024,128]{2,1,0:T(8,128)(2,1)} %all-to-all-done.4.mine_ref), channel_id=1, source_target_pairs={{0,64},{64,0},{1,65},{65,1},{2,66},{66,2},{3,67},{67,3},{4,68},{68... | collective-permute-start | bytes 3145736 | tf_op jit(solution)/shard_map/ppermute | solution.py:86
  136.3 8.0 %attend_own.1 = (f32[8,2,80,256]{3,2,1,0:T(8,128)}, f32[8,2,8,256]{3,2,1,0:T(8,128)}) custom-call(s32[74]{0:T(128)} %pad_add_fusion.table, bf16[8,256,128]{2,1,0:T(8,128)(2,1)} %get-tuple-element.14.query_ref, bf16[8,512,128]{2,1,0:T(8,128)(2,1)} %get-tuple-element.15.own_ref), custom_call_target="tpu_custom_call" | custom-call | tf_op jit(solution)/shard_map/attend_own/pallas_call | solution.py:246
  144.2 2.7 %collective-permute-done.5.high_ref = bf16[8,512,128]{2,1,0:T(8,128)(2,1)S(1)} collective-permute-done((bf16[8,512,128]{2,1,0:T(8,128)(2,1)}, bf16[8,512,128]{2,1,0:T(8,128)(2,1)S(1)}, u32[]{:S(2)}, u32[]{:S(2)}) %collective-permute-start.5) | collective-permute-done | bytes 1048608 | tf_op jit(solution)/shard_map/ppermute | solution.py:362
  146.9 11.7 %attend.1 = bf16[8,128,256]{2,1,0:T(8,128)(2,1)} custom-call(s32[74]{0:T(128)} %pad_add_fusion.table, bf16[8,256,128]{2,1,0:T(8,128)(2,1)} %get-tuple-element.14.query_ref, bf16[8,512,128]{2,1,0:T(8,128)(2,1)S(1)} %collective-permute-done.4.low_ref, bf16[8,512,128]{2,1,0:T(8,128)(2,1)S(1)} %collective-permute-done.5.high_ref, ...), custom_call_target="tpu_custom_call" | custom-call | tf_op jit(solution)/shard_map/attend/pallas_call | solution.py:281
  158.6 15.3 %all_to_all.27 = bf16[8,128,256]{2,1,0:T(8,128)(2,1)S(1)} all-to-all(bf16[8,128,256]{2,1,0:T(8,128)(2,1)} %attend.1), channel_id=1, replica_groups=mesh['x'=4,'c'=2,'y'=8,'z'=8] {'x','c'}, dimensions={0} | all-to-all | bytes 1048576 | tf_op jit(solution)/shard_map/all_to_all | solution.py:370
  173.9 3.7 %project_out.1 = bf16[256,1024]{1,0:T(8,128)(2,1)} custom-call(s32[74]{0:T(128)} %pad_add_fusion.table, bf16[1024,256]{1,0:T(8,128)(2,1)S(1)} %bitcast.14, bf16[4,1024,128]{2,1,0:T(8,128)(2,1)} %all-to-all-done.4.mine_ref, bf16[4,1024,128]{2,1,0:T(8,128)(2,1)S(1)} %collective-permute-done.6.other_ref, bf16[256,1024]{1,0:T(8,128)(2,1)} %bitcast.16), custom_call_target="tpu_custom_call" | custom-call | tf_op jit(solution)/shard_map/project_out/pallas_call | solution.py:315
  (25 shorter events, 6.6 us)
Async XLA Ops:
  2.4 35.3 %copy-start.2 = (bf16[64,2,640]{2,1,0:T(2,128)(2,1)S(1)}, bf16[64,2,640]{2,1,0:T(2,128)(2,1)}, u32[]{:S(2)}) copy-start(bf16[64,2,640]{2,1,0:T(2,128)(2,1)} %get-tuple-element.12) | copy-start | bytes 491524
  2.4 12.8 %collective-permute-start = (bf16[256,1024]{1,0:T(8,128)(2,1)}, bf16[256,1024]{1,0:T(8,128)(2,1)S(1)}, u32[]{:S(2)}, u32[]{:S(2)}) collective-permute-start(bf16[256,1024]{1,0:T(8,128)(2,1)} %get-tuple-element.13), channel_id=1, source_target_pairs={{0,128},{128,256},{256,384},{384,0},{1,129},{129,257},{257,385},{3... | collective-permute-start | bytes 1572872 | tf_op jit(solution)/shard_map/ppermute | solution.py:86
  6.4 10.8 %collective-permute-start.1 = (bf16[256,1024]{1,0:T(8,128)(2,1)}, bf16[256,1024]{1,0:T(8,128)(2,1)S(1)}, u32[]{:S(2)}, u32[]{:S(2)}) collective-permute-start(bf16[256,1024]{1,0:T(8,128)(2,1)} %get-tuple-element.13), channel_id=1, source_target_pairs={{0,384},{128,0},{256,128},{384,256},{1,385},{129,1},{257,129},{385... | collective-permute-start | bytes 1572872 | tf_op jit(solution)/shard_map/ppermute | solution.py:86
  9.6 21.5 %collective-permute-start.2 = (bf16[256,1024]{1,0:T(8,128)(2,1)}, bf16[256,1024]{1,0:T(8,128)(2,1)S(1)}, u32[]{:S(2)}, u32[]{:S(2)}) collective-permute-start(bf16[256,1024]{1,0:T(8,128)(2,1)} %get-tuple-element.13), channel_id=1, source_target_pairs={{0,256},{128,384},{256,0},{384,128},{1,257},{129,385},{257,1},{385... | collective-permute-start | bytes 1572872 | tf_op jit(solution)/shard_map/ppermute | solution.py:86
  32.0 37.1 %collective-permute-start.3 = (bf16[1024,1024]{1,0:T(8,128)(2,1)}, bf16[1024,1024]{1,0:T(8,128)(2,1)S(1)}, u32[]{:S(2)}, u32[]{:S(2)}) collective-permute-start(bf16[1024,1024]{1,0:T(8,128)(2,1)} %constant_dynamic-update-slice_fusion.mine_ref), channel_id=1, source_target_pairs={{0,64},{64,0},{1,65},{65,1},{2,66},{66,2},{3,67},{67,3},{4,68},{68... | collective-permute-start | bytes 6291464 | tf_op jit(solution)/shard_map/ppermute | solution.py:86
  61.3 13.0 %copy-start.1 = (bf16[128,640]{1,0:T(8,128)(2,1)}, bf16[128,640]{1,0:T(8,128)(2,1)S(1)}, u32[]{:S(2)}) copy-start(bf16[128,640]{1,0:T(8,128)(2,1)S(1)} %reshape.32) | copy-start | bytes 491524
  62.3 28.9 %all-to-all-start.1 = ((bf16[8,128,384]{2,1,0:T(8,128)(2,1)}), bf16[8,128,384]{2,1,0:T(8,128)(2,1)S(1)}, u32[]{:S(2)}, u32[]{:S(2)}) async-start(bf16[8,128,384]{2,1,0:T(8,128)(2,1)} %broadcast_in_dim.8), calls=%async_computation.1 | async-start | bytes 1572864 | tf_op jit(solution)/shard_map/all_to_all | solution.py:91
  69.1 1.4 copy-start
  91.3 6.1 %slice-start = ((bf16[128,640]{1,0:T(8,128)(2,1)}), bf16[128,128]{1,0:T(8,128)(2,1)S(1)}, s32[]{:S(2)}) async-start(bf16[128,640]{1,0:T(8,128)(2,1)} %copy-done.1), calls=%async_computation.5 | async-start | bytes 65536 | tf_op jit(solution)/shard_map/slice | solution.py:364
  110.2 21.7 %all-to-all-start.4 = ((bf16[4,1024,128]{2,1,0:T(8,128)(2,1)}), bf16[4,1024,128]{2,1,0:T(8,128)(2,1)}, u32[]{:S(2)}, u32[]{:S(2)}) async-start(bf16[4,1024,128]{2,1,0:T(8,128)(2,1)} %broadcast_in_dim.22), calls=%async_computation.4 | async-start | bytes 2097152 | tf_op jit(solution)/shard_map/all_to_all | solution.py:91
  117.5 26.8 %collective-permute-start.4 = (bf16[8,512,128]{2,1,0:T(8,128)(2,1)}, bf16[8,512,128]{2,1,0:T(8,128)(2,1)S(1)}, u32[]{:S(2)}, u32[]{:S(2)}) collective-permute-start(bf16[8,512,128]{2,1,0:T(8,128)(2,1)} %get-tuple-element.15.own_ref), channel_id=1, source_target_pairs={{0,1},{1,2},{2,3},{3,4},{4,5},{5,6},{6,7},{7,8},{8,9},{9,10},{10,1... | collective-permute-start | bytes 3145736 | tf_op jit(solution)/shard_map/ppermute | solution.py:361
  120.3 26.6 %collective-permute-start.5 = (bf16[8,512,128]{2,1,0:T(8,128)(2,1)}, bf16[8,512,128]{2,1,0:T(8,128)(2,1)S(1)}, u32[]{:S(2)}, u32[]{:S(2)}) collective-permute-start(bf16[8,512,128]{2,1,0:T(8,128)(2,1)} %get-tuple-element.15.own_ref), channel_id=1, source_target_pairs={{1,0},{2,1},{3,2},{4,3},{5,4},{6,5},{7,6},{8,7},{9,8},{10,9},{11,1... | collective-permute-start | bytes 3145736 | tf_op jit(solution)/shard_map/ppermute | solution.py:362
  131.9 42.0 %collective-permute-start.6 = (bf16[4,1024,128]{2,1,0:T(8,128)(2,1)}, bf16[4,1024,128]{2,1,0:T(8,128)(2,1)S(1)}, u32[]{:S(2)}, u32[]{:S(2)}) collective-permute-start(bf16[4,1024,128]{2,1,0:T(8,128)(2,1)} %all-to-all-done.4.mine_ref), channel_id=1, source_target_pairs={{0,64},{64,0},{1,65},{65,1},{2,66},{66,2},{3,67},{67,3},{4,68},{68... | collective-permute-start | bytes 3145736 | tf_op jit(solution)/shard_map/ppermute | solution.py:86

commit v7 on v6

--- a/solution.py
+++ b/solution.py
@@ -130,7 +130,7 @@
 
     @pl.when(pl.program_id(0) < 2)
     def _():
-        project(mine_ref[...])
+        project(mine_ref[pl.ds(pl.multiple_of(pl.program_id(0) * 512, 512), 512), :])
 
     @pl.when(pl.program_id(0) >= 2)
     def _():
@@ -142,7 +142,7 @@
         qkv_kernel,
         grid=(4,),
         in_specs=[
-            pl.BlockSpec((512, 1024), lambda s: (jnp.minimum(s, 1), 0)),
+            pl.BlockSpec(memory_space=pltpu.VMEM),
             pl.BlockSpec((512, 1024), lambda s: (jnp.maximum(s - 2, 0), 0)),
             pl.BlockSpec(memory_space=pltpu.VMEM),
         ],
@@ -156,22 +156,7 @@
         ],
         scratch_shapes=[pltpu.VMEM((1024, 384), BF16)],
         name="project_qkv",
-    )(mine, other, on_chip(weight))
-
-
-def settle_kernel(in_ref, out_ref):
-    out_ref[...] = in_ref[...]
-
-
-def settle(value):
-    return pl.pallas_call(
-        settle_kernel,
-        grid=(4,),
-        in_specs=[pl.BlockSpec((256, 1024), lambda i: (i, 0))],
-        out_specs=pl.BlockSpec((256, 1024), lambda i: (i, 0)),
-        out_shape=jax.ShapeDtypeStruct((1024, 1024), BF16),
-        name="settle",
-    )(value)
+    )(on_chip(mine), other, on_chip(weight))
 
 
 def near_places(table, slot, refs):
@@ -189,8 +174,8 @@
 def run_units(table, query_ref, refs, score_ref, weight_ref, known_top, finish):
     lanes = lax.broadcasted_iota(jnp.int32, (256, 128), 1)
     units = []
-    for place in range(2):
-        places = near_places(table, pl.program_id(0) * 2 + place, refs)
+    for place in range(4):
+        places = near_places(table, pl.program_id(0) * 4 + place, refs)
         for head in range(2):
             inside = (lanes >= head * 64) & (lanes < head * 64 + 64)
             query = jnp.where(inside, query_ref[place], jnp.zeros((), BF16))
@@ -198,11 +183,11 @@
     count = len(units[0][2])
     ones = jnp.ones((16, count * 256), BF16)
     tops = []
-    for turn in range(5):
+    for turn in range(9):
         column_tops = []
         for entry in range(count):
             rows = slice(entry * 256, entry * 256 + 256)
-            if turn < 4:
+            if turn < 8:
                 _, _, places, query = units[turn]
                 ref, slot, penalty = places[entry]
                 scores = lax.dot_general(
@@ -225,7 +210,7 @@
             values = jnp.concatenate([jnp.concatenate(halves, axis=1), ones], axis=0)
             total = jnp.dot(values, weight_ref[(turn - 1) % 2], preferred_element_type=F32)
             finish(place, head, tops[-1], total)
-        if turn < 4:
+        if turn < 8:
             top = functools.reduce(jnp.maximum, column_tops)
             if known_top is not None:
                 top = jnp.maximum(top, known_top(*units[turn][:2]))
@@ -247,11 +232,11 @@
         attend_own_kernel,
         grid_spec=pltpu.PrefetchScalarGridSpec(
             num_scalar_prefetch=1,
-            grid=(4,),
-            in_specs=[pl.BlockSpec((2, 256, 128), lambda s, t: (s, 0, 0)), WHOLE],
+            grid=(2,),
+            in_specs=[pl.BlockSpec((4, 256, 128), lambda s, t: (s, 0, 0)), WHOLE],
             out_specs=[
-                pl.BlockSpec((2, 2, 80, 256), lambda s, t: (s, 0, 0, 0)),
-                pl.BlockSpec((2, 2, 8, 256), lambda s, t: (s, 0, 0, 0)),
+                pl.BlockSpec((4, 2, 80, 256), lambda s, t: (s, 0, 0, 0)),
+                pl.BlockSpec((4, 2, 8, 256), lambda s, t: (s, 0, 0, 0)),
             ],
             scratch_shapes=[pltpu.VMEM((2, 768, 256), F32), pltpu.VMEM((2, 768, 256), BF16)],
         ),
@@ -271,7 +256,7 @@
 
     def finish(place, head, top, total):
         total += own_total_ref[place, head] * jnp.exp2(known_top(place, head) - top)
-        region = region_of(pl.program_id(0) * 2 + place, table[72], table[73])
+        region = region_of(pl.program_id(0) * 4 + place, table[72], table[73])
         out_ref[region, head * 64 : head * 64 + 64, :] = (total[:64] / total[64:65]).astype(BF16)
 
     run_units(table, query_ref, [(0, low_ref), (2, high_ref)], score_ref, weight_ref, known_top, finish)
@@ -282,13 +267,13 @@
         attend_kernel,
         grid_spec=pltpu.PrefetchScalarGridSpec(
             num_scalar_prefetch=1,
-            grid=(4,),
+            grid=(2,),
             in_specs=[
-                pl.BlockSpec((2, 256, 128), lambda s, t: (s, 0, 0)),
+                pl.BlockSpec((4, 256, 128), lambda s, t: (s, 0, 0)),
                 WHOLE,
                 WHOLE,
-                pl.BlockSpec((2, 2, 80, 256), lambda s, t: (s, 0, 0, 0)),
-                pl.BlockSpec((2, 2, 8, 256), lambda s, t: (s, 0, 0, 0)),
+                pl.BlockSpec((4, 2, 80, 256), lambda s, t: (s, 0, 0, 0)),
+                pl.BlockSpec((4, 2, 8, 256), lambda s, t: (s, 0, 0, 0)),
             ],
             out_specs=pl.BlockSpec((8, 128, 256), lambda s, t: (0, 0, 0)),
             scratch_shapes=[pltpu.VMEM((2, 1536, 256), F32), pltpu.VMEM((2, 1536, 256), BF16)],
@@ -345,7 +330,6 @@
         neighbours.reshape(1, 8), tokens, norm_gain.reshape(1, 1024), qkv_weight, out_weight
     )
     mine, other = gathered_line(normed)
-    other = settle(other)
 
     swapped = lax.all_to_all(parts, ("x", "c", "z"), 0, 0, tiled=True)
     masks = lax.dynamic_index_in_dim(swapped.reshape(8, 8, 2, 640), z, 1, keepdims=False)

time: 178 us -> 176 us (0.989)
  waiting for transfers between devices: 44.2 us -> 52.2 us
  Pallas kernels: 35.6 us -> 30.4 us
  local copies, waits for them, and re-layouts: 8.07 us -> 3.51 us
    all_to_all x2, waiting for transfers between devices: 27.2 us -> 32.4 us  [from_everyone(): lax.all_to_all(jnp.broadcast_to(value[None], (n, *value.shape)), axes, 0,...]
    pallas_call x2 -> x1, Pallas kernels: 9.9 us -> 5.75 us  [project_qkv(): pl.pallas_call(qkv_kernel, grid=(4,), in_specs=[pl.BlockSpec(memory_space...]
    unnamed x9 -> x5, local copies, waits for them, and re-layouts: 4.92 us -> 1.16 us
    ppermute x5, waiting for transfers between devices: 14.3 us -> 16.7 us  [shift(): return lax.ppermute(value, axis, [(i, (i + step) % n) for i in range(n)])]
  transfers between devices with their start and end apart: 9 -> 9, of which waited for: 5 -> 6; matrix products, arithmetic and copies ran while one was open for 3% -> 2% of each run, Pallas kernels for 13% -> 11%
where the time goes in v7:
time: 176 us; the launch traced here: 175 us
  waiting for transfers between devices  52.2 us (30%)
  blocking collectives  50.5 us (29%)
  starting transfers between devices  37.7 us (21%)
  Pallas kernels  30.4 us (17%)
  local copies, waits for them, and re-layouts  3.51 us (2%)
    all_to_all x2, waiting for transfers between devices, from_everyone(): lax.all_to_all(jnp.broadcast_to(value[None], (n, *value.shape)), axes, 0,...  32.4 us
    all_to_all x1, blocking collectives, layer(): swapped = lax.all_to_all(parts, ('x', 'c', 'z'), 0, 0, tiled=True)  23.5 us
    ppermute x5, starting transfers between devices, shift(): return lax.ppermute(value, axis, [(i, (i + step) % n) for i in range(n)])  19.5 us
    ppermute x5, waiting for transfers between devices, shift(): return lax.ppermute(value, axis, [(i, (i + step) % n) for i in range(n)])  16.7 us
    all_to_all x1, blocking collectives, layer(): mixed = lax.all_to_all(mixed, LINE, 0, 0, tiled=True).reshape(1024, 256)  15.3 us
    all_to_all x2, starting transfers between devices, from_everyone(): lax.all_to_all(jnp.broadcast_to(value[None], (n, *value.shape)), axes, 0,...  14.1 us
    all_to_all x1, blocking collectives, from_everyone(): lax.all_to_all(jnp.broadcast_to(value[None], (n, *value.shape)), axes, 0,...  11.6 us
    pallas_call x1, Pallas kernels, attend(): pl.pallas_call(attend_kernel, grid_spec=pltpu.PrefetchScalarGridSpec(num_...  11 us
  transfers between devices with their start and end apart: 9, of which 6 were waited for; matrix products, arithmetic and copies ran while one was open for 2% of the time, Pallas kernels for 11%

profile of v7, /device:TPU:1, one launch (start us, length us, event | category | flops | bytes accessed | tf_op | source)
XLA Modules:
  0.0 175.1 jit_solution(3387664655572814990)
XLA Ops:
  0.0 2.4 %prepare.1 = (bf16[256,1024]{1,0:T(8,128)(2,1)}, bf16[64,2,640]{2,1,0:T(2,128)(2,1)}) custom-call(s32[1,8]{1,0:T(1,128)} %bitcast.21, bf16[256,1024]{1,0:T(8,128)(2,1)} %bitcast.15, f32[1,1024]{1,0:T(1,128)} %bitcast.20, bf16[2,3072]{1,0:T(2,128)(2,1)} %weight_ref.1, bf16[2,1024]{1,0:T(2,128)(2,1)} %out_weight_ref.1), custom_call_target="tpu_custom_call" | custom-call | tf_op jit(solution)/shard_map/prepare/pallas_call | solution.py:62
  2.4 4.1 %collective-permute-start = (bf16[256,1024]{1,0:T(8,128)(2,1)}, bf16[256,1024]{1,0:T(8,128)(2,1)S(1)}, u32[]{:S(2)}, u32[]{:S(2)}) collective-permute-start(bf16[256,1024]{1,0:T(8,128)(2,1)} %get-tuple-element.13), channel_id=1, source_target_pairs={{0,128},{128,256},{256,384},{384,0},{1,129},{129,257},{257,385},{3... | collective-permute-start | bytes 1572872 | tf_op jit(solution)/shard_map/ppermute | solution.py:86
  6.4 3.2 %collective-permute-start.1 = (bf16[256,1024]{1,0:T(8,128)(2,1)}, bf16[256,1024]{1,0:T(8,128)(2,1)S(1)}, u32[]{:S(2)}, u32[]{:S(2)}) collective-permute-start(bf16[256,1024]{1,0:T(8,128)(2,1)} %get-tuple-element.13), channel_id=1, source_target_pairs={{0,384},{128,0},{256,128},{384,256},{1,385},{129,1},{257,129},{385... | collective-permute-start | bytes 1572872 | tf_op jit(solution)/shard_map/ppermute | solution.py:86
  9.6 3.6 %collective-permute-start.2 = (bf16[256,1024]{1,0:T(8,128)(2,1)}, bf16[256,1024]{1,0:T(8,128)(2,1)S(1)}, u32[]{:S(2)}, u32[]{:S(2)}) collective-permute-start(bf16[256,1024]{1,0:T(8,128)(2,1)} %get-tuple-element.13), channel_id=1, source_target_pairs={{0,256},{128,384},{256,0},{384,128},{1,257},{129,385},{257,1},{385... | collective-permute-start | bytes 1572872 | tf_op jit(solution)/shard_map/ppermute | solution.py:86
  13.3 1.1 constant_dynamic-update-slice_fusion.3
  14.5 2.7 %collective-permute-done.1 = bf16[256,1024]{1,0:T(8,128)(2,1)S(1)} collective-permute-done((bf16[256,1024]{1,0:T(8,128)(2,1)}, bf16[256,1024]{1,0:T(8,128)(2,1)S(1)}, u32[]{:S(2)}, u32[]{:S(2)}) %collective-permute-start.1) | collective-permute-done | bytes 524320 | tf_op jit(solution)/shard_map/ppermute | solution.py:86
  17.2 13.9 %collective-permute-done.2 = bf16[256,1024]{1,0:T(8,128)(2,1)S(1)} collective-permute-done((bf16[256,1024]{1,0:T(8,128)(2,1)}, bf16[256,1024]{1,0:T(8,128)(2,1)S(1)}, u32[]{:S(2)}, u32[]{:S(2)}) %collective-permute-start.2) | collective-permute-done | bytes 524320 | tf_op jit(solution)/shard_map/ppermute | solution.py:86
  31.2 4.9 %collective-permute-start.3 = (bf16[1024,1024]{1,0:T(8,128)(2,1)S(1)}, bf16[1024,1024]{1,0:T(8,128)(2,1)}, u32[]{:S(2)}, u32[]{:S(2)}) collective-permute-start(bf16[1024,1024]{1,0:T(8,128)(2,1)S(1)} %constant_dynamic-update-slice_fusion.mine_ref), channel_id=1, source_target_pairs={{0,64},{64,0},{1,65},{65,1},{2,66},{66,2},{3,67},{67,3},{4,68},{68... | collective-permute-start | bytes 6291464 | tf_op jit(solution)/shard_map/ppermute | solution.py:86
  36.1 23.5 %all_to_all.25 = bf16[64,2,640]{2,1,0:T(2,128)(2,1)S(1)} all-to-all(bf16[64,2,640]{2,1,0:T(2,128)(2,1)S(1)} %copy-done), channel_id=1, replica_groups=mesh['x'=4,'c'=2,'y'=8,'z'=8] {'x','c','z'}, dimensions={0} | all-to-all | bytes 327680 | tf_op jit(solution)/shard_map/all_to_all | solution.py:334
  60.7 6.8 %all-to-all-start.1 = ((bf16[8,128,384]{2,1,0:T(8,128)(2,1)}), bf16[8,128,384]{2,1,0:T(8,128)(2,1)S(1)}, u32[]{:S(2)}, u32[]{:S(2)}) async-start(bf16[8,128,384]{2,1,0:T(8,128)(2,1)} %broadcast_in_dim.8), calls=%async_computation.1 | async-start | bytes 1572864 | tf_op jit(solution)/shard_map/all_to_all | solution.py:91
  67.6 22.1 %all-to-all-done.1.gathered_ref = bf16[8,128,384]{2,1,0:T(8,128)(2,1)S(1)} async-done(((bf16[8,128,384]{2,1,0:T(8,128)(2,1)}), bf16[8,128,384]{2,1,0:T(8,128)(2,1)S(1)}, u32[]{:S(2)}, u32[]{:S(2)}) %all-to-all-start.1) | async-done | bytes 786464 | tf_op jit(solution)/shard_map/all_to_all | solution.py:91
  89.7 5.8 %project_qkv.1 = (bf16[8,512,128]{2,1,0:T(8,128)(2,1)}, bf16[8,256,128]{2,1,0:T(8,128)(2,1)}) custom-call(bf16[1024,1024]{1,0:T(8,128)(2,1)S(1)} %constant_dynamic-update-slice_fusion.mine_ref, bf16[1024,1024]{1,0:T(8,128)(2,1)} %collective-permute-done.3.other_ref, bf16[8,128,384]{2,1,0:T(8,128)(2,1)S(1)} %all-to-all-done.1.gathered_ref), custom_call_target="tpu_custom_call" | custom-call | tf_op jit(solution)/shard_map/project_qkv/pallas_call | solution.py:141
  95.5 11.6 %all_to_all.26 = bf16[8,128,128]{2,1,0:T(8,128)(2,1)S(1)} all-to-all(bf16[8,128,128]{2,1,0:T(8,128)(2,1)S(1)} %broadcast_in_dim.9), channel_id=1, replica_groups=mesh['x'=4,'c'=2,'y'=8,'z'=8] {'y'}, dimensions={0} | all-to-all | bytes 524288 | tf_op jit(solution)/shard_map/all_to_all | solution.py:91
  107.1 1.1 broadcast_in_dim.22
  108.2 7.3 %all-to-all-start.4 = ((bf16[4,1024,128]{2,1,0:T(8,128)(2,1)}), bf16[4,1024,128]{2,1,0:T(8,128)(2,1)}, u32[]{:S(2)}, u32[]{:S(2)}) async-start(bf16[4,1024,128]{2,1,0:T(8,128)(2,1)} %broadcast_in_dim.22), calls=%async_computation.4 | async-start | bytes 2097152 | tf_op jit(solution)/shard_map/all_to_all | solution.py:91
  115.6 2.8 %collective-permute-start.4 = (bf16[8,512,128]{2,1,0:T(8,128)(2,1)}, bf16[8,512,128]{2,1,0:T(8,128)(2,1)S(1)}, u32[]{:S(2)}, u32[]{:S(2)}) collective-permute-start(bf16[8,512,128]{2,1,0:T(8,128)(2,1)} %get-tuple-element.15.own_ref), channel_id=1, source_target_pairs={{0,1},{1,2},{2,3},{3,4},{4,5},{5,6},{6,7},{7,8},{8,9},{9,10},{10,1... | collective-permute-start | bytes 3145736 | tf_op jit(solution)/shard_map/ppermute | solution.py:345
  118.4 1.3 collective-permute-start.5
  119.7 10.3 %all-to-all-done.4.mine_ref = bf16[4,1024,128]{2,1,0:T(8,128)(2,1)} async-done(((bf16[4,1024,128]{2,1,0:T(8,128)(2,1)}), bf16[4,1024,128]{2,1,0:T(8,128)(2,1)}, u32[]{:S(2)}, u32[]{:S(2)}) %all-to-all-start.4) | async-done | bytes 1048608 | tf_op jit(solution)/shard_map/all_to_all | solution.py:91
  129.9 3.7 %collective-permute-start.6 = (bf16[4,1024,128]{2,1,0:T(8,128)(2,1)}, bf16[4,1024,128]{2,1,0:T(8,128)(2,1)S(1)}, u32[]{:S(2)}, u32[]{:S(2)}) collective-permute-start(bf16[4,1024,128]{2,1,0:T(8,128)(2,1)} %all-to-all-done.4.mine_ref), channel_id=1, source_target_pairs={{0,64},{64,0},{1,65},{65,1},{2,66},{66,2},{3,67},{67,3},{4,68},{68... | collective-permute-start | bytes 3145736 | tf_op jit(solution)/shard_map/ppermute | solution.py:86
  134.3 7.6 %attend_own.1 = (f32[8,2,80,256]{3,2,1,0:T(8,128)}, f32[8,2,8,256]{3,2,1,0:T(8,128)}) custom-call(s32[74]{0:T(128)} %pad_add_fusion.table, bf16[8,256,128]{2,1,0:T(8,128)(2,1)} %get-tuple-element.14.query_ref, bf16[8,512,128]{2,1,0:T(8,128)(2,1)} %get-tuple-element.15.own_ref), custom_call_target="tpu_custom_call" | custom-call | tf_op jit(solution)/shard_map/attend_own/pallas_call | solution.py:231
  141.9 3.1 %collective-permute-done.5.high_ref = bf16[8,512,128]{2,1,0:T(8,128)(2,1)S(1)} collective-permute-done((bf16[8,512,128]{2,1,0:T(8,128)(2,1)}, bf16[8,512,128]{2,1,0:T(8,128)(2,1)S(1)}, u32[]{:S(2)}, u32[]{:S(2)}) %collective-permute-start.5) | collective-permute-done | bytes 1048608 | tf_op jit(solution)/shard_map/ppermute | solution.py:346
  145.0 11.0 %attend.1 = bf16[8,128,256]{2,1,0:T(8,128)(2,1)} custom-call(s32[74]{0:T(128)} %pad_add_fusion.table, bf16[8,256,128]{2,1,0:T(8,128)(2,1)} %get-tuple-element.14.query_ref, bf16[8,512,128]{2,1,0:T(8,128)(2,1)S(1)} %collective-permute-done.4.low_ref, bf16[8,512,128]{2,1,0:T(8,128)(2,1)S(1)} %collective-permute-done.5.high_ref, ...), custom_call_target="tpu_custom_call" | custom-call | tf_op jit(solution)/shard_map/attend/pallas_call | solution.py:266
  156.0 15.3 %all_to_all.27 = bf16[8,128,256]{2,1,0:T(8,128)(2,1)S(1)} all-to-all(bf16[8,128,256]{2,1,0:T(8,128)(2,1)} %attend.1), channel_id=1, replica_groups=mesh['x'=4,'c'=2,'y'=8,'z'=8] {'x','c'}, dimensions={0} | all-to-all | bytes 1048576 | tf_op jit(solution)/shard_map/all_to_all | solution.py:354
  171.3 3.7 %project_out.1 = bf16[256,1024]{1,0:T(8,128)(2,1)} custom-call(s32[74]{0:T(128)} %pad_add_fusion.table, bf16[1024,256]{1,0:T(8,128)(2,1)S(1)} %bitcast.14, bf16[4,1024,128]{2,1,0:T(8,128)(2,1)} %all-to-all-done.4.mine_ref, bf16[4,1024,128]{2,1,0:T(8,128)(2,1)S(1)} %collective-permute-done.6.other_ref, bf16[256,1024]{1,0:T(8,128)(2,1)} %bitcast.16), custom_call_target="tpu_custom_call" | custom-call | tf_op jit(solution)/shard_map/project_out/pallas_call | solution.py:300
  (19 shorter events, 2.0 us)
Async XLA Ops:
  2.4 33.8 %copy-start = (bf16[64,2,640]{2,1,0:T(2,128)(2,1)S(1)}, bf16[64,2,640]{2,1,0:T(2,128)(2,1)}, u32[]{:S(2)}) copy-start(bf16[64,2,640]{2,1,0:T(2,128)(2,1)} %get-tuple-element.12) | copy-start | bytes 491524
  2.4 12.1 %collective-permute-start = (bf16[256,1024]{1,0:T(8,128)(2,1)}, bf16[256,1024]{1,0:T(8,128)(2,1)S(1)}, u32[]{:S(2)}, u32[]{:S(2)}) collective-permute-start(bf16[256,1024]{1,0:T(8,128)(2,1)} %get-tuple-element.13), channel_id=1, source_target_pairs={{0,128},{128,256},{256,384},{384,0},{1,129},{129,257},{257,385},{3... | collective-permute-start | bytes 1572872 | tf_op jit(solution)/shard_map/ppermute | solution.py:86
  6.4 10.8 %collective-permute-start.1 = (bf16[256,1024]{1,0:T(8,128)(2,1)}, bf16[256,1024]{1,0:T(8,128)(2,1)S(1)}, u32[]{:S(2)}, u32[]{:S(2)}) collective-permute-start(bf16[256,1024]{1,0:T(8,128)(2,1)} %get-tuple-element.13), channel_id=1, source_target_pairs={{0,384},{128,0},{256,128},{384,256},{1,385},{129,1},{257,129},{385... | collective-permute-start | bytes 1572872 | tf_op jit(solution)/shard_map/ppermute | solution.py:86
  9.6 21.5 %collective-permute-start.2 = (bf16[256,1024]{1,0:T(8,128)(2,1)}, bf16[256,1024]{1,0:T(8,128)(2,1)S(1)}, u32[]{:S(2)}, u32[]{:S(2)}) collective-permute-start(bf16[256,1024]{1,0:T(8,128)(2,1)} %get-tuple-element.13), channel_id=1, source_target_pairs={{0,256},{128,384},{256,0},{384,128},{1,257},{129,385},{257,1},{385... | collective-permute-start | bytes 1572872 | tf_op jit(solution)/shard_map/ppermute | solution.py:86
  31.2 58.5 %collective-permute-start.3 = (bf16[1024,1024]{1,0:T(8,128)(2,1)S(1)}, bf16[1024,1024]{1,0:T(8,128)(2,1)}, u32[]{:S(2)}, u32[]{:S(2)}) collective-permute-start(bf16[1024,1024]{1,0:T(8,128)(2,1)S(1)} %constant_dynamic-update-slice_fusion.mine_ref), channel_id=1, source_target_pairs={{0,64},{64,0},{1,65},{65,1},{2,66},{66,2},{3,67},{67,3},{4,68},{68... | collective-permute-start | bytes 6291464 | tf_op jit(solution)/shard_map/ppermute | solution.py:86
  60.7 28.9 %all-to-all-start.1 = ((bf16[8,128,384]{2,1,0:T(8,128)(2,1)}), bf16[8,128,384]{2,1,0:T(8,128)(2,1)S(1)}, u32[]{:S(2)}, u32[]{:S(2)}) async-start(bf16[8,128,384]{2,1,0:T(8,128)(2,1)} %broadcast_in_dim.8), calls=%async_computation.1 | async-start | bytes 1572864 | tf_op jit(solution)/shard_map/all_to_all | solution.py:91
  108.2 21.7 %all-to-all-start.4 = ((bf16[4,1024,128]{2,1,0:T(8,128)(2,1)}), bf16[4,1024,128]{2,1,0:T(8,128)(2,1)}, u32[]{:S(2)}, u32[]{:S(2)}) async-start(bf16[4,1024,128]{2,1,0:T(8,128)(2,1)} %broadcast_in_dim.22), calls=%async_computation.4 | async-start | bytes 2097152 | tf_op jit(solution)/shard_map/all_to_all | solution.py:91
  115.6 26.4 %collective-permute-start.4 = (bf16[8,512,128]{2,1,0:T(8,128)(2,1)}, bf16[8,512,128]{2,1,0:T(8,128)(2,1)S(1)}, u32[]{:S(2)}, u32[]{:S(2)}) collective-permute-start(bf16[8,512,128]{2,1,0:T(8,128)(2,1)} %get-tuple-element.15.own_ref), channel_id=1, source_target_pairs={{0,1},{1,2},{2,3},{3,4},{4,5},{5,6},{6,7},{7,8},{8,9},{9,10},{10,1... | collective-permute-start | bytes 3145736 | tf_op jit(solution)/shard_map/ppermute | solution.py:345
  118.4 26.7 %collective-permute-start.5 = (bf16[8,512,128]{2,1,0:T(8,128)(2,1)}, bf16[8,512,128]{2,1,0:T(8,128)(2,1)S(1)}, u32[]{:S(2)}, u32[]{:S(2)}) collective-permute-start(bf16[8,512,128]{2,1,0:T(8,128)(2,1)} %get-tuple-element.15.own_ref), channel_id=1, source_target_pairs={{1,0},{2,1},{3,2},{4,3},{5,4},{6,5},{7,6},{8,7},{9,8},{10,9},{11,1... | collective-permute-start | bytes 3145736 | tf_op jit(solution)/shard_map/ppermute | solution.py:346
  129.9 41.4 %collective-permute-start.6 = (bf16[4,1024,128]{2,1,0:T(8,128)(2,1)}, bf16[4,1024,128]{2,1,0:T(8,128)(2,1)S(1)}, u32[]{:S(2)}, u32[]{:S(2)}) collective-permute-start(bf16[4,1024,128]{2,1,0:T(8,128)(2,1)} %all-to-all-done.4.mine_ref), channel_id=1, source_target_pairs={{0,64},{64,0},{1,65},{65,1},{2,66},{66,2},{3,67},{67,3},{4,68},{68... | collective-permute-start | bytes 3145736 | tf_op jit(solution)/shard_map/ppermute | solution.py:86

commit v8 on v7

--- a/solution.py
+++ b/solution.py
@@ -315,8 +315,9 @@
     )(table, on_chip(mixed), mine, on_chip(other), voxels)
 
 
-def gathered_line(value):
-    pieces = [value]
+def gathered_line(value, after):
+    own, _ = lax.optimization_barrier((value, after))
+    pieces = [own]
     for step in (1, -1, 2):
         pieces.append(shift(value, "x", step))
     mine = jnp.concatenate(pieces, axis=0)
@@ -329,7 +330,6 @@
     normed, parts = prepare(
         neighbours.reshape(1, 8), tokens, norm_gain.reshape(1, 1024), qkv_weight, out_weight
     )
-    mine, other = gathered_line(normed)
 
     swapped = lax.all_to_all(parts, ("x", "c", "z"), 0, 0, tiled=True)
     masks = lax.dynamic_index_in_dim(swapped.reshape(8, 8, 2, 640), z, 1, keepdims=False)
@@ -340,6 +340,7 @@
     swapped = swapped.reshape(128, 640)
 
     weight = from_everyone(swapped[:, :384], "y")
+    mine, other = gathered_line(normed, swapped)
     own, queries = project_qkv(mine, other, weight)
     line = [(i, i + 1) for i in range(63)]
     low = lax.ppermute(own, PLANE, line)

time: 176 us -> 171 us (0.972)
  blocking collectives: 50.5 us -> 30.5 us
  starting transfers between devices: 37.7 us -> 55 us
  waiting for transfers between devices: 52.2 us -> 48.1 us
  local copies, waits for them, and re-layouts: 3.51 us -> 5.63 us
    all_to_all x1 -> x0, blocking collectives: 23.5 us -> none  [layer(): swapped = lax.all_to_all(parts, ('x', 'c', 'z'), 0, 0, tiled=True)]
    all_to_all x0 -> x1, starting transfers between devices: none -> 14 us  [layer(): swapped = lax.all_to_all(parts, ('x', 'c', 'z'), 0, 0, tiled=True)]
    ppermute x5, waiting for transfers between devices: 16.7 us -> 8.68 us  [shift(): return lax.ppermute(value, axis, [(i, (i + step) % n) for i in range(n)])]
    ppermute x5, starting transfers between devices: 19.5 us -> 25.2 us  [shift(): return lax.ppermute(value, axis, [(i, (i + step) % n) for i in range(n)])]
    all_to_all x0 -> x1, waiting for transfers between devices: none -> 3.33 us  [layer(): swapped = lax.all_to_all(parts, ('x', 'c', 'z'), 0, 0, tiled=True)]
    all_to_all x1, blocking collectives: 11.6 us -> 14.6 us  [from_everyone(): lax.all_to_all(jnp.broadcast_to(value[None], (n, *value.shape)), axes, 0,...]
    all_to_all x2, starting transfers between devices: 14.1 us -> 11.5 us  [from_everyone(): lax.all_to_all(jnp.broadcast_to(value[None], (n, *value.shape)), axes, 0,...]
  transfers between devices with their start and end apart: 9 -> 10, of which waited for: 6 -> 6; matrix products, arithmetic and copies ran while one was open for 2% -> 2% of each run, Pallas kernels for 11% -> 11%
where the time goes in v8:
time: 171 us; the launch traced here: 170 us
  starting transfers between devices  55 us (32%)
  waiting for transfers between devices  48.1 us (28%)
  blocking collectives  30.5 us (18%)
  Pallas kernels  30.4 us (18%)
  local copies, waits for them, and re-layouts  5.63 us (3%)
    all_to_all x2, waiting for transfers between devices, from_everyone(): lax.all_to_all(jnp.broadcast_to(value[None], (n, *value.shape)), axes, 0,...  33.7 us
    ppermute x5, starting transfers between devices, shift(): return lax.ppermute(value, axis, [(i, (i + step) % n) for i in range(n)])  25.2 us
    all_to_all x1, blocking collectives, layer(): mixed = lax.all_to_all(mixed, LINE, 0, 0, tiled=True).reshape(1024, 256)  15.9 us
    all_to_all x1, blocking collectives, from_everyone(): lax.all_to_all(jnp.broadcast_to(value[None], (n, *value.shape)), axes, 0,...  14.6 us
    all_to_all x1, starting transfers between devices, layer(): swapped = lax.all_to_all(parts, ('x', 'c', 'z'), 0, 0, tiled=True)  14 us
    all_to_all x2, starting transfers between devices, from_everyone(): lax.all_to_all(jnp.broadcast_to(value[None], (n, *value.shape)), axes, 0,...  11.5 us
    pallas_call x1, Pallas kernels, attend(): pl.pallas_call(attend_kernel, grid_spec=pltpu.PrefetchScalarGridSpec(num_...  11 us
    ppermute x5, waiting for transfers between devices, shift(): return lax.ppermute(value, axis, [(i, (i + step) % n) for i in range(n)])  8.68 us
  transfers between devices with their start and end apart: 10, of which 6 were waited for; matrix products, arithmetic and copies ran while one was open for 2% of the time, Pallas kernels for 11%

profile of v8, /device:TPU:1, one launch (start us, length us, event | category | flops | bytes accessed | tf_op | source)
XLA Modules:
  0.0 170.4 jit_solution(11773066428050800131)
XLA Ops:
  0.0 2.4 %prepare.1 = (bf16[256,1024]{1,0:T(8,128)(2,1)}, bf16[64,2,640]{2,1,0:T(2,128)(2,1)}) custom-call(s32[1,8]{1,0:T(1,128)} %bitcast.21, bf16[256,1024]{1,0:T(8,128)(2,1)} %bitcast.15, f32[1,1024]{1,0:T(1,128)} %bitcast.20, bf16[2,3072]{1,0:T(2,128)(2,1)} %weight_ref.1, bf16[2,1024]{1,0:T(2,128)(2,1)} %out_weight_ref.1), custom_call_target="tpu_custom_call" | custom-call | tf_op jit(solution)/shard_map/prepare/pallas_call | solution.py:62
  2.4 3.9 %collective-permute-start = (bf16[256,1024]{1,0:T(8,128)(2,1)}, bf16[256,1024]{1,0:T(8,128)(2,1)S(1)}, u32[]{:S(2)}, u32[]{:S(2)}) collective-permute-start(bf16[256,1024]{1,0:T(8,128)(2,1)} %get-tuple-element.15), channel_id=1, source_target_pairs={{0,128},{128,256},{256,384},{384,0},{1,129},{129,257},{257,385},{3... | collective-permute-start | bytes 1572872 | tf_op jit(solution)/shard_map/ppermute | solution.py:86
  6.3 14.0 %all-to-all-start = ((bf16[64,2,640]{2,1,0:T(2,128)(2,1)}), bf16[64,2,640]{2,1,0:T(2,128)(2,1)S(1)}, u32[]{:S(2)}, u32[]{:S(2)}) async-start(bf16[64,2,640]{2,1,0:T(2,128)(2,1)} %get-tuple-element.13), calls=%async_computation | async-start | bytes 327680 | tf_op jit(solution)/shard_map/all_to_all | solution.py:334
  20.3 4.7 %collective-permute-start.1 = (bf16[256,1024]{1,0:T(8,128)(2,1)}, bf16[256,1024]{1,0:T(8,128)(2,1)}, u32[]{:S(2)}, u32[]{:S(2)}) collective-permute-start(bf16[256,1024]{1,0:T(8,128)(2,1)} %get-tuple-element.15), channel_id=1, source_target_pairs={{0,384},{128,0},{256,128},{384,256},{1,385},{129,1},{257,129},{385... | collective-permute-start | bytes 1572872 | tf_op jit(solution)/shard_map/ppermute | solution.py:86
  25.1 2.3 %collective-permute-start.2 = (bf16[256,1024]{1,0:T(8,128)(2,1)}, bf16[256,1024]{1,0:T(8,128)(2,1)}, u32[]{:S(2)}, u32[]{:S(2)}) collective-permute-start(bf16[256,1024]{1,0:T(8,128)(2,1)} %get-tuple-element.15), channel_id=1, source_target_pairs={{0,256},{128,384},{256,0},{384,128},{1,257},{129,385},{257,1},{385... | collective-permute-start | bytes 1572872 | tf_op jit(solution)/shard_map/ppermute | solution.py:86
  27.4 3.3 %all-to-all-done = bf16[64,2,640]{2,1,0:T(2,128)(2,1)S(1)} async-done(((bf16[64,2,640]{2,1,0:T(2,128)(2,1)}), bf16[64,2,640]{2,1,0:T(2,128)(2,1)S(1)}, u32[]{:S(2)}, u32[]{:S(2)}) %all-to-all-start) | async-done | bytes 163872 | tf_op jit(solution)/shard_map/all_to_all | solution.py:334
  30.8 1.1 constant_dynamic-update-slice_fusion.3
  32.0 5.6 %collective-permute-done.1 = bf16[256,1024]{1,0:T(8,128)(2,1)} collective-permute-done((bf16[256,1024]{1,0:T(8,128)(2,1)}, bf16[256,1024]{1,0:T(8,128)(2,1)}, u32[]{:S(2)}, u32[]{:S(2)}) %collective-permute-start.1) | collective-permute-done | bytes 524320 | tf_op jit(solution)/shard_map/ppermute | solution.py:86
  38.6 3.1 %collective-permute-done.2 = bf16[256,1024]{1,0:T(8,128)(2,1)} collective-permute-done((bf16[256,1024]{1,0:T(8,128)(2,1)}, bf16[256,1024]{1,0:T(8,128)(2,1)}, u32[]{:S(2)}, u32[]{:S(2)}) %collective-permute-start.2) | collective-permute-done | bytes 524320 | tf_op jit(solution)/shard_map/ppermute | solution.py:86
  42.8 10.6 %collective-permute-start.3 = (bf16[1024,1024]{1,0:T(8,128)(2,1)S(1)}, bf16[1024,1024]{1,0:T(8,128)(2,1)}, u32[]{:S(2)}, u32[]{:S(2)}) collective-permute-start(bf16[1024,1024]{1,0:T(8,128)(2,1)S(1)} %constant_dynamic-update-slice_fusion.mine_ref), channel_id=1, source_target_pairs={{0,64},{64,0},{1,65},{65,1},{2,66},{66,2},{3,67},{67,3},{4,68},{68... | collective-permute-start | bytes 6291464 | tf_op jit(solution)/shard_map/ppermute | solution.py:86
  54.4 6.8 %all-to-all-start.1 = ((bf16[8,128,384]{2,1,0:T(8,128)(2,1)}), bf16[8,128,384]{2,1,0:T(8,128)(2,1)S(1)}, u32[]{:S(2)}, u32[]{:S(2)}) async-start(bf16[8,128,384]{2,1,0:T(8,128)(2,1)} %broadcast_in_dim.8), calls=%async_computation.1 | async-start | bytes 1572864 | tf_op jit(solution)/shard_map/all_to_all | solution.py:91
  61.2 23.6 %all-to-all-done.1.gathered_ref = bf16[8,128,384]{2,1,0:T(8,128)(2,1)S(1)} async-done(((bf16[8,128,384]{2,1,0:T(8,128)(2,1)}), bf16[8,128,384]{2,1,0:T(8,128)(2,1)S(1)}, u32[]{:S(2)}, u32[]{:S(2)}) %all-to-all-start.1) | async-done | bytes 786464 | tf_op jit(solution)/shard_map/all_to_all | solution.py:91
  84.9 5.8 %project_qkv.1 = (bf16[8,512,128]{2,1,0:T(8,128)(2,1)}, bf16[8,256,128]{2,1,0:T(8,128)(2,1)}) custom-call(bf16[1024,1024]{1,0:T(8,128)(2,1)S(1)} %constant_dynamic-update-slice_fusion.mine_ref, bf16[1024,1024]{1,0:T(8,128)(2,1)} %collective-permute-done.3.other_ref, bf16[8,128,384]{2,1,0:T(8,128)(2,1)S(1)} %all-to-all-done.1.gathered_ref), custom_call_target="tpu_custom_call" | custom-call | tf_op jit(solution)/shard_map/project_qkv/pallas_call | solution.py:141
  90.7 14.6 %all_to_all.25 = bf16[8,128,128]{2,1,0:T(8,128)(2,1)S(1)} all-to-all(bf16[8,128,128]{2,1,0:T(8,128)(2,1)S(1)} %broadcast_in_dim.9), channel_id=1, replica_groups=mesh['x'=4,'c'=2,'y'=8,'z'=8] {'y'}, dimensions={0} | all-to-all | bytes 524288 | tf_op jit(solution)/shard_map/all_to_all | solution.py:91
  106.4 4.6 %all-to-all-start.4 = ((bf16[4,1024,128]{2,1,0:T(8,128)(2,1)}), bf16[4,1024,128]{2,1,0:T(8,128)(2,1)}, u32[]{:S(2)}, u32[]{:S(2)}) async-start(bf16[4,1024,128]{2,1,0:T(8,128)(2,1)} %broadcast_in_dim.22), calls=%async_computation.4 | async-start | bytes 2097152 | tf_op jit(solution)/shard_map/all_to_all | solution.py:91
  111.1 3.1 %collective-permute-start.4 = (bf16[8,512,128]{2,1,0:T(8,128)(2,1)}, bf16[8,512,128]{2,1,0:T(8,128)(2,1)S(1)}, u32[]{:S(2)}, u32[]{:S(2)}) collective-permute-start(bf16[8,512,128]{2,1,0:T(8,128)(2,1)} %get-tuple-element.17.own_ref), channel_id=1, source_target_pairs={{0,1},{1,2},{2,3},{3,4},{4,5},{5,6},{6,7},{7,8},{8,9},{9,10},{10,1... | collective-permute-start | bytes 3145736 | tf_op jit(solution)/shard_map/ppermute | solution.py:346
  114.1 1.3 collective-permute-start.5
  115.4 10.1 %all-to-all-done.4.mine_ref = bf16[4,1024,128]{2,1,0:T(8,128)(2,1)} async-done(((bf16[4,1024,128]{2,1,0:T(8,128)(2,1)}), bf16[4,1024,128]{2,1,0:T(8,128)(2,1)}, u32[]{:S(2)}, u32[]{:S(2)}) %all-to-all-start.4) | async-done | bytes 1048608 | tf_op jit(solution)/shard_map/all_to_all | solution.py:91
  125.5 3.6 %collective-permute-start.6 = (bf16[4,1024,128]{2,1,0:T(8,128)(2,1)}, bf16[4,1024,128]{2,1,0:T(8,128)(2,1)S(1)}, u32[]{:S(2)}, u32[]{:S(2)}) collective-permute-start(bf16[4,1024,128]{2,1,0:T(8,128)(2,1)} %all-to-all-done.4.mine_ref), channel_id=1, source_target_pairs={{0,64},{64,0},{1,65},{65,1},{2,66},{66,2},{3,67},{67,3},{4,68},{68... | collective-permute-start | bytes 3145736 | tf_op jit(solution)/shard_map/ppermute | solution.py:86
  129.9 7.6 %attend_own.1 = (f32[8,2,80,256]{3,2,1,0:T(8,128)}, f32[8,2,8,256]{3,2,1,0:T(8,128)}) custom-call(s32[74]{0:T(128)} %pad_add_fusion.table, bf16[8,256,128]{2,1,0:T(8,128)(2,1)} %get-tuple-element.16.query_ref, bf16[8,512,128]{2,1,0:T(8,128)(2,1)} %get-tuple-element.17.own_ref), custom_call_target="tpu_custom_call" | custom-call | tf_op jit(solution)/shard_map/attend_own/pallas_call | solution.py:231
  137.4 2.4 %collective-permute-done.5.high_ref = bf16[8,512,128]{2,1,0:T(8,128)(2,1)S(1)} collective-permute-done((bf16[8,512,128]{2,1,0:T(8,128)(2,1)}, bf16[8,512,128]{2,1,0:T(8,128)(2,1)S(1)}, u32[]{:S(2)}, u32[]{:S(2)}) %collective-permute-start.5) | collective-permute-done | bytes 1048608 | tf_op jit(solution)/shard_map/ppermute | solution.py:347
  139.8 11.0 %attend.1 = bf16[8,128,256]{2,1,0:T(8,128)(2,1)} custom-call(s32[74]{0:T(128)} %pad_add_fusion.table, bf16[8,256,128]{2,1,0:T(8,128)(2,1)} %get-tuple-element.16.query_ref, bf16[8,512,128]{2,1,0:T(8,128)(2,1)S(1)} %collective-permute-done.4.low_ref, bf16[8,512,128]{2,1,0:T(8,128)(2,1)S(1)} %collective-permute-done.5.high_ref, ...), custom_call_target="tpu_custom_call" | custom-call | tf_op jit(solution)/shard_map/attend/pallas_call | solution.py:266
  150.8 15.9 %all_to_all.26 = bf16[8,128,256]{2,1,0:T(8,128)(2,1)S(1)} all-to-all(bf16[8,128,256]{2,1,0:T(8,128)(2,1)} %attend.1), channel_id=1, replica_groups=mesh['x'=4,'c'=2,'y'=8,'z'=8] {'x','c'}, dimensions={0} | all-to-all | bytes 1048576 | tf_op jit(solution)/shard_map/all_to_all | solution.py:355
  166.6 3.7 %project_out.1 = bf16[256,1024]{1,0:T(8,128)(2,1)} custom-call(s32[74]{0:T(128)} %pad_add_fusion.table, bf16[1024,256]{1,0:T(8,128)(2,1)S(1)} %bitcast.14, bf16[4,1024,128]{2,1,0:T(8,128)(2,1)} %all-to-all-done.4.mine_ref, bf16[4,1024,128]{2,1,0:T(8,128)(2,1)S(1)} %collective-permute-done.6.other_ref, bf16[256,1024]{1,0:T(8,128)(2,1)} %bitcast.16), custom_call_target="tpu_custom_call" | custom-call | tf_op jit(solution)/shard_map/project_out/pallas_call | solution.py:300
  (21 shorter events, 5.1 us)
Async XLA Ops:
  2.4 29.5 %collective-permute-start = (bf16[256,1024]{1,0:T(8,128)(2,1)}, bf16[256,1024]{1,0:T(8,128)(2,1)S(1)}, u32[]{:S(2)}, u32[]{:S(2)}) collective-permute-start(bf16[256,1024]{1,0:T(8,128)(2,1)} %get-tuple-element.15), channel_id=1, source_target_pairs={{0,128},{128,256},{256,384},{384,0},{1,129},{129,257},{257,385},{3... | collective-permute-start | bytes 1572872 | tf_op jit(solution)/shard_map/ppermute | solution.py:86
  6.3 24.4 %all-to-all-start = ((bf16[64,2,640]{2,1,0:T(2,128)(2,1)}), bf16[64,2,640]{2,1,0:T(2,128)(2,1)S(1)}, u32[]{:S(2)}, u32[]{:S(2)}) async-start(bf16[64,2,640]{2,1,0:T(2,128)(2,1)} %get-tuple-element.13), calls=%async_computation | async-start | bytes 327680 | tf_op jit(solution)/shard_map/all_to_all | solution.py:334
  20.3 17.2 %collective-permute-start.1 = (bf16[256,1024]{1,0:T(8,128)(2,1)}, bf16[256,1024]{1,0:T(8,128)(2,1)}, u32[]{:S(2)}, u32[]{:S(2)}) collective-permute-start(bf16[256,1024]{1,0:T(8,128)(2,1)} %get-tuple-element.15), channel_id=1, source_target_pairs={{0,384},{128,0},{256,128},{384,256},{1,385},{129,1},{257,129},{385... | collective-permute-start | bytes 1572872 | tf_op jit(solution)/shard_map/ppermute | solution.py:86
  25.1 16.6 %collective-permute-start.2 = (bf16[256,1024]{1,0:T(8,128)(2,1)}, bf16[256,1024]{1,0:T(8,128)(2,1)}, u32[]{:S(2)}, u32[]{:S(2)}) collective-permute-start(bf16[256,1024]{1,0:T(8,128)(2,1)} %get-tuple-element.15), channel_id=1, source_target_pairs={{0,256},{128,384},{256,0},{384,128},{1,257},{129,385},{257,1},{385... | collective-permute-start | bytes 1572872 | tf_op jit(solution)/shard_map/ppermute | solution.py:86
  30.8 30.5 %copy-start = (bf16[128,640]{1,0:T(8,128)(2,1)}, bf16[128,640]{1,0:T(8,128)(2,1)S(1)}, u32[]{:S(2)}) copy-start(bf16[128,640]{1,0:T(8,128)(2,1)S(1)} %reshape.32) | copy-start | bytes 491524
  42.8 42.1 %collective-permute-start.3 = (bf16[1024,1024]{1,0:T(8,128)(2,1)S(1)}, bf16[1024,1024]{1,0:T(8,128)(2,1)}, u32[]{:S(2)}, u32[]{:S(2)}) collective-permute-start(bf16[1024,1024]{1,0:T(8,128)(2,1)S(1)} %constant_dynamic-update-slice_fusion.mine_ref), channel_id=1, source_target_pairs={{0,64},{64,0},{1,65},{65,1},{2,66},{66,2},{3,67},{67,3},{4,68},{68... | collective-permute-start | bytes 6291464 | tf_op jit(solution)/shard_map/ppermute | solution.py:86
  54.4 30.5 %all-to-all-start.1 = ((bf16[8,128,384]{2,1,0:T(8,128)(2,1)}), bf16[8,128,384]{2,1,0:T(8,128)(2,1)S(1)}, u32[]{:S(2)}, u32[]{:S(2)}) async-start(bf16[8,128,384]{2,1,0:T(8,128)(2,1)} %broadcast_in_dim.8), calls=%async_computation.1 | async-start | bytes 1572864 | tf_op jit(solution)/shard_map/all_to_all | solution.py:91
  61.2 29.4 %slice-start = ((bf16[128,640]{1,0:T(8,128)(2,1)}), bf16[128,128]{1,0:T(8,128)(2,1)S(1)}, s32[]{:S(2)}) async-start(bf16[128,640]{1,0:T(8,128)(2,1)} %copy-done), calls=%async_computation.5 | async-start | bytes 65536 | tf_op jit(solution)/shard_map/slice | solution.py:349
  106.4 19.1 %all-to-all-start.4 = ((bf16[4,1024,128]{2,1,0:T(8,128)(2,1)}), bf16[4,1024,128]{2,1,0:T(8,128)(2,1)}, u32[]{:S(2)}, u32[]{:S(2)}) async-start(bf16[4,1024,128]{2,1,0:T(8,128)(2,1)} %broadcast_in_dim.22), calls=%async_computation.4 | async-start | bytes 2097152 | tf_op jit(solution)/shard_map/all_to_all | solution.py:91
  111.1 26.4 %collective-permute-start.4 = (bf16[8,512,128]{2,1,0:T(8,128)(2,1)}, bf16[8,512,128]{2,1,0:T(8,128)(2,1)S(1)}, u32[]{:S(2)}, u32[]{:S(2)}) collective-permute-start(bf16[8,512,128]{2,1,0:T(8,128)(2,1)} %get-tuple-element.17.own_ref), channel_id=1, source_target_pairs={{0,1},{1,2},{2,3},{3,4},{4,5},{5,6},{6,7},{7,8},{8,9},{9,10},{10,1... | collective-permute-start | bytes 3145736 | tf_op jit(solution)/shard_map/ppermute | solution.py:346
  114.1 25.7 %collective-permute-start.5 = (bf16[8,512,128]{2,1,0:T(8,128)(2,1)}, bf16[8,512,128]{2,1,0:T(8,128)(2,1)S(1)}, u32[]{:S(2)}, u32[]{:S(2)}) collective-permute-start(bf16[8,512,128]{2,1,0:T(8,128)(2,1)} %get-tuple-element.17.own_ref), channel_id=1, source_target_pairs={{1,0},{2,1},{3,2},{4,3},{5,4},{6,5},{7,6},{8,7},{9,8},{10,9},{11,1... | collective-permute-start | bytes 3145736 | tf_op jit(solution)/shard_map/ppermute | solution.py:347
  125.5 41.2 %collective-permute-start.6 = (bf16[4,1024,128]{2,1,0:T(8,128)(2,1)}, bf16[4,1024,128]{2,1,0:T(8,128)(2,1)S(1)}, u32[]{:S(2)}, u32[]{:S(2)}) collective-permute-start(bf16[4,1024,128]{2,1,0:T(8,128)(2,1)} %all-to-all-done.4.mine_ref), channel_id=1, source_target_pairs={{0,64},{64,0},{1,65},{65,1},{2,66},{66,2},{3,67},{67,3},{4,68},{68... | collective-permute-start | bytes 3145736 | tf_op jit(solution)/shard_map/ppermute | solution.py:86
